TPU v7x, 256 devices: a whole 4x4x8 slice. The times are simulated.
256 devices in a mesh: tm: 4 (over z_lo, core), firm: 64 (over y, x, z_hi).
Axes of the slice: x: 4, y: 4, z: 8 (z_hi: 4, z_lo: 2; z = z_hi * 2 + z_lo), core: 2. Of those that a mesh axis runs over, the one named last changes fastest.
Arguments:
- features: bfloat16 [32, 16384, 256], P('tm', 'firm'), may hold values from -6 to 6
- supply_counts: int32 [32, 16384, 3, 256], P('tm', 'firm'), may hold values from 0 to 3
- bank_ids: int32 [32, 16384], P('tm', 'firm'), may hold values from 0 to 511
- sector_ids: int32 [32, 16384], P('tm', 'firm'), may hold values from 0 to 255
- bank_table: bfloat16 [512, 256], P('firm'), may hold values from -6 to 6
- sector_table: bfloat16 [256, 256], P('firm'), may hold values from -6 to 6
- w_supply: bfloat16 [256, 256], replicated, may hold values from -0.375 to 0.375
- w_query: bfloat16 [256, 256], replicated, may hold values from -0.375 to 0.375
- w_key: bfloat16 [256, 256], replicated, may hold values from -0.375 to 0.375
- w_value: bfloat16 [256, 256], replicated, may hold values from -0.375 to 0.375
- w_out: bfloat16 [256, 256], replicated, may hold values from -0.375 to 0.375
- w_in: bfloat16 [256, 1024], replicated, may hold values from -0.375 to 0.375
- w_down: bfloat16 [1024, 256], replicated, may hold values from -0.1875 to 0.1875
- gain_mix: float32 [256], replicated, may hold values from 0.1 to 1.9
- gain_ffn: float32 [256], replicated, may hold values from 0.1 to 1.9
Outputs:
- result: bfloat16 [32, 16384, 256], P('tm', 'firm')
All inputs are finite; a program needn't handle non-finite values.
Results may differ from a plain program's by a relative error of at most 0.0059.
Values may be sent and summed in bfloat16 or wider, within the bound.
No kernel may reach another device: no remote copies, remote signals or barrier semaphores. Data moves between devices by JAX's collectives and lax.ppermute only.
A program may use at most 64 MiB of HBM per device.

v0:
```python
import jax
import jax.numpy as jnp
from jax import lax
from jax.sharding import PartitionSpec as P

HEADS = 4


def padded(x, sides, width):
    for axis, dim in sides:
        devices, length = (lax.axis_size(axis), x.shape[dim])
        up = [(i, (i + 1) % devices) for i in range(devices - 1)]
        down = [(j, i) for i, j in up]
        last = lax.slice_in_dim(x, length - width, length, axis=dim)
        leading = lax.slice_in_dim(x, 0, width, axis=dim)
        before = lax.ppermute(last, axis, up)
        after = lax.ppermute(leading, axis, down)
        x = jnp.concatenate([before, x, after], axis=dim)
    return x


def from_behind(x, axis, by):
    devices = lax.axis_size(axis)
    pairs = [(i, i + by) for i in range(devices) if 0 <= i + by < devices]
    return lax.ppermute(x, axis, pairs)


def rms_norm(values, gain):
    scale = lax.rsqrt(jnp.mean(values * values, axis=-1, keepdims=True) + 1e-06)
    return values * scale * gain


def body(
    features,
    supply_counts,
    bank_ids,
    sector_ids,
    bank_table,
    sector_table,
    w_supply,
    w_query,
    w_key,
    w_value,
    w_out,
    w_in,
    w_down,
    gain_mix,
    gain_ffn,
):
    months, firms, width = features.shape
    rows = months * firms
    flat = features.reshape(rows, width)
    supplied = (
        jnp.dot(flat, w_supply, preferred_element_type=jnp.float32)
        .astype(jnp.bfloat16)
        .reshape(months, firms, width)
    )
    extended = padded(supplied, (("firm", 1),), firms)
    tiles = supply_counts.reshape(months, firms, 3 * firms).astype(jnp.bfloat16)
    degree = 1.0 + jnp.sum(supply_counts, axis=(2, 3)).astype(jnp.float32)
    message = jnp.einsum("mfs,msd->mfd", tiles, extended, preferred_element_type=jnp.float32)
    message = message * lax.rsqrt(degree)[..., None]
    bank_local = bank_table.shape[0]
    sector_local = sector_table.shape[0]
    per_owner = bank_local + sector_local
    hub_local = jnp.concatenate([bank_table, sector_table], axis=0)
    bank_flat = bank_ids.reshape(rows)
    sector_flat = sector_ids.reshape(rows)
    bank_pos = bank_flat // bank_local * per_owner + bank_flat % bank_local
    sector_pos = sector_flat // sector_local * per_owner + bank_local + sector_flat % sector_local
    hub_whole = lax.all_gather(hub_local, "firm", axis=0, tiled=True)
    hubs = jnp.take(hub_whole, bank_pos, axis=0).astype(jnp.float32) + jnp.take(
        hub_whole, sector_pos, axis=0
    ).astype(jnp.float32)
    mixed = flat.astype(jnp.float32) + message.reshape(rows, width) + hubs
    normed = rms_norm(mixed, gain_mix).astype(jnp.bfloat16)
    query = (
        jnp.dot(normed, w_query, preferred_element_type=jnp.float32)
        .astype(jnp.bfloat16)
        .reshape(months, firms, width)
    )
    key = (
        jnp.dot(normed, w_key, preferred_element_type=jnp.float32)
        .astype(jnp.bfloat16)
        .reshape(months, firms, width)
    )
    value = (
        jnp.dot(normed, w_value, preferred_element_type=jnp.float32)
        .astype(jnp.bfloat16)
        .reshape(months, firms, width)
    )
    earlier_key, earlier_value = from_behind((key, value), "tm", 1)
    earlier_key = earlier_key[months - 3 :]
    earlier_value = earlier_value[months - 3 :]
    keys_all = jnp.concatenate([earlier_key, key], axis=0)
    values_all = jnp.concatenate([earlier_value, value], axis=0)
    heads = HEADS
    head_size = width // heads
    query4 = query.reshape(months, firms, heads, head_size)
    first_month = lax.axis_index("tm") * months
    month_local = lax.iota(jnp.int32, months)
    total = jnp.zeros((months, firms, heads, head_size), jnp.float32)
    for lag in range(4):
        key_l = keys_all[3 - lag : 3 - lag + months].reshape(months, firms, heads, head_size)
        value_l = values_all[3 - lag : 3 - lag + months].reshape(months, firms, heads, head_size)
        score = jnp.einsum(
            "mfhd,mfhd->mfh", query4, key_l, preferred_element_type=jnp.float32
        ) / jnp.sqrt(jnp.float32(head_size)) - jnp.log(jnp.float32(4.0))
        valid = (first_month + month_local - lag >= 0).astype(jnp.float32)[:, None, None]
        total = total + (jax.nn.sigmoid(score) * valid)[..., None] * value_l.astype(jnp.float32)
    attended = total.astype(jnp.bfloat16).reshape(rows, width)
    second = mixed + jnp.dot(attended, w_out, preferred_element_type=jnp.float32)
    normed2 = rms_norm(second, gain_ffn).astype(jnp.bfloat16)
    inner = jax.nn.gelu(jnp.dot(normed2, w_in, preferred_element_type=jnp.float32)).astype(
        jnp.bfloat16
    )
    final = second + jnp.dot(inner, w_down, preferred_element_type=jnp.float32)
    return final.astype(jnp.bfloat16).reshape(months, firms, width)


def solution(mesh):
    in_specs = (
        P("tm", "firm", None),
        P("tm", "firm", None, None),
        P("tm", "firm"),
        P("tm", "firm"),
        P("firm", None),
        P("firm", None),
        P(),
        P(),
        P(),
        P(),
        P(),
        P(),
        P(),
        P(),
        P(),
    )
    out_specs = P("tm", "firm", None)
    return jax.shard_map(body, mesh=mesh, in_specs=in_specs, out_specs=out_specs, check_vma=False)
```

profile of v0, /device:TPU:1, one launch (start us, length us, event | category | flops | bytes accessed | tf_op | source)
XLA Modules:
  0.0 347.4 jit_solution(13643477030206423323)
XLA Ops:
  0.0 1.7 convolution_convert_fusion.3
  3.1 7.4 %collective-permute-start = (bf16[8,256,256]{2,1,0:T(8,128)(2,1)S(1)}, bf16[8,256,256]{2,1,0:T(8,128)(2,1)}, u32[]{:S(2)}, u32[]{:S(2)}) collective-permute-start(bf16[8,256,256]{2,1,0:T(8,128)(2,1)S(1)} %bitcast.95), channel_id=1, source_target_pairs={{0,1},{1,2},{2,3},{3,4},{4,5},{5,6},{6,7},{7,8},{8,9},{9,10},{10,1... | collective-permute-start | bytes 3145736 | tf_op jit(solution)/shard_map/ppermute | solution.py:16
  10.4 198.2 %all-gather = bf16[64,12,256]{2,1,0:T(8,128)(2,1)S(1)} all-gather(bf16[1,12,256]{2,1,0:T(8,128)(2,1)S(1)} %maximum_bitcast_fusion), channel_id=1, replica_groups=mesh['tm'=4,'firm'=64] {'firm'}, dimensions={0}, use_global_device_ids=true | all-gather | bytes 399360 | tf_op jit(solution)/shard_map/all_gather | solution.py:71
  208.6 6.6 %copy.26 = s32[8,256,3,256]{1,3,2,0:T(8,128)} copy(s32[8,256,3,256]{3,1,2,0:T(8,128)} %param.18) | data formatting | bytes 12582912 | tf_op args[1]
  215.2 3.1 reduce_sum.27
  218.5 9.1 %gather_fusion.1 = bf16[2048,256]{1,0:T(8,128)(2,1)} fusion(bf16[768,256]{1,0:T(8,128)(2,1)S(1)} %reshape.138, s32[2048]{0:T(1024)S(1)} %broadcast_clamp_fusion), kind=kCustom, calls=%fused_computation.1.clone | custom fusion | bytes 2105344 | tf_op jit(solution)/shard_map/jit(_take)/gather | solution.py:72
  227.6 9.0 %gather_fusion = bf16[2048,256]{1,0:T(8,128)(2,1)} fusion(bf16[768,256]{1,0:T(8,128)(2,1)S(1)} %reshape.138, s32[2048]{0:T(1024)S(1)} %broadcast_clamp_fusion.1), kind=kCustom, calls=%fused_computation.clone | custom fusion | bytes 2105344 | tf_op jit(solution)/shard_map/jit(_take)/gather | solution.py:72
  236.6 5.2 %convert_element_type.105 = bf16[8,256,3,256]{1,3,2,0:T(8,128)(2,1)} convert(s32[8,256,3,256]{1,3,2,0:T(8,128)} %copy.26) | non-fusion elementwise | flops 1572864 | bytes 9437184 | tf_op jit(solution)/shard_map/convert_element_type | solution.py:59
  241.8 3.8 %fusion.29 = f32[8,256,256]{1,2,0:T(8,128)S(1)} fusion(bf16[8,256,768]{1,2,0:T(8,128)(2,1)} %bitcast.93, bf16[8,256,256]{2,1,0:T(8,128)(2,1)} %collective-permute-done.1, bf16[8,256,256]{2,1,0:T(8,128)(2,1)S(1)} %bitcast.96, bf16[8,256,256]{2,1,0:T(8,128)(2,1)} %collective-permute-done, f32[8,256]{1,0:T(8,128)S(1)} %add_rsqrt_fusion.2), kind=kOutput, calls=%fused_computation.47 | convolution fusion | flops 815267840 | bytes 8396800 | tf_op jit(solution)/shard_map/mfs,msd->mfd/dot_general | solution.py:61
  245.7 2.1 multiply_reduce_fusion.5
  249.2 1.4 convolution_convert_fusion.1
  250.6 2.3 copy.31
  252.9 38.6 %collective-permute-start.2 = (bf16[8,256,256]{1,2,0:T(8,128)(2,1)}, bf16[8,256,256]{1,2,0:T(8,128)(2,1)}, u32[]{:S(2)}, u32[]{:S(2)}) collective-permute-start(bf16[8,256,256]{1,2,0:T(8,128)(2,1)} %copy.31), channel_id=1, source_target_pairs={{0,64},{64,128},{128,192},{1,65},{65,129},{129,193},{2,66},{66,130... | collective-permute-start | bytes 3145736 | tf_op jit(solution)/shard_map/ppermute | solution.py:25
  291.6 2.3 copy.29
  293.8 2.7 convolution_convert_fusion.2
  296.5 2.3 copy.28
  298.8 1.6 copy.59
  300.7 1.5 convert.11
  302.3 1.4 convolution_convert_fusion
  303.7 2.1 collective-permute-start.3
  306.3 2.2 copy.61
  308.5 2.9 copy.30
  312.4 2.2 fusion.34
  316.3 2.2 copy.63
  318.5 2.9 copy.34
  321.7 2.2 copy.64
  323.9 2.9 copy.35
  327.0 2.2 copy.62
  329.2 2.9 copy.33
  333.2 2.0 fusion.33
  336.1 4.9 %multiply_reduce_fusion.4 = (f32[2048]{0:T(1024)S(1)}, f32[2048,256]{1,0:T(8,128)}) fusion(f32[2048,256]{1,0:T(8,128)S(1)} %get-tuple-element.10, bf16[256,256]{1,0:T(8,128)(2,1)S(1)} %copy-done.10, f32[2048,256]{1,0:T(8,128)} %copy.35, bf16[2048,256]{1,0:T(8,128)(2,1)S(1)} %bitcast.91, f32[2048,256]{1,0:T(8,128)S(1)} %copy-done.5, ...), kind=kOutput, calls=%fused_computation.40 | convolution fusion | flops 276297728 | bytes 16916480 | tf_op jit(solution)/shard_map/dot_general | solution.py:112
  341.1 6.4 %fusion.21 = bf16[2048,256]{1,0:T(8,128)(2,1)} fusion(f32[2048,256]{1,0:T(8,128)} %get-tuple-element.22, bf16[1024,256]{1,0:T(8,128)(2,1)S(1)} %copy-done, bf16[256,1024]{1,0:T(8,128)(2,1)S(1)} %copy-done.19, f32[256]{0:T(256)S(1)} %copy-done.20, f32[2048]{0:T(1024)S(1)} %add_rsqrt_fusion), kind=kOutput, calls=%fused_computation.21 | convolution fusion | flops 2168979456 | bytes 4203520 | tf_op jit(solution)/shard_map/dot_general | solution.py:117
  (73 shorter events, 8.8 us)
Async XLA Ops:
  0.0 341.1 %copy-start = (bf16[1024,256]{1,0:T(8,128)(2,1)S(1)}, bf16[1024,256]{1,0:T(8,128)(2,1)}, u32[]{:S(2)}) copy-start(bf16[1024,256]{1,0:T(8,128)(2,1)} %param.29) | copy-start | bytes 1572868
  0.0 10.4 %copy-start.17 = (bf16[4,256]{1,0:T(4,128)(2,1)S(1)}, bf16[4,256]{1,0:T(4,128)(2,1)}, u32[]{:S(2)}) copy-start(bf16[4,256]{1,0:T(4,128)(2,1)} %param.22) | copy-start | bytes 6148
  0.0 10.4 %copy-start.16 = (bf16[8,256]{1,0:T(8,128)(2,1)S(1)}, bf16[8,256]{1,0:T(8,128)(2,1)}, u32[]{:S(2)}) copy-start(bf16[8,256]{1,0:T(8,128)(2,1)} %param.21) | copy-start | bytes 12292
  0.0 208.6 %copy-start.14 = (s32[8,256]{1,0:T(8,128)S(1)}, s32[8,256]{1,0:T(8,128)}, u32[]{:S(2)}) copy-start(s32[8,256]{1,0:T(8,128)} %param.19) | copy-start | bytes 24580
  0.0 208.6 %copy-start.15 = (s32[8,256]{1,0:T(8,128)S(1)}, s32[8,256]{1,0:T(8,128)}, u32[]{:S(2)}) copy-start(s32[8,256]{1,0:T(8,128)} %param.20) | copy-start | bytes 24580
  1.8 240.0 %collective-permute-start.1 = (bf16[8,256,256]{2,1,0:T(8,128)(2,1)S(1)}, bf16[8,256,256]{2,1,0:T(8,128)(2,1)}, u32[]{:S(2)}, u32[]{:S(2)}) collective-permute-start(bf16[8,256,256]{2,1,0:T(8,128)(2,1)S(1)} %bitcast.94), channel_id=1, source_target_pairs={{1,0},{2,1},{3,2},{4,3},{5,4},{6,5},{7,6},{8,7},{9,8},{10,9},{11,1... | collective-permute-start | bytes 3145736 | tf_op jit(solution)/shard_map/ppermute | solution.py:17
  3.1 238.7 %collective-permute-start = (bf16[8,256,256]{2,1,0:T(8,128)(2,1)S(1)}, bf16[8,256,256]{2,1,0:T(8,128)(2,1)}, u32[]{:S(2)}, u32[]{:S(2)}) collective-permute-start(bf16[8,256,256]{2,1,0:T(8,128)(2,1)S(1)} %bitcast.95), channel_id=1, source_target_pairs={{0,1},{1,2},{2,3},{3,4},{4,5},{5,6},{6,7},{7,8},{8,9},{9,10},{10,1... | collective-permute-start | bytes 3145736 | tf_op jit(solution)/shard_map/ppermute | solution.py:16
  241.8 3.9 %copy-start.7 = (bf16[8,256,256]{2,1,0:T(8,128)(2,1)S(1)}, bf16[8,256,256]{2,1,0:T(8,128)(2,1)}, u32[]{:S(2)}) copy-start(bf16[8,256,256]{2,1,0:T(8,128)(2,1)} %param.17) | copy-start | bytes 3145732
  241.8 3.9 %copy-start.8 = (bf16[2048,256]{1,0:T(8,128)(2,1)S(1)}, bf16[2048,256]{1,0:T(8,128)(2,1)}, u32[]{:S(2)}) copy-start(bf16[2048,256]{1,0:T(8,128)(2,1)} %gather_fusion.1) | copy-start | bytes 3145732
  241.8 3.9 %copy-start.9 = (bf16[2048,256]{1,0:T(8,128)(2,1)S(1)}, bf16[2048,256]{1,0:T(8,128)(2,1)}, u32[]{:S(2)}) copy-start(bf16[2048,256]{1,0:T(8,128)(2,1)} %gather_fusion) | copy-start | bytes 3145732
  245.7 2.2 copy-start.18
  247.8 1.4 copy-start.11
  248.2 1.0 copy-start.1
  250.6 43.2 %copy-start.12 = (bf16[256,256]{1,0:T(8,128)(2,1)S(1)}, bf16[256,256]{1,0:T(8,128)(2,1)}, u32[]{:S(2)}) copy-start(bf16[256,256]{1,0:T(8,128)(2,1)} %param.24) | copy-start | bytes 393220
  252.9 58.5 %collective-permute-start.2 = (bf16[8,256,256]{1,2,0:T(8,128)(2,1)}, bf16[8,256,256]{1,2,0:T(8,128)(2,1)}, u32[]{:S(2)}, u32[]{:S(2)}) collective-permute-start(bf16[8,256,256]{1,2,0:T(8,128)(2,1)} %copy.31), channel_id=1, source_target_pairs={{0,64},{64,128},{128,192},{1,65},{65,129},{129,193},{2,66},{66,130... | collective-permute-start | bytes 3145736 | tf_op jit(solution)/shard_map/ppermute | solution.py:25
  298.8 1.6 copy-start.6
  300.7 1.5 copy-start.2
  300.7 1.5 copy-start.13
  303.7 28.5 %collective-permute-start.3 = (bf16[8,256,256]{2,1,0:T(8,128)(2,1)}, bf16[8,256,256]{2,1,0:T(8,128)(2,1)}, u32[]{:S(2)}, u32[]{:S(2)}) collective-permute-start(bf16[8,256,256]{2,1,0:T(8,128)(2,1)} %bitcast.8), channel_id=1, source_target_pairs={{0,64},{64,128},{128,192},{1,65},{65,129},{129,193},{2,66},{66,130... | collective-permute-start | bytes 3145736 | tf_op jit(solution)/shard_map/ppermute | solution.py:25
  312.4 2.3 copy-start.3
  333.2 2.3 copy-start.4
  333.2 2.9 copy-start.5
  333.2 2.9 copy-start.10
  336.1 4.9 %copy-start.19 = (bf16[256,1024]{1,0:T(8,128)(2,1)S(1)}, bf16[256,1024]{1,0:T(8,128)(2,1)}, u32[]{:S(2)}) copy-start(bf16[256,1024]{1,0:T(8,128)(2,1)} %param.28) | copy-start | bytes 1572868
  336.1 4.9 %copy-start.20 = (f32[256]{0:T(256)S(1)}, f32[256]{0:T(256)}, u32[]{:S(2)}) copy-start(f32[256]{0:T(256)} %param.31) | copy-start | bytes 3076
where the time goes:
time: 348 us; the launch traced here: 347 us
  blocking collectives  198 us (57%)
  local copies, waits for them, and re-layouts  58.7 us (17%)
  starting transfers between devices  49.4 us (14%)
  matrix products  22.3 us (6%)
  other arithmetic  18.5 us (5%)
    all_gather x1, blocking collectives, body(): hub_whole = lax.all_gather(hub_local, 'firm', axis=0, tiled=True)  198 us
    ppermute x2, starting transfers between devices, from_behind(): return lax.ppermute(x, axis, pairs)  40.7 us
    unnamed x52, local copies, waits for them, and re-layouts  19.5 us
    mul x8, local copies, waits for them, and re-layouts, body(): (jax.nn.sigmoid(score) * valid)[..., None] * value_l.astype(jnp.float32)  12.2 us
    gather x1, local copies, waits for them, and re-layouts, body(): jnp.take(hub_whole, sector_pos, axis=0).astype(jnp.float32)  9.06 us
    gather x1, local copies, waits for them, and re-layouts, body(): jnp.take(hub_whole, bank_pos, axis=0).astype(jnp.float32)  9 us
    ppermute x1, starting transfers between devices, padded(): before = lax.ppermute(last, axis, up)  7.35 us
  transfers between devices with their start and end apart: 4, of which 0 were waited for; matrix products, arithmetic and copies ran while one was open for 21% of the time, Pallas kernels for 0%

commit v1 on v0

v1 whole, which is shorter than its diff:
```python
import jax
import jax.numpy as jnp
from jax import lax
from jax.experimental import pallas as pl
from jax.experimental.pallas import tpu as pltpu
from jax.sharding import PartitionSpec as P
import math

HEADS = 4
LAGS = 3
EARLY = 5
SLOT = 16
LOG2 = math.log(2.0)
GELU = math.sqrt(2.0 / math.pi)
BF = jnp.bfloat16
F32 = jnp.float32


def mm(a, b):
    return jnp.dot(a, b, preferred_element_type=F32)


def rms_norm(values, gain):
    scale = lax.rsqrt(jnp.mean(values * values, axis=-1, keepdims=True) + 1e-06)
    return values * scale * gain


def mix_month(counts, own, before, after, bank_pos, sector_pos, table, w_supply, gain_mix):
    firms = own.shape[0]
    tiles = [counts[k].astype(F32) for k in range(3)]
    degree = 1.0 + jnp.sum(tiles[0] + tiles[1] + tiles[2], axis=-1, keepdims=True)
    message = jnp.zeros(own.shape, F32)
    for tile, block in zip(tiles, (before, own, after)):
        supplied = mm(block, w_supply).astype(BF)
        message = message + mm(tile.astype(BF), supplied)
    rows = lax.broadcasted_iota(jnp.int32, (table.shape[0], firms), 0)
    chosen = jnp.where((rows == bank_pos) | (rows == sector_pos), 1.0, 0.0).astype(BF)
    hubs = lax.dot_general(chosen, table, (((0,), (0,)), ((), ())), preferred_element_type=F32)
    mixed = own.astype(F32) + message * lax.rsqrt(degree) + hubs
    return mixed, rms_norm(mixed, gain_mix).astype(BF)


def attend(query, keys, values, head_sum):
    total = jnp.zeros(query.shape, F32)
    for key, value in zip(keys, values):
        half = mm(query * key, head_sum) - LOG2
        total = total + (0.5 + 0.5 * jnp.tanh(half)) * value.astype(F32)
    return total.astype(BF)


def finish_month(mixed, attended, w_out, w_in, w_down, gain_ffn):
    second = mixed + mm(attended, w_out)
    normed2 = rms_norm(second, gain_ffn).astype(BF)
    x = mm(normed2, w_in)
    inner = (0.5 * x * (1.0 + jnp.tanh(GELU * (x + 0.044715 * (x * x * x))))).astype(BF)
    return (second + mm(inner, w_down)).astype(BF)


def head_matrix(width):
    size = width // HEADS
    row = lax.broadcasted_iota(jnp.int32, (width, width), 0) // size
    col = lax.broadcasted_iota(jnp.int32, (width, width), 1) // size
    return jnp.where(row == col, 0.5 / math.sqrt(size), 0.0).astype(BF)


def late_kernel(counts, own, before, after, pos, table, w_supply, gain_mix, mixed_out, normed_out):
    mixed, normed = mix_month(
        counts, own[...], before[...], after[...], pos[0:1], pos[1:2], table[...], w_supply[...], gain_mix[...]
    )
    mixed_out[...] = mixed
    normed_out[...] = normed


def early_kernel(
    counts, own, before, after, pos, table, w_supply, gain_mix,
    late_mixed, late_normed, w_qkv, head_sum, w_out, w_in, w_down, gain_ffn,
    result, mixed_out, normed_out, mixed_now, normed_now, ring,
):
    month = pl.program_id(0)
    width = own.shape[-1]

    @pl.when(month < EARLY)
    def _():
        mixed, normed = mix_month(
            counts, own[...], before[...], after[...], pos[0:1], pos[1:2], table[...], w_supply[...], gain_mix[...]
        )
        mixed_now[...] = mixed
        normed_now[...] = normed

    @pl.when(month >= EARLY)
    def _():
        mixed_now[...] = late_mixed[...]
        normed_now[...] = late_normed[...]

    @pl.when(month < LAGS)
    def _():
        mixed_out[...] = mixed_now[...]
        normed_out[...] = normed_now[...]
        ring[lax.rem(month, 4)] = mm(normed_now[...], w_qkv[:, width:]).astype(BF)

    @pl.when(month >= LAGS)
    def _():
        qkv = mm(normed_now[...], w_qkv[...]).astype(BF)
        ring[lax.rem(month, 4)] = qkv[:, width:]
        slots = [lax.rem(month + 4 - lag, 4) for lag in range(LAGS + 1)]
        attended = attend(
            qkv[:, :width], [ring[s, :, :width] for s in slots], [ring[s, :, width:] for s in slots], head_sum[...]
        )
        result[...] = finish_month(mixed_now[...], attended, w_out[...], w_in[...], w_down[...], gain_ffn[...])


def first_kernel(
    mixed, normed, earlier, w_qkv, head_sum, w_out, w_in, w_down, gain_ffn, started, result, ring,
):
    del started
    month = pl.program_id(0)
    width = normed.shape[-1]

    @pl.when(month == 0)
    def _():
        for i in range(LAGS):
            ring[i + 1] = mm(earlier[i], w_qkv[:, width:]).astype(BF)

    qkv = mm(normed[...], w_qkv[...]).astype(BF)
    ring[lax.rem(month, 4)] = qkv[:, width:]
    slots = [lax.rem(month + 4 - lag, 4) for lag in range(LAGS + 1)]
    attended = attend(
        qkv[:, :width], [ring[s, :, :width] for s in slots], [ring[s, :, width:] for s in slots], head_sum[...]
    )
    result[...] = finish_month(mixed[...], attended, w_out[...], w_in[...], w_down[...], gain_ffn[...])


def month_spec(shape, index):
    return pl.BlockSpec((None,) + shape, lambda m: (index(m),) + (0,) * len(shape))


def whole(*shape):
    return pl.BlockSpec(shape, lambda m: (0,) * len(shape))


def body(
    features, supply_counts, bank_ids, sector_ids, bank_table, sector_table,
    w_supply, w_query, w_key, w_value, w_out, w_in, w_down, gain_mix, gain_ffn,
):
    months, firms, width = features.shape
    inner = w_in.shape[1]
    devices = lax.axis_size("firm")
    me = lax.axis_index("firm")
    up = [(i, i + 1) for i in range(devices - 1)]
    down = [(j, i) for i, j in up]
    late_count = months - EARLY

    def swap(x, bits):
        return lax.ppermute(x, "firm", [(i, i ^ bits) for i in range(devices)])

    late = features[EARLY:]
    late_before = lax.ppermute(late, "firm", up)
    late_after = lax.ppermute(late, "firm", down)

    bank_local, sector_local = bank_table.shape[0], sector_table.shape[0]
    hub = jnp.concatenate(
        [bank_table, sector_table, jnp.zeros((SLOT - bank_local - sector_local, width), BF)], axis=0
    )
    hub = jnp.concatenate([hub, swap(hub, 1), swap(hub, 2), swap(hub, 3)], axis=0)

    early = features[:EARLY]
    early_before = lax.ppermute(early, "firm", up)
    early_after = lax.ppermute(early, "firm", down)

    for stage in (4, 8, 16, 32):
        hub = jnp.concatenate([hub, swap(hub, stage)], axis=0)

    bank_pos = ((bank_ids // bank_local) ^ me) * SLOT + bank_ids % bank_local
    sector_pos = ((sector_ids // sector_local) ^ me) * SLOT + bank_local + sector_ids % sector_local
    pos = jnp.stack([bank_pos, sector_pos], axis=1)

    counts = jnp.transpose(supply_counts, (0, 2, 1, 3))
    gain_mix = gain_mix.reshape(1, width)
    gain_ffn = gain_ffn.reshape(1, width)
    w_qkv = jnp.concatenate([w_query, w_key, w_value], axis=1)
    head_sum = head_matrix(width)
    hub_rows = hub.shape[0]

    mix_flops = 2 * firms * width * (3 * width + 3 * firms + hub_rows)
    end_flops = 2 * firms * width * (8 * width + 2 * inner)

    def cost(mixes, ends):
        return pl.CostEstimate(
            flops=mixes * mix_flops + ends * end_flops,
            bytes_accessed=mixes * firms * width * 24 + ends * firms * width * 10,
            transcendentals=ends * firms * (inner + 4 * width),
        )

    f32_month = (firms, width)
    late_mixed, late_normed = pl.pallas_call(
        late_kernel,
        grid=(late_count,),
        in_specs=[
            month_spec((3, firms, firms), lambda m: m + EARLY),
            month_spec(f32_month, lambda m: m + EARLY),
            month_spec(f32_month, lambda m: m),
            month_spec(f32_month, lambda m: m),
            month_spec((2, firms), lambda m: m + EARLY),
            whole(hub_rows, width),
            whole(width, width),
            whole(1, width),
        ],
        out_specs=[month_spec(f32_month, lambda m: m)] * 2,
        out_shape=[
            jax.ShapeDtypeStruct((late_count, firms, width), F32),
            jax.ShapeDtypeStruct((late_count, firms, width), BF),
        ],
        cost_estimate=cost(late_count, 0),
        name="late_mix",
    )(counts, features, late_before, late_after, pos, hub, w_supply, gain_mix)

    earlier = lax.ppermute(late_normed, "tm", [(i, i + 1) for i in range(lax.axis_size("tm") - 1)])

    clamp = lambda m: jnp.minimum(m, EARLY - 1)
    tail = lambda m: jnp.maximum(m - EARLY, 0)
    first = lambda m: jnp.minimum(m, LAGS - 1)
    weights = (w_qkv, head_sum, w_out, w_in, w_down, gain_ffn)
    weight_specs = [
        whole(width, 3 * width), whole(width, width), whole(width, width),
        whole(width, inner), whole(inner, width), whole(1, width),
    ]
    started, first_mixed, first_normed = pl.pallas_call(
        early_kernel,
        grid=(months,),
        in_specs=[
            month_spec((3, firms, firms), clamp),
            month_spec(f32_month, clamp),
            month_spec(f32_month, clamp),
            month_spec(f32_month, clamp),
            month_spec((2, firms), clamp),
            whole(hub_rows, width),
            whole(width, width),
            whole(1, width),
            month_spec(f32_month, tail),
            month_spec(f32_month, tail),
        ] + weight_specs,
        out_specs=[
            month_spec(f32_month, lambda m: jnp.maximum(m, LAGS)),
            month_spec(f32_month, first),
            month_spec(f32_month, first),
        ],
        out_shape=[
            jax.ShapeDtypeStruct((months, firms, width), BF),
            jax.ShapeDtypeStruct((LAGS, firms, width), F32),
            jax.ShapeDtypeStruct((LAGS, firms, width), BF),
        ],
        scratch_shapes=[
            pltpu.VMEM((firms, width), F32),
            pltpu.VMEM((firms, width), BF),
            pltpu.VMEM((4, firms, 2 * width), BF),
        ],
        cost_estimate=cost(EARLY, months - LAGS),
        name="early_mix_and_finish",
    )(counts, features, early_before, early_after, pos, hub, w_supply, gain_mix, late_mixed, late_normed, *weights)

    return pl.pallas_call(
        first_kernel,
        grid=(LAGS,),
        in_specs=[
            month_spec(f32_month, lambda m: m),
            month_spec(f32_month, lambda m: m),
            whole(LAGS, firms, width),
        ] + weight_specs + [pl.BlockSpec(memory_space=pl.ANY)],
        out_specs=month_spec(f32_month, lambda m: m),
        out_shape=jax.ShapeDtypeStruct((months, firms, width), BF),
        scratch_shapes=[pltpu.VMEM((4, firms, 2 * width), BF)],
        input_output_aliases={9: 0},
        cost_estimate=cost(0, LAGS),
        name="first_finish",
    )(first_mixed, first_normed, earlier, *weights, started)


def solution(mesh):
    in_specs = (
        P("tm", "firm", None),
        P("tm", "firm", None, None),
        P("tm", "firm"),
        P("tm", "firm"),
        P("firm", None),
        P("firm", None),
    ) + (P(),) * 9
    return jax.shard_map(body, mesh=mesh, in_specs=in_specs, out_specs=P("tm", "firm", None), check_vma=False)
```

time: 348 us -> 120 us (0.34)
  the two profiles are of different devices: /device:TPU:1 before, /device:TPU:25 now
where the time goes in v1:
time: 120 us; the launch traced here: 119 us
  starting transfers between devices  49.5 us (41%)
  Pallas kernels  28.6 us (24%)
  local copies, waits for them, and re-layouts  19.1 us (16%)
  waiting for transfers between devices  17.8 us (15%)
  other arithmetic  3.59 us (3%)
    ppermute x1, starting transfers between devices, body(): lax.ppermute(late_normed, 'tm', [(i, i + 1) for i in range(lax.axis_size(...  19.5 us
    ppermute x7, waiting for transfers between devices, swap(): return lax.ppermute(x, 'firm', [(i, i ^ bits) for i in range(devices)])  17.8 us
    pallas_call x1, Pallas kernels, body(): pl.pallas_call(early_kernel, grid=(months,), in_specs=[month_spec((3, fir...  16.2 us
    concatenate x4, local copies, waits for them, and re-layouts, body(): hub = jnp.concatenate([hub, swap(hub, stage)], axis=0)  11.2 us
    ppermute x7, starting transfers between devices, swap(): return lax.ppermute(x, 'firm', [(i, i ^ bits) for i in range(devices)])  9.82 us
    ppermute x1, starting transfers between devices, body(): early_after = lax.ppermute(early, 'firm', down)  8.48 us
    ppermute x1, starting transfers between devices, body(): late_after = lax.ppermute(late, 'firm', down)  7.86 us
    pallas_call x1, Pallas kernels, body(): pl.pallas_call(first_kernel, grid=(LAGS,), in_specs=[month_spec(f32_month...  7.2 us
  transfers between devices with their start and end apart: 12, of which 4 were waited for; matrix products, arithmetic and copies ran while one was open for 17% of the time, Pallas kernels for 18%

profile of v1, /device:TPU:25, one launch (start us, length us, event | category | flops | bytes accessed | tf_op | source)
XLA Modules:
  0.0 118.8 jit_solution(9176816571348215416)
XLA Ops:
  0.0 0.7 pad_maximum_fusion
  0.7 3.0 %collective-permute-start.2 = (bf16[16,256]{1,0:T(8,128)(2,1)S(1)}, bf16[16,256]{1,0:T(8,128)(2,1)S(1)}, u32[]{:S(2)}, u32[]{:S(2)}) collective-permute-start(bf16[16,256]{1,0:T(8,128)(2,1)S(1)} %pad_maximum_fusion), channel_id=1, source_target_pairs={{0,1},{1,0},{2,3},{3,2},{4,5},{5,4},{6,7},{7,6},{8,9},{9,8},{10,11... | collective-permute-start | bytes 24584 | tf_op jit(solution)/shard_map/ppermute | solution.py:154
  3.7 5.1 %collective-permute-start.3 = (bf16[16,256]{1,0:T(8,128)(2,1)S(1)}, bf16[16,256]{1,0:T(8,128)(2,1)S(1)}, u32[]{:S(2)}, u32[]{:S(2)}) collective-permute-start(bf16[16,256]{1,0:T(8,128)(2,1)S(1)} %pad_maximum_fusion), channel_id=1, source_target_pairs={{0,2},{1,3},{2,0},{3,1},{4,6},{5,7},{6,4},{7,5},{8,10},{9,11},{10,... | collective-permute-start | bytes 24584 | tf_op jit(solution)/shard_map/ppermute | solution.py:154
  8.8 1.0 slice.7
  9.8 7.9 %collective-permute-start.10 = (bf16[3,256,256]{2,1,0:T(8,128)(2,1)S(1)}, bf16[3,256,256]{2,1,0:T(8,128)(2,1)S(1)}, u32[]{:S(2)}, u32[]{:S(2)}) collective-permute-start(bf16[3,256,256]{2,1,0:T(8,128)(2,1)S(1)} %slice.7), channel_id=1, source_target_pairs={{1,0},{2,1},{3,2},{4,3},{5,4},{6,5},{7,6},{8,7},{9,8},{10,9},{11,1... | collective-permute-start | bytes 1179656 | tf_op jit(solution)/shard_map/ppermute | solution.py:158
  17.7 1.9 %collective-permute-start.9 = (bf16[3,256,256]{2,1,0:T(8,128)(2,1)S(1)}, bf16[3,256,256]{2,1,0:T(8,128)(2,1)S(1)}, u32[]{:S(2)}, u32[]{:S(2)}) collective-permute-start(bf16[3,256,256]{2,1,0:T(8,128)(2,1)S(1)} %slice.7), channel_id=1, source_target_pairs={{0,1},{1,2},{2,3},{3,4},{4,5},{5,6},{6,7},{7,8},{8,9},{9,10},{10,1... | collective-permute-start | bytes 1179656 | tf_op jit(solution)/shard_map/ppermute | solution.py:157
  19.6 0.7 fusion.3
  20.4 0.7 fusion.7
  21.1 0.9 constant_dynamic-update-slice_fusion.2
  22.0 1.1 slice.6
  23.1 1.9 %collective-permute-start = (bf16[5,256,256]{2,1,0:T(8,128)(2,1)S(1)}, bf16[5,256,256]{2,1,0:T(8,128)(2,1)}, u32[]{:S(2)}, u32[]{:S(2)}) collective-permute-start(bf16[5,256,256]{2,1,0:T(8,128)(2,1)S(1)} %slice.6), channel_id=1, source_target_pairs={{0,1},{1,2},{2,3},{3,4},{4,5},{5,6},{6,7},{7,8},{8,9},{9,10},{10,1... | collective-permute-start | bytes 1966088 | tf_op jit(solution)/shard_map/ppermute | solution.py:167
  25.1 8.5 %collective-permute-start.1 = (bf16[5,256,256]{2,1,0:T(8,128)(2,1)S(1)}, bf16[5,256,256]{2,1,0:T(8,128)(2,1)}, u32[]{:S(2)}, u32[]{:S(2)}) collective-permute-start(bf16[5,256,256]{2,1,0:T(8,128)(2,1)S(1)} %slice.6), channel_id=1, source_target_pairs={{1,0},{2,1},{3,2},{4,3},{5,4},{6,5},{7,6},{8,7},{9,8},{10,9},{11,1... | collective-permute-start | bytes 1966088 | tf_op jit(solution)/shard_map/ppermute | solution.py:168
  33.6 1.4 %concatenate.27 = bf16[64,256]{1,0:T(8,128)(2,1)S(1)} concatenate(bf16[8,256]{1,0:T(8,128)(2,1)} %param.19, bf16[4,256]{1,0:T(4,128)(2,1)} %param.20, bf16[4,256]{1,0:T(4,128)(2,1)S(1)} %broadcast_in_dim.11, bf16[16,256]{1,0:T(8,128)(2,1)S(1)} %collective-permute-done.2, bf16[16,256]{1,0:T(8,128)(2,1)S(1)} %collective-permute-done.3, bf16[16,256]{1,0:T(8,128)(2,1)S(1)} %collective-permute-done.4), dimensions={0} | concatenate | bytes 65536 | tf_op jit(solution)/shard_map/concatenate | solution.py:164
  35.1 0.9 constant_dynamic-update-slice_fusion.1
  36.0 2.2 %collective-permute-done.5 = bf16[64,256]{1,0:T(8,128)(2,1)S(1)} collective-permute-done((bf16[64,256]{1,0:T(8,128)(2,1)S(1)}, bf16[64,256]{1,0:T(8,128)(2,1)S(1)}, u32[]{:S(2)}, u32[]{:S(2)}) %collective-permute-start.5) | collective-permute-done | bytes 32800 | tf_op jit(solution)/shard_map/ppermute | solution.py:154
  38.2 1.4 %concatenate.28 = bf16[128,256]{1,0:T(8,128)(2,1)S(1)} concatenate(bf16[8,256]{1,0:T(8,128)(2,1)} %param.19, bf16[4,256]{1,0:T(4,128)(2,1)} %param.20, bf16[4,256]{1,0:T(4,128)(2,1)S(1)} %broadcast_in_dim.11, bf16[16,256]{1,0:T(8,128)(2,1)S(1)} %collective-permute-done.2, bf16[16,256]{1,0:T(8,128)(2,1)S(1)} %collective-permute-done.3, ...), dimensions={0} | concatenate | bytes 131072 | tf_op jit(solution)/shard_map/concatenate | solution.py:171
  39.7 0.9 constant_dynamic-update-slice_fusion.w_qkv
  40.6 4.8 %collective-permute-done.6 = bf16[128,256]{1,0:T(8,128)(2,1)S(1)} collective-permute-done((bf16[128,256]{1,0:T(8,128)(2,1)S(1)}, bf16[128,256]{1,0:T(8,128)(2,1)S(1)}, u32[]{:S(2)}, u32[]{:S(2)}) %collective-permute-start.6) | collective-permute-done | bytes 65568 | tf_op jit(solution)/shard_map/ppermute | solution.py:154
  45.5 1.4 %concatenate.29 = bf16[256,256]{1,0:T(8,128)(2,1)S(1)} concatenate(bf16[8,256]{1,0:T(8,128)(2,1)} %param.19, bf16[4,256]{1,0:T(4,128)(2,1)} %param.20, bf16[4,256]{1,0:T(4,128)(2,1)S(1)} %broadcast_in_dim.11, bf16[16,256]{1,0:T(8,128)(2,1)S(1)} %collective-permute-done.2, bf16[16,256]{1,0:T(8,128)(2,1)S(1)} %collective-permute-done.3, ...), dimensions={0} | concatenate | bytes 262144 | tf_op jit(solution)/shard_map/concatenate | solution.py:171
  47.4 0.6 pad_add_fusion.pos
  48.0 5.4 %collective-permute-done.7 = bf16[256,256]{1,0:T(8,128)(2,1)S(1)} collective-permute-done((bf16[256,256]{1,0:T(8,128)(2,1)S(1)}, bf16[256,256]{1,0:T(8,128)(2,1)S(1)}, u32[]{:S(2)}, u32[]{:S(2)}) %collective-permute-start.7) | collective-permute-done | bytes 131104 | tf_op jit(solution)/shard_map/ppermute | solution.py:154
  53.4 1.4 %concatenate.30 = bf16[512,256]{1,0:T(8,128)(2,1)S(1)} concatenate(bf16[8,256]{1,0:T(8,128)(2,1)} %param.19, bf16[4,256]{1,0:T(4,128)(2,1)} %param.20, bf16[4,256]{1,0:T(4,128)(2,1)S(1)} %broadcast_in_dim.11, bf16[16,256]{1,0:T(8,128)(2,1)S(1)} %collective-permute-done.2, bf16[16,256]{1,0:T(8,128)(2,1)S(1)} %collective-permute-done.3, ...), dimensions={0} | concatenate | bytes 524288 | tf_op jit(solution)/shard_map/concatenate | solution.py:171
  54.8 1.0 collective-permute-start.8
  55.8 0.8 select_convert_fusion.head_sum
  56.6 5.4 %collective-permute-done.8 = bf16[512,256]{1,0:T(8,128)(2,1)S(1)} collective-permute-done((bf16[512,256]{1,0:T(8,128)(2,1)S(1)}, bf16[512,256]{1,0:T(8,128)(2,1)S(1)}, u32[]{:S(2)}, u32[]{:S(2)}) %collective-permute-start.8) | collective-permute-done | bytes 262176 | tf_op jit(solution)/shard_map/ppermute | solution.py:154
  62.0 7.0 %concatenate.31.table = bf16[1024,256]{1,0:T(8,128)(2,1)} concatenate(bf16[8,256]{1,0:T(8,128)(2,1)} %param.19, bf16[4,256]{1,0:T(4,128)(2,1)} %param.20, bf16[4,256]{1,0:T(4,128)(2,1)S(1)} %broadcast_in_dim.11, bf16[16,256]{1,0:T(8,128)(2,1)S(1)} %collective-permute-done.2, bf16[16,256]{1,0:T(8,128)(2,1)S(1)} %collective-permute-done.3, ...), dimensions={0} | concatenate | bytes 1048576 | tf_op jit(solution)/shard_map/concatenate | solution.py:171
  69.1 0.7 copy-done
  69.9 5.2 %late_mix.1 = (f32[3,256,256]{2,1,0:T(8,128)}, bf16[3,256,256]{2,1,0:T(8,128)(2,1)}) custom-call(s32[8,3,256,256]{3,2,1,0:T(8,128)} %bitcast.5, bf16[8,256,256]{2,1,0:T(8,128)(2,1)} %own.3, bf16[3,256,256]{2,1,0:T(8,128)(2,1)} %copy-done.1, bf16[3,256,256]{2,1,0:T(8,128)(2,1)} %copy-done, s32[8,2,256]{2,1,0:T(2,128)} %pad_add_fusion.pos, ...), custom_call_target="tpu_custom_call" | custom-call | flops 1006632960 | bytes 4718592 | tf_op jit(solution)/shard_map/late_mix/pallas_call | solution.py:195
  75.1 19.5 %collective-permute-start.11 = (bf16[3,256,256]{2,1,0:T(8,128)(2,1)}, bf16[3,256,256]{2,1,0:T(8,128)(2,1)S(1)}, u32[]{:S(2)}, u32[]{:S(2)}) collective-permute-start(bf16[3,256,256]{2,1,0:T(8,128)(2,1)} %get-tuple-element.11.late_normed), channel_id=1, source_target_pairs={{0,64},{64,128},{128,192},{1,65},{65,129},{129,193},{2,66},{66,130... | collective-permute-start | bytes 1179656 | tf_op jit(solution)/shard_map/ppermute | solution.py:217
  94.6 16.2 %early_mix_and_finish.1 = (bf16[8,256,256]{2,1,0:T(8,128)(2,1)}, f32[3,256,256]{2,1,0:T(8,128)}, bf16[3,256,256]{2,1,0:T(8,128)(2,1)}) custom-call(s32[8,3,256,256]{3,2,1,0:T(8,128)} %bitcast.6, bf16[8,256,256]{2,1,0:T(8,128)(2,1)} %own.3, bf16[5,256,256]{2,1,0:T(8,128)(2,1)} %collective-permute-done.before, ...), custom_call_target="tpu_custom_call" | custom-call | flops 4362076160 | bytes 11141120 | tf_op jit(solution)/shard_map/early_mix_and_finish/pallas_call | solution.py:227
  110.8 0.8 copy-done.3
  111.5 7.2 %first_finish.1 = bf16[8,256,256]{2,1,0:T(8,128)(2,1)} custom-call(f32[3,256,256]{2,1,0:T(8,128)} %get-tuple-element.12.mixed, bf16[3,256,256]{2,1,0:T(8,128)(2,1)} %get-tuple-element.13.normed, bf16[3,256,256]{2,1,0:T(8,128)(2,1)} %copy-done.3, bf16[256,768]{1,0:T(8,128)(2,1)} %copy-done.2, ...), custom_call_target="tpu_custom_call", output_to_operand_aliasing={{}: (9, {})} | custom-call | flops 1610612736 | bytes 1966080 | tf_op jit(solution)/shard_map/first_finish/pallas_call | solution.py:261
  (23 shorter events, 0.9 us)
Async XLA Ops:
  0.7 22.4 %collective-permute-start.2 = (bf16[16,256]{1,0:T(8,128)(2,1)S(1)}, bf16[16,256]{1,0:T(8,128)(2,1)S(1)}, u32[]{:S(2)}, u32[]{:S(2)}) collective-permute-start(bf16[16,256]{1,0:T(8,128)(2,1)S(1)} %pad_maximum_fusion), channel_id=1, source_target_pairs={{0,1},{1,0},{2,3},{3,2},{4,5},{5,4},{6,7},{7,6},{8,9},{9,8},{10,11... | collective-permute-start | bytes 24584 | tf_op jit(solution)/shard_map/ppermute | solution.py:154
  3.7 21.4 %collective-permute-start.3 = (bf16[16,256]{1,0:T(8,128)(2,1)S(1)}, bf16[16,256]{1,0:T(8,128)(2,1)S(1)}, u32[]{:S(2)}, u32[]{:S(2)}) collective-permute-start(bf16[16,256]{1,0:T(8,128)(2,1)S(1)} %pad_maximum_fusion), channel_id=1, source_target_pairs={{0,2},{1,3},{2,0},{3,1},{4,6},{5,7},{6,4},{7,5},{8,10},{9,11},{10,... | collective-permute-start | bytes 24584 | tf_op jit(solution)/shard_map/ppermute | solution.py:154
  8.8 24.8 %collective-permute-start.4 = (bf16[16,256]{1,0:T(8,128)(2,1)S(1)}, bf16[16,256]{1,0:T(8,128)(2,1)S(1)}, u32[]{:S(2)}, u32[]{:S(2)}) collective-permute-start(bf16[16,256]{1,0:T(8,128)(2,1)S(1)} %pad_maximum_fusion), channel_id=1, source_target_pairs={{0,3},{1,2},{2,1},{3,0},{4,7},{5,6},{6,5},{7,4},{8,11},{9,10},{10,... | collective-permute-start | bytes 24584 | tf_op jit(solution)/shard_map/ppermute | solution.py:154
  9.8 59.2 %collective-permute-start.10 = (bf16[3,256,256]{2,1,0:T(8,128)(2,1)S(1)}, bf16[3,256,256]{2,1,0:T(8,128)(2,1)S(1)}, u32[]{:S(2)}, u32[]{:S(2)}) collective-permute-start(bf16[3,256,256]{2,1,0:T(8,128)(2,1)S(1)} %slice.7), channel_id=1, source_target_pairs={{1,0},{2,1},{3,2},{4,3},{5,4},{6,5},{7,6},{8,7},{9,8},{10,9},{11,1... | collective-permute-start | bytes 1179656 | tf_op jit(solution)/shard_map/ppermute | solution.py:158
  17.7 51.3 %collective-permute-start.9 = (bf16[3,256,256]{2,1,0:T(8,128)(2,1)S(1)}, bf16[3,256,256]{2,1,0:T(8,128)(2,1)S(1)}, u32[]{:S(2)}, u32[]{:S(2)}) collective-permute-start(bf16[3,256,256]{2,1,0:T(8,128)(2,1)S(1)} %slice.7), channel_id=1, source_target_pairs={{0,1},{1,2},{2,3},{3,4},{4,5},{5,6},{6,7},{7,8},{8,9},{9,10},{10,1... | collective-permute-start | bytes 1179656 | tf_op jit(solution)/shard_map/ppermute | solution.py:157
  23.1 71.4 %collective-permute-start = (bf16[5,256,256]{2,1,0:T(8,128)(2,1)S(1)}, bf16[5,256,256]{2,1,0:T(8,128)(2,1)}, u32[]{:S(2)}, u32[]{:S(2)}) collective-permute-start(bf16[5,256,256]{2,1,0:T(8,128)(2,1)S(1)} %slice.6), channel_id=1, source_target_pairs={{0,1},{1,2},{2,3},{3,4},{4,5},{5,6},{6,7},{7,8},{8,9},{9,10},{10,1... | collective-permute-start | bytes 1966088 | tf_op jit(solution)/shard_map/ppermute | solution.py:167
  25.1 69.5 %collective-permute-start.1 = (bf16[5,256,256]{2,1,0:T(8,128)(2,1)S(1)}, bf16[5,256,256]{2,1,0:T(8,128)(2,1)}, u32[]{:S(2)}, u32[]{:S(2)}) collective-permute-start(bf16[5,256,256]{2,1,0:T(8,128)(2,1)S(1)} %slice.6), channel_id=1, source_target_pairs={{1,0},{2,1},{3,2},{4,3},{5,4},{6,5},{7,6},{8,7},{9,8},{10,9},{11,1... | collective-permute-start | bytes 1966088 | tf_op jit(solution)/shard_map/ppermute | solution.py:168
  35.0 3.2 %collective-permute-start.5 = (bf16[64,256]{1,0:T(8,128)(2,1)S(1)}, bf16[64,256]{1,0:T(8,128)(2,1)S(1)}, u32[]{:S(2)}, u32[]{:S(2)}) collective-permute-start(bf16[64,256]{1,0:T(8,128)(2,1)S(1)} %concatenate.27), channel_id=1, source_target_pairs={{0,4},{1,5},{2,6},{3,7},{4,0},{5,1},{6,2},{7,3},{8,12},{9,13},{10,... | collective-permute-start | bytes 98312 | tf_op jit(solution)/shard_map/ppermute | solution.py:154
  39.6 5.8 %collective-permute-start.6 = (bf16[128,256]{1,0:T(8,128)(2,1)S(1)}, bf16[128,256]{1,0:T(8,128)(2,1)S(1)}, u32[]{:S(2)}, u32[]{:S(2)}) collective-permute-start(bf16[128,256]{1,0:T(8,128)(2,1)S(1)} %concatenate.28), channel_id=1, source_target_pairs={{0,8},{1,9},{2,10},{3,11},{4,12},{5,13},{6,14},{7,15},{8,0},{9,1},... | collective-permute-start | bytes 196616 | tf_op jit(solution)/shard_map/ppermute | solution.py:154
  40.6 53.9 %copy-start.2 = (bf16[256,768]{1,0:T(8,128)(2,1)}, bf16[256,768]{1,0:T(8,128)(2,1)S(1)}, u32[]{:S(2)}) copy-start(bf16[256,768]{1,0:T(8,128)(2,1)S(1)} %constant_dynamic-update-slice_fusion.w_qkv) | copy-start | bytes 1179652
  46.9 6.6 %collective-permute-start.7 = (bf16[256,256]{1,0:T(8,128)(2,1)S(1)}, bf16[256,256]{1,0:T(8,128)(2,1)S(1)}, u32[]{:S(2)}, u32[]{:S(2)}) collective-permute-start(bf16[256,256]{1,0:T(8,128)(2,1)S(1)} %concatenate.29), channel_id=1, source_target_pairs={{0,16},{1,17},{2,18},{3,19},{4,20},{5,21},{6,22},{7,23},{8,24},{9,... | collective-permute-start | bytes 393224 | tf_op jit(solution)/shard_map/ppermute | solution.py:154
  54.8 7.2 %collective-permute-start.8 = (bf16[512,256]{1,0:T(8,128)(2,1)S(1)}, bf16[512,256]{1,0:T(8,128)(2,1)S(1)}, u32[]{:S(2)}, u32[]{:S(2)}) collective-permute-start(bf16[512,256]{1,0:T(8,128)(2,1)S(1)} %concatenate.30), channel_id=1, source_target_pairs={{0,32},{1,33},{2,34},{3,35},{4,36},{5,37},{6,38},{7,39},{8,40},{9,... | collective-permute-start | bytes 786440 | tf_op jit(solution)/shard_map/ppermute | solution.py:154
  69.0 0.7 copy-start
  69.0 0.9 copy-start.1
  75.1 35.7 %collective-permute-start.11 = (bf16[3,256,256]{2,1,0:T(8,128)(2,1)}, bf16[3,256,256]{2,1,0:T(8,128)(2,1)S(1)}, u32[]{:S(2)}, u32[]{:S(2)}) collective-permute-start(bf16[3,256,256]{2,1,0:T(8,128)(2,1)} %get-tuple-element.11.late_normed), channel_id=1, source_target_pairs={{0,64},{64,128},{128,192},{1,65},{65,129},{129,193},{2,66},{66,130... | collective-permute-start | bytes 1179656 | tf_op jit(solution)/shard_map/ppermute | solution.py:217
  110.8 0.8 copy-start.3

commit v2 on v0

v2 whole, which is shorter than its diff:
```python
import math

import jax
import jax.numpy as jnp
from jax import lax
from jax.experimental import pallas as pl
from jax.experimental.pallas import tpu as pltpu
from jax.sharding import PartitionSpec as P

HEADS = 4
LAGS = 3
HALF = 4
SLOT = 16
LOG2 = math.log(2.0)
GELU = math.sqrt(2.0 / math.pi)
BF = jnp.bfloat16
F32 = jnp.float32
VM = pl.BlockSpec(memory_space=pltpu.VMEM)
SM = pl.BlockSpec(memory_space=pltpu.SMEM)
ANY = pl.BlockSpec(memory_space=pl.ANY)


def mm(a, b):
    return jnp.dot(a, b, preferred_element_type=F32)


def rms_norm(values, gain):
    scale = lax.rsqrt(jnp.mean(values * values, axis=-1, keepdims=True) + 1e-06)
    return values * scale * gain


def head_matrix(width):
    size = width // HEADS
    row = lax.broadcasted_iota(jnp.int32, (width, width), 0) // size
    col = lax.broadcasted_iota(jnp.int32, (width, width), 1) // size
    return jnp.where(row == col, 0.5 / math.sqrt(size), 0.0).astype(BF)


def attend(query, keys, values, head_sum):
    total = jnp.zeros(query.shape, F32)
    for key, value in zip(keys, values):
        value = value.astype(F32)
        total = total + (value + jnp.tanh(mm(query * key, head_sum) - LOG2) * value)
    return (0.5 * total).astype(BF)


def finish(mixed, attended, w_out, w_in, w_down, gain_ffn):
    second = mixed + mm(attended, w_out)
    normed2 = rms_norm(second, gain_ffn).astype(BF)
    x = mm(normed2, w_in)
    half = 0.5 * x
    inner = (half + half * jnp.tanh(x * (GELU + (GELU * 0.044715) * (x * x)))).astype(BF)
    return (second + mm(inner, w_down)).astype(BF)


def stack(parts):
    return jnp.concatenate(parts, axis=0)


def lagged(parts, count):
    return [stack(parts[LAGS - lag : LAGS - lag + count]) for lag in range(LAGS + 1)]


def own_kernel(where, counts, own, w_supply, base, tiles, scale):
    even = 2 - 2 * where[1]
    odd = 2 * where[1]
    for m in range(own.shape[0]):
        part = [counts[m, k].astype(F32) for k in range(3)]
        degree = 1.0 + jnp.sum(part[0] + part[1] + part[2], axis=-1, keepdims=True)
        inverse = lax.rsqrt(degree)
        feats = own[m]
        supplied = mm(feats, w_supply[...]).astype(BF)
        base[m] = feats.astype(F32) + inverse * mm(part[1].astype(BF), supplied)
        scale[m] = jnp.broadcast_to(inverse, scale.shape[1:])
        tiles[m, 0] = counts[m, even].astype(F32).astype(BF)
        tiles[m, 1] = counts[m, odd].astype(F32).astype(BF)


def mix(m, base, tiles, scale, even_rows, odd_rows, w_supply):
    message = mm(tiles[m, 0], mm(even_rows, w_supply).astype(BF))
    message = message + mm(tiles[m, 1], mm(odd_rows, w_supply).astype(BF))
    spread = jnp.concatenate([scale[m]] * (base.shape[-1] // scale.shape[-1]), axis=-1)
    return base + spread * message


def late_kernel(
    where, base, tiles, scale, even_rows, odd_rows, banks, sectors, *rest,
):
    tables, (w_supply, w_query, w_key, w_value, gain_mix) = rest[:4], rest[4:9]
    early_base, mixed_out, normed_out, query_out, key_out, value_out = rest[9:]
    me = where[0]
    rows_each, firms = tables[0].shape[0], base.shape[1]
    row = lax.broadcasted_iota(jnp.int32, (rows_each, firms), 0)
    normed = []
    for m in list(range(HALF, 2 * HALF)) + list(range(HALF)):
        bank, sector = banks[m : m + 1], sectors[m : m + 1]
        bank = (lax.shift_right_logical(bank, 3) ^ me) * SLOT + (bank & 7)
        sector = (lax.shift_right_logical(sector, 2) ^ me) * SLOT + 8 + (sector & 3)
        total = base[m]
        for i, table in enumerate(tables):
            chosen = jnp.where((row == bank - i * rows_each) | (row == sector - i * rows_each), 1.0, 0.0)
            total = total + lax.dot_general(
                chosen.astype(BF), table[...], (((0,), (0,)), ((), ())), preferred_element_type=F32
            )
        if m < HALF:
            early_base[m] = total
        else:
            mixed = mix(m, total, tiles, scale, even_rows[m - HALF], odd_rows[m - HALF], w_supply[...])
            mixed_out[m - HALF] = mixed
            normed.append(rms_norm(mixed, gain_mix[...]).astype(BF))
            if m >= 2 * HALF - LAGS:
                normed_out[m - 2 * HALF + LAGS] = normed[-1]
    shape = query_out.shape
    rows = stack(normed)
    query_out[...] = mm(rows, w_query[...]).astype(BF).reshape(shape)
    key_out[...] = mm(rows, w_key[...]).astype(BF).reshape(shape)
    value_out[...] = mm(rows, w_value[...]).astype(BF).reshape(shape)


def write_back(final, buffer, result, sems, first):
    firms = buffer.shape[1]
    copies = []
    for i in range(buffer.shape[0]):
        buffer[i] = final[i * firms : (i + 1) * firms]
        copies.append(pltpu.make_async_copy(buffer.at[i], result.at[first + i], sems.at[i]))
        copies[-1].start()
    for copy in copies:
        copy.wait()


def last_kernel(mixed, query, key, value, w_out, w_in, w_down, gain_ffn, result, buffer, sems):
    attended = attend(
        query[LAGS], [key[LAGS - j] for j in range(LAGS + 1)], [value[LAGS - j] for j in range(LAGS + 1)],
        head_matrix(query.shape[-1]),
    )
    final = finish(mixed[LAGS], attended, w_out[...], w_in[...], w_down[...], gain_ffn[...])
    write_back(final, buffer, result, sems, 2 * HALF - 1)


def early_kernel(
    base, tiles, scale, even_rows, odd_rows, late_mixed, late_query, late_key, late_value,
    w_supply, w_query, w_key, w_value, gain_mix, w_out, w_in, w_down, gain_ffn, started,
    result, mixed_out, query_out, key_out, value_out, buffer, sems,
):
    del started
    firms = base.shape[1]
    mixed, normed = [], []
    for m in range(HALF):
        mixed.append(mix(m, base[m], tiles, scale, even_rows[m], odd_rows[m], w_supply[...]))
        normed.append(rms_norm(mixed[-1], gain_mix[...]).astype(BF))
    rows = stack(normed)
    cut = lambda rows: [rows[i * firms : (i + 1) * firms] for i in range(HALF)]
    query = cut(mm(rows, w_query[...]).astype(BF))
    key = cut(mm(rows, w_key[...]).astype(BF))
    value = cut(mm(rows, w_value[...]).astype(BF))
    for m in range(LAGS):
        mixed_out[m], query_out[m], key_out[m], value_out[m] = mixed[m], query[m], key[m], value[m]
    keys = lagged(key + [late_key[m] for m in range(LAGS)], HALF)
    values = lagged(value + [late_value[m] for m in range(LAGS)], HALF)
    queries = stack([query[LAGS]] + [late_query[m] for m in range(LAGS)])
    attended = attend(queries, keys, values, head_matrix(base.shape[-1]))
    total = stack([mixed[LAGS]] + [late_mixed[m] for m in range(LAGS)])
    final = finish(total, attended, w_out[...], w_in[...], w_down[...], gain_ffn[...])
    write_back(final, buffer, result, sems, LAGS)


def first_kernel(
    earlier, mixed, query, key, value, w_key, w_value, w_out, w_in, w_down, gain_ffn, started, result, buffer, sems,
):
    del started
    firms, width = mixed.shape[1:]
    rows = earlier[...].reshape(LAGS * firms, width)
    cut = lambda rows: [rows[i * firms : (i + 1) * firms] for i in range(LAGS)]
    keys = lagged(cut(mm(rows, w_key[...]).astype(BF)) + [key[m] for m in range(LAGS)], LAGS)
    values = lagged(cut(mm(rows, w_value[...]).astype(BF)) + [value[m] for m in range(LAGS)], LAGS)
    flat = (LAGS * firms, width)
    attended = attend(query[...].reshape(flat), keys, values, head_matrix(width))
    final = finish(mixed[...].reshape(flat), attended, w_out[...], w_in[...], w_down[...], gain_ffn[...])
    write_back(final, buffer, result, sems, 0)


def body(
    features, supply_counts, bank_ids, sector_ids, bank_table, sector_table,
    w_supply, w_query, w_key, w_value, w_out, w_in, w_down, gain_mix, gain_ffn,
):
    months, firms, width = features.shape
    inner = w_in.shape[1]
    devices = lax.axis_size("firm")
    me = lax.axis_index("firm")
    where = jnp.stack([me, me & 1]).astype(jnp.int32)
    even_pairs = [(i, i ^ 1) for i in range(devices)]
    odd_pairs = [(i, i + 1) for i in range(1, devices - 1, 2)]
    odd_pairs = odd_pairs + [(j, i) for i, j in odd_pairs]

    def swap(x, bits):
        return lax.ppermute(x, "firm", [(i, i ^ bits) for i in range(devices)])

    late = features[HALF:]
    late_even = lax.ppermute(late, "firm", even_pairs)
    late_odd = lax.ppermute(late, "firm", odd_pairs)

    spare = SLOT - bank_table.shape[0] - sector_table.shape[0]
    hub = jnp.concatenate([bank_table, sector_table, jnp.zeros((spare, width), BF)], axis=0)
    hub, late = lax.optimization_barrier((hub, late))
    hub = jnp.concatenate([hub] + [swap(hub, i) for i in (1, 2, 3)], axis=0)

    early = features[:HALF]
    early_even = lax.ppermute(early, "firm", even_pairs)
    early_odd = lax.ppermute(early, "firm", odd_pairs)

    hub = jnp.concatenate([hub] + [swap(hub, i) for i in (4, 8, 12)], axis=0)
    tables = [hub] + [swap(hub, i) for i in (16, 32, 48)]

    counts = jnp.transpose(supply_counts, (0, 2, 1, 3))
    gain_mix = gain_mix.reshape(1, width)
    gain_ffn = gain_ffn.reshape(1, width)

    def cost(units, mebibytes):
        return pl.CostEstimate(
            flops=2 * units * firms * width * width, bytes_accessed=mebibytes << 20, transcendentals=0
        )

    def like(count, dtype, lanes=width):
        return jax.ShapeDtypeStruct((count, firms, lanes), dtype)

    params = pltpu.CompilerParams(vmem_limit_bytes=28 << 20)
    step = lambda *shape: pl.BlockSpec((2,) + shape, lambda m: (m,) + (0,) * len(shape))
    base, tiles, scale = pl.pallas_call(
        own_kernel,
        grid=(months // 2,),
        in_specs=[
            SM, step(3, firms, firms), step(firms, width), pl.BlockSpec((width, width), lambda m: (0, 0)),
        ],
        out_specs=[step(firms, width), step(2, firms, firms), step(firms, 128)],
        out_shape=[
            like(months, F32), jax.ShapeDtypeStruct((months, 2, firms, firms), BF), like(months, F32, 128),
        ],
        compiler_params=params,
        cost_estimate=cost(16, 12),
        name="own_block",
    )(where, counts, features, w_supply)

    early_base, late_mixed, late_normed, late_query, late_key, late_value = pl.pallas_call(
        late_kernel,
        in_specs=[SM] + [VM] * 16,
        out_specs=[VM] * 6,
        out_shape=[
            like(HALF, F32), like(HALF, F32), like(LAGS, BF), like(HALF, BF), like(HALF, BF), like(HALF, BF),
        ],
        compiler_params=params,
        cost_estimate=cost(60, 12),
        name="late_months",
    )(
        where, base, tiles, scale, late_even, late_odd, bank_ids, sector_ids, *tables,
        w_supply, w_query, w_key, w_value, gain_mix,
    )

    earlier = lax.ppermute(late_normed, "tm", [(i, i + 1) for i in range(lax.axis_size("tm") - 1)])
    end_weights = (w_out, w_in, w_down, gain_ffn)

    def scratch(count):
        return [pltpu.VMEM((count, firms, width), BF), pltpu.SemaphoreType.DMA((count,))]

    result = pl.pallas_call(
        last_kernel,
        in_specs=[VM] * 8,
        out_specs=ANY,
        out_shape=like(months, BF),
        scratch_shapes=scratch(1),
        compiler_params=params,
        cost_estimate=cost(16, 3),
        name="last_month",
    )(late_mixed, late_query, late_key, late_value, *end_weights)

    result, mixed, query, key, value = pl.pallas_call(
        early_kernel,
        in_specs=[VM] * 18 + [ANY],
        out_specs=[ANY] + [VM] * 4,
        out_shape=[like(months, BF), like(LAGS, F32), like(LAGS, BF), like(LAGS, BF), like(LAGS, BF)],
        scratch_shapes=scratch(HALF),
        input_output_aliases={18: 0},
        compiler_params=params,
        cost_estimate=cost(90, 8),
        name="early_months",
    )(
        early_base, tiles, scale, early_even, early_odd, late_mixed, late_query, late_key, late_value,
        w_supply, w_query, w_key, w_value, gain_mix, *end_weights, result,
    )

    return pl.pallas_call(
        first_kernel,
        in_specs=[VM] * 11 + [ANY],
        out_specs=ANY,
        out_shape=like(months, BF),
        scratch_shapes=scratch(LAGS),
        input_output_aliases={11: 0},
        compiler_params=params,
        cost_estimate=cost(54, 4),
        name="first_months",
    )(earlier, mixed, query, key, value, w_key, w_value, *end_weights, result)


def solution(mesh):
    in_specs = (
        P("tm", "firm", None),
        P("tm", "firm", None, None),
        P("tm", "firm"),
        P("tm", "firm"),
        P("firm", None),
        P("firm", None),
    ) + (P(),) * 9
    return jax.shard_map(body, mesh=mesh, in_specs=in_specs, out_specs=P("tm", "firm", None), check_vma=False)
```

time: 348 us -> 80.3 us (0.23)
  the two profiles are of different devices: /device:TPU:1 before, /device:TPU:25 now
where the time goes in v2:
time: 80.3 us; the launch traced here: 80 us
  starting transfers between devices  46.7 us (58%)
  Pallas kernels  18.3 us (23%)
  waiting for transfers between devices  9.28 us (12%)
  local copies, waits for them, and re-layouts  5.28 us (7%)
    ppermute x9, starting transfers between devices, swap(): return lax.ppermute(x, 'firm', [(i, i ^ bits) for i in range(devices)])  26.7 us
    ppermute x9, waiting for transfers between devices, swap(): return lax.ppermute(x, 'firm', [(i, i ^ bits) for i in range(devices)])  9.27 us
    ppermute x1, starting transfers between devices, body(): lax.ppermute(late_normed, 'tm', [(i, i + 1) for i in range(lax.axis_size(...  8.75 us
    pallas_call x1, Pallas kernels, body(): pl.pallas_call(early_kernel, in_specs=[VM] * 18 + [ANY], out_specs=[ANY]...  5.49 us
    ppermute x1, starting transfers between devices, body(): late_odd = lax.ppermute(late, 'firm', odd_pairs)  5.16 us
    pallas_call x1, Pallas kernels, body(): pl.pallas_call(late_kernel, in_specs=[SM] + [VM] * 16, out_specs=[VM] * 6...  4.42 us
    ppermute x1, starting transfers between devices, body(): early_odd = lax.ppermute(early, 'firm', odd_pairs)  4.35 us
    pallas_call x1, Pallas kernels, body(): pl.pallas_call(first_kernel, in_specs=[VM] * 11 + [ANY], out_specs=ANY, o...  3.64 us
  transfers between devices with their start and end apart: 14, of which 4 were waited for; matrix products, arithmetic and copies ran while one was open for 0% of the time, Pallas kernels for 18%

profile of v2, /device:TPU:25, one launch (start us, length us, event | category | flops | bytes accessed | tf_op | source)
XLA Modules:
  0.0 80.0 jit_solution(1742733919742806438)
XLA Ops:
  0.0 2.3 %fusion = (bf16[4,256,256]{2,1,0:T(8,128)(2,1)}, bf16[4,256,256]{2,1,0:T(8,128)(2,1)}) fusion(bf16[8,256,256]{2,1,0:T(8,128)(2,1)} %own.1), kind=kLoop, calls=%fused_computation.13 | loop fusion | bytes 2097152 | tf_op jit(solution)/shard_map/slice | solution.py:207
  2.4 0.1 pad.2.clone
  2.4 0.1 maximum_maximum_fusion
  2.5 6.0 %collective-permute-start.4 = (bf16[16,256]{1,0:T(8,128)(2,1)S(1)}, bf16[16,256]{1,0:T(8,128)(2,1)S(1)}, u32[]{:S(2)}, u32[]{:S(2)}) collective-permute-start(bf16[16,256]{1,0:T(8,128)(2,1)S(1)} %maximum_maximum_fusion), channel_id=1, source_target_pairs={{0,3},{1,2},{2,1},{3,0},{4,7},{5,6},{6,5},{7,4},{8,11},{9,10},{10,... | collective-permute-start | bytes 24584 | tf_op jit(solution)/shard_map/ppermute | solution.py:196
  8.6 1.0 %collective-permute-start.3 = (bf16[16,256]{1,0:T(8,128)(2,1)S(1)}, bf16[16,256]{1,0:T(8,128)(2,1)S(1)}, u32[]{:S(2)}, u32[]{:S(2)}) collective-permute-start(bf16[16,256]{1,0:T(8,128)(2,1)S(1)} %maximum_maximum_fusion), channel_id=1, source_target_pairs={{0,2},{1,3},{2,0},{3,1},{4,6},{5,7},{6,4},{7,5},{8,10},{9,11},{10,... | collective-permute-start | bytes 24584 | tf_op jit(solution)/shard_map/ppermute | solution.py:196
  9.5 1.2 %collective-permute-start.2 = (bf16[16,256]{1,0:T(8,128)(2,1)S(1)}, bf16[16,256]{1,0:T(8,128)(2,1)S(1)}, u32[]{:S(2)}, u32[]{:S(2)}) collective-permute-start(bf16[16,256]{1,0:T(8,128)(2,1)S(1)} %maximum_maximum_fusion), channel_id=1, source_target_pairs={{0,1},{1,0},{2,3},{3,2},{4,5},{5,4},{6,7},{7,6},{8,9},{9,8},{10,11... | collective-permute-start | bytes 24584 | tf_op jit(solution)/shard_map/ppermute | solution.py:196
  10.7 2.3 %collective-permute-done.2 = bf16[16,256]{1,0:T(8,128)(2,1)S(1)} collective-permute-done((bf16[16,256]{1,0:T(8,128)(2,1)S(1)}, bf16[16,256]{1,0:T(8,128)(2,1)S(1)}, u32[]{:S(2)}, u32[]{:S(2)}) %collective-permute-start.2) | collective-permute-done | bytes 8224 | tf_op jit(solution)/shard_map/ppermute | solution.py:196
  13.0 2.0 %collective-permute-done.3 = bf16[16,256]{1,0:T(8,128)(2,1)S(1)} collective-permute-done((bf16[16,256]{1,0:T(8,128)(2,1)S(1)}, bf16[16,256]{1,0:T(8,128)(2,1)S(1)}, u32[]{:S(2)}, u32[]{:S(2)}) %collective-permute-start.3) | collective-permute-done | bytes 8224 | tf_op jit(solution)/shard_map/ppermute | solution.py:196
  15.0 1.3 %collective-permute-start.5 = (bf16[64,256]{1,0:T(8,128)(2,1)S(1)}, bf16[64,256]{1,0:T(8,128)(2,1)S(1)}, u32[]{:S(2)}, u32[]{:S(2)}) collective-permute-start(bf16[64,256]{1,0:T(8,128)(2,1)S(1)} %get-tuple-element.37), channel_id=1, source_target_pairs={{0,4},{1,5},{2,6},{3,7},{4,0},{5,1},{6,2},{7,3},{8,12},{9,13},{10,... | collective-permute-start | bytes 98312 | tf_op jit(solution)/shard_map/ppermute | solution.py:196
  16.3 5.2 %collective-permute-start.1 = (bf16[4,256,256]{2,1,0:T(8,128)(2,1)}, bf16[4,256,256]{2,1,0:T(8,128)(2,1)S(1)}, u32[]{:S(2)}, u32[]{:S(2)}) collective-permute-start(bf16[4,256,256]{2,1,0:T(8,128)(2,1)} %get-tuple-element.36), channel_id=1, source_target_pairs={{1,2},{3,4},{5,6},{7,8},{9,10},{11,12},{13,14},{15,16},{17,18},{19... | collective-permute-start | bytes 1572872 | tf_op jit(solution)/shard_map/ppermute | solution.py:200
  21.4 0.1 collective-permute-start
  21.5 1.3 %collective-permute-start.7 = (bf16[64,256]{1,0:T(8,128)(2,1)S(1)}, bf16[64,256]{1,0:T(8,128)(2,1)S(1)}, u32[]{:S(2)}, u32[]{:S(2)}) collective-permute-start(bf16[64,256]{1,0:T(8,128)(2,1)S(1)} %get-tuple-element.37), channel_id=1, source_target_pairs={{0,12},{1,13},{2,14},{3,15},{4,8},{5,9},{6,10},{7,11},{8,4},{9,5},... | collective-permute-start | bytes 98312 | tf_op jit(solution)/shard_map/ppermute | solution.py:196
  22.8 0.6 collective-permute-start.6
  23.5 4.1 %collective-permute-done.6 = bf16[64,256]{1,0:T(8,128)(2,1)S(1)} collective-permute-done((bf16[64,256]{1,0:T(8,128)(2,1)S(1)}, bf16[64,256]{1,0:T(8,128)(2,1)S(1)}, u32[]{:S(2)}, u32[]{:S(2)}) %collective-permute-start.6) | collective-permute-done | bytes 32800 | tf_op jit(solution)/shard_map/ppermute | solution.py:196
  27.6 0.4 collective-permute-start.10
  28.0 2.3 %collective-permute-start.9 = (bf16[256,256]{1,0:T(8,128)(2,1)S(1)}, bf16[256,256]{1,0:T(8,128)(2,1)}, u32[]{:S(2)}, u32[]{:S(2)}) collective-permute-start(bf16[256,256]{1,0:T(8,128)(2,1)S(1)} %constant_dynamic-update-slice_fusion.4.rest_0_), channel_id=1, source_target_pairs={{0,32},{1,33},{2,34},{3,35},{4,36},{5,37},{6,38},{7,39},{8,40},{9,... | collective-permute-start | bytes 393224 | tf_op jit(solution)/shard_map/ppermute | solution.py:196
  30.3 4.3 %collective-permute-start.13 = (bf16[4,256,256]{2,1,0:T(8,128)(2,1)}, bf16[4,256,256]{2,1,0:T(8,128)(2,1)S(1)}, u32[]{:S(2)}, u32[]{:S(2)}) collective-permute-start(bf16[4,256,256]{2,1,0:T(8,128)(2,1)} %get-tuple-element.35), channel_id=1, source_target_pairs={{1,2},{3,4},{5,6},{7,8},{9,10},{11,12},{13,14},{15,16},{17,18},{19... | collective-permute-start | bytes 1572872 | tf_op jit(solution)/shard_map/ppermute | solution.py:209
  34.7 1.6 %collective-permute-start.12 = (bf16[4,256,256]{2,1,0:T(8,128)(2,1)}, bf16[4,256,256]{2,1,0:T(8,128)(2,1)S(1)}, u32[]{:S(2)}, u32[]{:S(2)}) collective-permute-start(bf16[4,256,256]{2,1,0:T(8,128)(2,1)} %get-tuple-element.35), channel_id=1, source_target_pairs={{0,1},{1,0},{2,3},{3,2},{4,5},{5,4},{6,7},{7,6},{8,9},{9,8},{10,11... | collective-permute-start | bytes 1572872 | tf_op jit(solution)/shard_map/ppermute | solution.py:208
  36.2 12.6 %collective-permute-start.8 = (bf16[256,256]{1,0:T(8,128)(2,1)S(1)}, bf16[256,256]{1,0:T(8,128)(2,1)S(1)}, u32[]{:S(2)}, u32[]{:S(2)}) collective-permute-start(bf16[256,256]{1,0:T(8,128)(2,1)S(1)} %constant_dynamic-update-slice_fusion.4.rest_0_), channel_id=1, source_target_pairs={{0,16},{1,17},{2,18},{3,19},{4,20},{5,21},{6,22},{7,23},{8,24},{9,... | collective-permute-start | bytes 393224 | tf_op jit(solution)/shard_map/ppermute | solution.py:196
  48.8 0.1 pad_add_fusion.where
  48.9 2.8 %copy-done = s32[8,256,3,256]{3,1,2,0:T(8,128)S(1)} copy-done((s32[8,256,3,256]{3,1,2,0:T(8,128)S(1)}, s32[8,256,3,256]{3,1,2,0:T(8,128)}, u32[]{:S(2)}) %copy-start) | copy-done | bytes 6291480
  51.7 0.0 copy-start.11
  51.7 0.0 copy-start.12
  51.7 2.7 %own_block.1 = (f32[8,256,256]{2,1,0:T(8,128)S(1)}, bf16[8,2,256,256]{3,2,1,0:T(8,128)(2,1)S(1)}, f32[8,256,128]{2,1,0:T(8,128)S(1)}) custom-call(s32[2]{0:T(128)S(1)} %pad_add_fusion.where, s32[8,3,256,256]{3,2,1,0:T(8,128)S(1)} %bitcast.5, bf16[8,256,256]{2,1,0:T(8,128)(2,1)S(1)} %copy-done.1, bf16[256,256]{1,0:T(8,128)(2,1)S(1)} %copy-done.4), custom_call_target="tpu_custom_call" | custom-call | flops 536870912 | bytes 12582912 | tf_op jit(solution)/shard_map/own_block/pallas_call | solution.py:228
  54.4 0.9 %collective-permute-done.8.rest_1_ = bf16[256,256]{1,0:T(8,128)(2,1)S(1)} collective-permute-done((bf16[256,256]{1,0:T(8,128)(2,1)S(1)}, bf16[256,256]{1,0:T(8,128)(2,1)S(1)}, u32[]{:S(2)}, u32[]{:S(2)}) %collective-permute-start.8) | collective-permute-done | bytes 131104 | tf_op jit(solution)/shard_map/ppermute | solution.py:196
  55.4 0.0 copy-start.5
  55.4 0.0 copy-start.6
  55.4 4.4 %late_months.1 = (f32[4,256,256]{2,1,0:T(8,128)S(1)}, f32[4,256,256]{2,1,0:T(8,128)S(1)}, bf16[3,256,256]{2,1,0:T(8,128)(2,1)S(1)}, bf16[4,256,256]{2,1,0:T(8,12...) custom-call(s32[2]{0:T(128)S(1)} %pad_add_fusion.where, ...), custom_call_target="tpu_custom_call" | custom-call | flops 2013265920 | bytes 12582912 | tf_op jit(solution)/shard_map/late_months/pallas_call | solution.py:243
  59.9 8.8 %collective-permute-start.11 = (bf16[3,256,256]{2,1,0:T(8,128)(2,1)S(1)}, bf16[3,256,256]{2,1,0:T(8,128)(2,1)S(1)}, u32[]{:S(2)}, u32[]{:S(2)}) collective-permute-start(bf16[3,256,256]{2,1,0:T(8,128)(2,1)S(1)} %get-tuple-element.24), channel_id=1, source_target_pairs={{0,64},{64,128},{128,192},{1,65},{65,129},{129,193},{2,66},{66,130... | collective-permute-start | bytes 1179656 | tf_op jit(solution)/shard_map/ppermute | solution.py:258
  68.7 2.0 %last_month.1.started = bf16[8,256,256]{2,1,0:T(8,128)(2,1)} custom-call(f32[4,256,256]{2,1,0:T(8,128)S(1)} %get-tuple-element.26.mixed.late_mixed, bf16[4,256,256]{2,1,0:T(8,128)(2,1)S(1)} %get-tuple-element.27.query.late_query, bf16[4,256,256]{2,1,0:T(8,128)(2,1)S(1)} %get-tuple-element.28.key.late_key, ...), custom_call_target="tpu_custom_call" | custom-call | flops 536870912 | bytes 3145728 | tf_op jit(solution)/shard_map/last_month/pallas_call | solution.py:264
  70.7 5.5 %early_months.1 = (bf16[8,256,256]{2,1,0:T(8,128)(2,1)}, f32[3,256,256]{2,1,0:T(8,128)S(1)}, bf16[3,256,256]{2,1,0:T(8,128)(2,1)S(1)}, bf16[3,256,256]{2,1,0:T(8,128)(2,1)S(1)}, bf16[3,256,256]{2,1,0:T(8,128)(2,1)S(1)}) custom-call(f32[4,256,256]{2,1,0:T(8,128)S(1)} %get-tuple-element.25.base, ...), custom_call_target="tpu_custom_call", output_to_operand_aliasing={{0}: (18, {})} | custom-call | flops 3019898880 | bytes 8388608 | tf_op jit(solution)/shard_map/early_months/pallas_call | solution.py:275
  76.2 3.6 %first_months.1 = bf16[8,256,256]{2,1,0:T(8,128)(2,1)} custom-call(bf16[3,256,256]{2,1,0:T(8,128)(2,1)S(1)} %collective-permute-done.11.earlier, f32[3,256,256]{2,1,0:T(8,128)S(1)} %get-tuple-element.30.mixed, bf16[3,256,256]{2,1,0:T(8,128)(2,1)S(1)} %get-tuple-element.31.query, ...), custom_call_target="tpu_custom_call", output_to_operand_aliasing={{}: (11, {})} | custom-call | flops 1811939328 | bytes 4194304 | tf_op jit(solution)/shard_map/first_months/pallas_call | solution.py:290
  (43 shorter events, 0.1 us)
Async XLA Ops:
  0.0 48.9 %copy-start.1 = (bf16[8,256,256]{2,1,0:T(8,128)(2,1)S(1)}, bf16[8,256,256]{2,1,0:T(8,128)(2,1)}, u32[]{:S(2)}) copy-start(bf16[8,256,256]{2,1,0:T(8,128)(2,1)} %own.1) | copy-start | bytes 3145732
  0.0 2.4 %copy-start.14 = (bf16[4,256]{1,0:T(4,128)(2,1)S(1)}, bf16[4,256]{1,0:T(4,128)(2,1)}, u32[]{:S(2)}) copy-start(bf16[4,256]{1,0:T(4,128)(2,1)} %param.20) | copy-start | bytes 6148
  0.0 2.4 %copy-start.13 = (bf16[8,256]{1,0:T(8,128)(2,1)S(1)}, bf16[8,256]{1,0:T(8,128)(2,1)}, u32[]{:S(2)}) copy-start(bf16[8,256]{1,0:T(8,128)(2,1)} %param.19) | copy-start | bytes 12292
  0.0 48.9 %copy-start.4 = (bf16[256,256]{1,0:T(8,128)(2,1)S(1)}, bf16[256,256]{1,0:T(8,128)(2,1)}, u32[]{:S(2)}) copy-start(bf16[256,256]{1,0:T(8,128)(2,1)} %w_supply.3) | copy-start | bytes 393220
  2.5 12.5 %collective-permute-start.4 = (bf16[16,256]{1,0:T(8,128)(2,1)S(1)}, bf16[16,256]{1,0:T(8,128)(2,1)S(1)}, u32[]{:S(2)}, u32[]{:S(2)}) collective-permute-start(bf16[16,256]{1,0:T(8,128)(2,1)S(1)} %maximum_maximum_fusion), channel_id=1, source_target_pairs={{0,3},{1,2},{2,1},{3,0},{4,7},{5,6},{6,5},{7,4},{8,11},{9,10},{10,... | collective-permute-start | bytes 24584 | tf_op jit(solution)/shard_map/ppermute | solution.py:196
  8.6 6.4 %collective-permute-start.3 = (bf16[16,256]{1,0:T(8,128)(2,1)S(1)}, bf16[16,256]{1,0:T(8,128)(2,1)S(1)}, u32[]{:S(2)}, u32[]{:S(2)}) collective-permute-start(bf16[16,256]{1,0:T(8,128)(2,1)S(1)} %maximum_maximum_fusion), channel_id=1, source_target_pairs={{0,2},{1,3},{2,0},{3,1},{4,6},{5,7},{6,4},{7,5},{8,10},{9,11},{10,... | collective-permute-start | bytes 24584 | tf_op jit(solution)/shard_map/ppermute | solution.py:196
  9.5 3.4 %collective-permute-start.2 = (bf16[16,256]{1,0:T(8,128)(2,1)S(1)}, bf16[16,256]{1,0:T(8,128)(2,1)S(1)}, u32[]{:S(2)}, u32[]{:S(2)}) collective-permute-start(bf16[16,256]{1,0:T(8,128)(2,1)S(1)} %maximum_maximum_fusion), channel_id=1, source_target_pairs={{0,1},{1,0},{2,3},{3,2},{4,5},{5,4},{6,7},{7,6},{8,9},{9,8},{10,11... | collective-permute-start | bytes 24584 | tf_op jit(solution)/shard_map/ppermute | solution.py:196
  15.0 8.5 %collective-permute-start.5 = (bf16[64,256]{1,0:T(8,128)(2,1)S(1)}, bf16[64,256]{1,0:T(8,128)(2,1)S(1)}, u32[]{:S(2)}, u32[]{:S(2)}) collective-permute-start(bf16[64,256]{1,0:T(8,128)(2,1)S(1)} %get-tuple-element.37), channel_id=1, source_target_pairs={{0,4},{1,5},{2,6},{3,7},{4,0},{5,1},{6,2},{7,3},{8,12},{9,13},{10,... | collective-permute-start | bytes 98312 | tf_op jit(solution)/shard_map/ppermute | solution.py:196
  16.3 39.1 %collective-permute-start.1 = (bf16[4,256,256]{2,1,0:T(8,128)(2,1)}, bf16[4,256,256]{2,1,0:T(8,128)(2,1)S(1)}, u32[]{:S(2)}, u32[]{:S(2)}) collective-permute-start(bf16[4,256,256]{2,1,0:T(8,128)(2,1)} %get-tuple-element.36), channel_id=1, source_target_pairs={{1,2},{3,4},{5,6},{7,8},{9,10},{11,12},{13,14},{15,16},{17,18},{19... | collective-permute-start | bytes 1572872 | tf_op jit(solution)/shard_map/ppermute | solution.py:200
  21.4 33.9 %collective-permute-start = (bf16[4,256,256]{2,1,0:T(8,128)(2,1)}, bf16[4,256,256]{2,1,0:T(8,128)(2,1)S(1)}, u32[]{:S(2)}, u32[]{:S(2)}) collective-permute-start(bf16[4,256,256]{2,1,0:T(8,128)(2,1)} %get-tuple-element.36), channel_id=1, source_target_pairs={{0,1},{1,0},{2,3},{3,2},{4,5},{5,4},{6,7},{7,6},{8,9},{9,8},{10,11... | collective-permute-start | bytes 1572872 | tf_op jit(solution)/shard_map/ppermute | solution.py:199
  21.5 6.0 %collective-permute-start.7 = (bf16[64,256]{1,0:T(8,128)(2,1)S(1)}, bf16[64,256]{1,0:T(8,128)(2,1)S(1)}, u32[]{:S(2)}, u32[]{:S(2)}) collective-permute-start(bf16[64,256]{1,0:T(8,128)(2,1)S(1)} %get-tuple-element.37), channel_id=1, source_target_pairs={{0,12},{1,13},{2,14},{3,15},{4,8},{5,9},{6,10},{7,11},{8,4},{9,5},... | collective-permute-start | bytes 98312 | tf_op jit(solution)/shard_map/ppermute | solution.py:196
  22.8 4.7 %collective-permute-start.6 = (bf16[64,256]{1,0:T(8,128)(2,1)S(1)}, bf16[64,256]{1,0:T(8,128)(2,1)S(1)}, u32[]{:S(2)}, u32[]{:S(2)}) collective-permute-start(bf16[64,256]{1,0:T(8,128)(2,1)S(1)} %get-tuple-element.37), channel_id=1, source_target_pairs={{0,8},{1,9},{2,10},{3,11},{4,12},{5,13},{6,14},{7,15},{8,0},{9,1},... | collective-permute-start | bytes 98312 | tf_op jit(solution)/shard_map/ppermute | solution.py:196
  27.6 7.1 %collective-permute-start.10 = (bf16[256,256]{1,0:T(8,128)(2,1)S(1)}, bf16[256,256]{1,0:T(8,128)(2,1)S(1)}, u32[]{:S(2)}, u32[]{:S(2)}) collective-permute-start(bf16[256,256]{1,0:T(8,128)(2,1)S(1)} %constant_dynamic-update-slice_fusion.4.rest_0_), channel_id=1, source_target_pairs={{0,48},{1,49},{2,50},{3,51},{4,52},{5,53},{6,54},{7,55},{8,56},{9,... | collective-permute-start | bytes 393224 | tf_op jit(solution)/shard_map/ppermute | solution.py:196
  28.0 8.2 %collective-permute-start.9 = (bf16[256,256]{1,0:T(8,128)(2,1)S(1)}, bf16[256,256]{1,0:T(8,128)(2,1)}, u32[]{:S(2)}, u32[]{:S(2)}) collective-permute-start(bf16[256,256]{1,0:T(8,128)(2,1)S(1)} %constant_dynamic-update-slice_fusion.4.rest_0_), channel_id=1, source_target_pairs={{0,32},{1,33},{2,34},{3,35},{4,36},{5,37},{6,38},{7,39},{8,40},{9,... | collective-permute-start | bytes 393224 | tf_op jit(solution)/shard_map/ppermute | solution.py:196
  30.3 40.4 %collective-permute-start.13 = (bf16[4,256,256]{2,1,0:T(8,128)(2,1)}, bf16[4,256,256]{2,1,0:T(8,128)(2,1)S(1)}, u32[]{:S(2)}, u32[]{:S(2)}) collective-permute-start(bf16[4,256,256]{2,1,0:T(8,128)(2,1)} %get-tuple-element.35), channel_id=1, source_target_pairs={{1,2},{3,4},{5,6},{7,8},{9,10},{11,12},{13,14},{15,16},{17,18},{19... | collective-permute-start | bytes 1572872 | tf_op jit(solution)/shard_map/ppermute | solution.py:209
  34.7 36.1 %collective-permute-start.12 = (bf16[4,256,256]{2,1,0:T(8,128)(2,1)}, bf16[4,256,256]{2,1,0:T(8,128)(2,1)S(1)}, u32[]{:S(2)}, u32[]{:S(2)}) collective-permute-start(bf16[4,256,256]{2,1,0:T(8,128)(2,1)} %get-tuple-element.35), channel_id=1, source_target_pairs={{0,1},{1,0},{2,3},{3,2},{4,5},{5,4},{6,7},{7,6},{8,9},{9,8},{10,11... | collective-permute-start | bytes 1572872 | tf_op jit(solution)/shard_map/ppermute | solution.py:208
  36.2 19.1 %collective-permute-start.8 = (bf16[256,256]{1,0:T(8,128)(2,1)S(1)}, bf16[256,256]{1,0:T(8,128)(2,1)S(1)}, u32[]{:S(2)}, u32[]{:S(2)}) collective-permute-start(bf16[256,256]{1,0:T(8,128)(2,1)S(1)} %constant_dynamic-update-slice_fusion.4.rest_0_), channel_id=1, source_target_pairs={{0,16},{1,17},{2,18},{3,19},{4,20},{5,21},{6,22},{7,23},{8,24},{9,... | collective-permute-start | bytes 393224 | tf_op jit(solution)/shard_map/ppermute | solution.py:196
  48.9 2.8 %copy-start = (s32[8,256,3,256]{3,1,2,0:T(8,128)S(1)}, s32[8,256,3,256]{3,1,2,0:T(8,128)}, u32[]{:S(2)}) copy-start(s32[8,256,3,256]{3,1,2,0:T(8,128)} %param.16) | copy-start | bytes 18874372
  51.7 3.7 %copy-start.7 = (bf16[256,256]{1,0:T(8,128)(2,1)S(1)}, bf16[256,256]{1,0:T(8,128)(2,1)}, u32[]{:S(2)}) copy-start(bf16[256,256]{1,0:T(8,128)(2,1)} %w_query.1) | copy-start | bytes 393220
  51.7 3.7 %copy-start.8 = (bf16[256,256]{1,0:T(8,128)(2,1)S(1)}, bf16[256,256]{1,0:T(8,128)(2,1)}, u32[]{:S(2)}) copy-start(bf16[256,256]{1,0:T(8,128)(2,1)} %w_key.3) | copy-start | bytes 393220
  51.7 3.7 %copy-start.9 = (bf16[256,256]{1,0:T(8,128)(2,1)S(1)}, bf16[256,256]{1,0:T(8,128)(2,1)}, u32[]{:S(2)}) copy-start(bf16[256,256]{1,0:T(8,128)(2,1)} %w_value.3) | copy-start | bytes 393220
  51.7 3.7 %copy-start.10 = (s32[8,256]{1,0:T(8,128)S(1)}, s32[8,256]{1,0:T(8,128)}, u32[]{:S(2)}) copy-start(s32[8,256]{1,0:T(8,128)} %banks.1) | copy-start | bytes 24580
  51.7 3.7 %copy-start.11 = (s32[8,256]{1,0:T(8,128)S(1)}, s32[8,256]{1,0:T(8,128)}, u32[]{:S(2)}) copy-start(s32[8,256]{1,0:T(8,128)} %sectors.1) | copy-start | bytes 24580
  51.7 3.7 %copy-start.12 = (f32[256]{0:T(256)S(1)}, f32[256]{0:T(256)}, u32[]{:S(2)}) copy-start(f32[256]{0:T(256)} %param.28) | copy-start | bytes 3076
  55.4 13.2 %copy-start.2 = (bf16[256,1024]{1,0:T(8,128)(2,1)S(1)}, bf16[256,1024]{1,0:T(8,128)(2,1)}, u32[]{:S(2)}) copy-start(bf16[256,1024]{1,0:T(8,128)(2,1)} %w_in.5) | copy-start | bytes 1572868
  55.4 13.2 %copy-start.3 = (bf16[1024,256]{1,0:T(8,128)(2,1)S(1)}, bf16[1024,256]{1,0:T(8,128)(2,1)}, u32[]{:S(2)}) copy-start(bf16[1024,256]{1,0:T(8,128)(2,1)} %w_down.5) | copy-start | bytes 1572868
  55.4 13.2 %copy-start.5 = (bf16[256,256]{1,0:T(8,128)(2,1)S(1)}, bf16[256,256]{1,0:T(8,128)(2,1)}, u32[]{:S(2)}) copy-start(bf16[256,256]{1,0:T(8,128)(2,1)} %w_out.5) | copy-start | bytes 393220
  55.4 13.2 %copy-start.6 = (f32[256]{0:T(256)S(1)}, f32[256]{0:T(256)}, u32[]{:S(2)}) copy-start(f32[256]{0:T(256)} %param.29) | copy-start | bytes 3076
  59.9 16.4 %collective-permute-start.11 = (bf16[3,256,256]{2,1,0:T(8,128)(2,1)S(1)}, bf16[3,256,256]{2,1,0:T(8,128)(2,1)S(1)}, u32[]{:S(2)}, u32[]{:S(2)}) collective-permute-start(bf16[3,256,256]{2,1,0:T(8,128)(2,1)S(1)} %get-tuple-element.24), channel_id=1, source_target_pairs={{0,64},{64,128},{128,192},{1,65},{65,129},{129,193},{2,66},{66,130... | collective-permute-start | bytes 1179656 | tf_op jit(solution)/shard_map/ppermute | solution.py:258

commit v3 on v2

--- a/solution.py
+++ b/solution.py
@@ -105,7 +105,7 @@
         if m < HALF:
             early_base[m] = total
         else:
-            mixed = mix(m, total, tiles, scale, even_rows[m - HALF], odd_rows[m - HALF], w_supply[...])
+            mixed = mix(m, total, tiles, scale, even_rows[(m - HALF) * firms : (m - HALF + 1) * firms], odd_rows[m - HALF], w_supply[...])
             mixed_out[m - HALF] = mixed
             normed.append(rms_norm(mixed, gain_mix[...]).astype(BF))
             if m >= 2 * HALF - LAGS:
@@ -195,29 +195,24 @@
     def swap(x, bits):
         return lax.ppermute(x, "firm", [(i, i ^ bits) for i in range(devices)])
 
-    late = features[HALF:]
-    late_even = lax.ppermute(late, "firm", even_pairs)
-    late_odd = lax.ppermute(late, "firm", odd_pairs)
-
     spare = SLOT - bank_table.shape[0] - sector_table.shape[0]
     hub = jnp.concatenate([bank_table, sector_table, jnp.zeros((spare, width), BF)], axis=0)
-    hub, late = lax.optimization_barrier((hub, late))
-    hub = jnp.concatenate([hub] + [swap(hub, i) for i in (1, 2, 3)], axis=0)
-
-    early = features[:HALF]
-    early_even = lax.ppermute(early, "firm", even_pairs)
-    early_odd = lax.ppermute(early, "firm", odd_pairs)
-
-    hub = jnp.concatenate([hub] + [swap(hub, i) for i in (4, 8, 12)], axis=0)
-    tables = [hub] + [swap(hub, i) for i in (16, 32, 48)]
+    across = swap(hub, 2)
+    late = features[HALF:]
+    plain = late.reshape(HALF * firms, width)
+    loaded = jnp.concatenate([plain, hub, jnp.zeros((SLOT, width), BF)], axis=0)
+    loaded, late, across = lax.optimization_barrier((loaded, late, across))
+    loaded = lax.dynamic_update_slice(loaded, across, (HALF * firms + SLOT, 0))
+    late_even = lax.ppermute(loaded, "firm", even_pairs)
+    late_odd = lax.ppermute(late, "firm", odd_pairs)
 
     counts = jnp.transpose(supply_counts, (0, 2, 1, 3))
     gain_mix = gain_mix.reshape(1, width)
     gain_ffn = gain_ffn.reshape(1, width)
 
-    def cost(units, mebibytes):
+    def cost(units, kibibytes):
         return pl.CostEstimate(
-            flops=2 * units * firms * width * width, bytes_accessed=mebibytes << 20, transcendentals=0
+            flops=2 * units * firms * width * width, bytes_accessed=kibibytes << 10, transcendentals=0
         )
 
     def like(count, dtype, lanes=width):
@@ -236,9 +231,26 @@
             like(months, F32), jax.ShapeDtypeStruct((months, 2, firms, firms), BF), like(months, F32, 128),
         ],
         compiler_params=params,
-        cost_estimate=cost(16, 12),
+        cost_estimate=cost(16, 1 << 16),
         name="own_block",
     )(where, counts, features, w_supply)
+
+    base, early = lax.optimization_barrier((base, features[:HALF]))
+    early_even = lax.ppermute(early, "firm", even_pairs)
+    early_odd = lax.ppermute(early, "firm", odd_pairs)
+
+    def spread(near):
+        hub = jnp.concatenate(near, axis=0)
+        hub = jnp.concatenate([hub] + [swap(hub, i) for i in (4, 8, 12)], axis=0)
+        return [hub] + [swap(hub, i) for i in (16, 32, 48)]
+
+    late_even, late_odd = lax.optimization_barrier((late_even, late_odd))
+    arrived = late_even[HALF * firms :]
+    near = [hub, arrived[:SLOT], across, arrived[SLOT:]]
+    plane = jax.ShapeDtypeStruct((SLOT * 16, width), BF)
+    tables = lax.cond(
+        me >= 0, spread, lambda near: [jnp.zeros(plane.shape, BF)] * 4, near
+    )
 
     early_base, late_mixed, late_normed, late_query, late_key, late_value = pl.pallas_call(
         late_kernel,
@@ -248,7 +260,7 @@
             like(HALF, F32), like(HALF, F32), like(LAGS, BF), like(HALF, BF), like(HALF, BF), like(HALF, BF),
         ],
         compiler_params=params,
-        cost_estimate=cost(60, 12),
+        cost_estimate=cost(1, 1),
         name="late_months",
     )(
         where, base, tiles, scale, late_even, late_odd, bank_ids, sector_ids, *tables,
@@ -268,7 +280,7 @@
         out_shape=like(months, BF),
         scratch_shapes=scratch(1),
         compiler_params=params,
-        cost_estimate=cost(16, 3),
+        cost_estimate=cost(1, 1),
         name="last_month",
     )(late_mixed, late_query, late_key, late_value, *end_weights)
 
@@ -280,7 +292,7 @@
         scratch_shapes=scratch(HALF),
         input_output_aliases={18: 0},
         compiler_params=params,
-        cost_estimate=cost(90, 8),
+        cost_estimate=cost(1, 1),
         name="early_months",
     )(
         early_base, tiles, scale, early_even, early_odd, late_mixed, late_query, late_key, late_value,
@@ -295,7 +307,7 @@
         scratch_shapes=scratch(LAGS),
         input_output_aliases={11: 0},
         compiler_params=params,
-        cost_estimate=cost(54, 4),
+        cost_estimate=cost(1, 1),
         name="first_months",
     )(earlier, mixed, query, key, value, w_key, w_value, *end_weights, result)
 

time: 80.3 us -> 108 us (1.34); the launches traced: 80 us -> 107 us
  waiting for transfers between devices: 9.28 us -> 33.5 us
  starting transfers between devices: 46.7 us -> 27.3 us
  local copies, waits for them, and re-layouts: 5.28 us -> 24.1 us
  Pallas kernels: 18.3 us -> 19.8 us
  other arithmetic: 0.15 us -> 1.56 us
    ppermute x1, waiting for transfers between devices: 0.01 us -> 23.8 us  [body(): late_odd = lax.ppermute(late, 'firm', odd_pairs)]
    ppermute x9 -> x7, starting transfers between devices: 26.7 us -> 13.5 us  [swap(): return lax.ppermute(x, 'firm', [(i, i ^ bits) for i in range(devices)])]
    ppermute x1, starting transfers between devices: 8.75 us -> 2.1 us  [body(): lax.ppermute(late_normed, 'tm', [(i, i + 1) for i in range(lax.axis_size(...]
    unnamed x35 -> x42, local copies, waits for them, and re-layouts: 2.87 us -> 9.2 us
    concatenate x3 -> x2, local copies, waits for them, and re-layouts: 0.08 us -> 5.58 us  [the longest x1 4.96 us: body(): loaded = jnp.concatenate([plain, hub, jnp.zeros((SLOT, width), BF)], axis=0)]
    cond x0 -> x5, local copies, waits for them, and re-layouts: none -> 5.12 us
    ppermute x1, starting transfers between devices: 4.35 us -> 7 us  [body(): early_odd = lax.ppermute(early, 'firm', odd_pairs)]
    ppermute x1, starting transfers between devices: 5.16 us -> 3.38 us  [body(): late_odd = lax.ppermute(late, 'firm', odd_pairs)]
  transfers between devices with their start and end apart: 14 -> 12, of which waited for: 4 -> 4; matrix products, arithmetic and copies ran while one was open for 0% -> 14% of each run, Pallas kernels for 18% -> 15%
where the time goes in v3:
time: 108 us; the launch traced here: 107 us
  waiting for transfers between devices  33.5 us (31%)
  starting transfers between devices  27.3 us (25%)
  local copies, waits for them, and re-layouts  24.1 us (22%)
  Pallas kernels  19.8 us (18%)
  other arithmetic  1.56 us (1%)
    ppermute x1, waiting for transfers between devices, body(): late_odd = lax.ppermute(late, 'firm', odd_pairs)  23.8 us
    ppermute x7, starting transfers between devices, swap(): return lax.ppermute(x, 'firm', [(i, i ^ bits) for i in range(devices)])  13.5 us
    ppermute x7, waiting for transfers between devices, swap(): return lax.ppermute(x, 'firm', [(i, i ^ bits) for i in range(devices)])  9.73 us
    unnamed x42, local copies, waits for them, and re-layouts  9.2 us
    ppermute x1, starting transfers between devices, body(): early_odd = lax.ppermute(early, 'firm', odd_pairs)  7 us
    pallas_call x1, Pallas kernels, body(): pl.pallas_call(early_kernel, in_specs=[VM] * 18 + [ANY], out_specs=[ANY]...  6.61 us
    cond x5, local copies, waits for them, and re-layouts  5.12 us
    concatenate x1, local copies, waits for them, and re-layouts, body(): loaded = jnp.concatenate([plain, hub, jnp.zeros((SLOT, width), BF)], axis=0)  4.96 us
  transfers between devices with their start and end apart: 12, of which 4 were waited for; matrix products, arithmetic and copies ran while one was open for 14% of the time, Pallas kernels for 15%

profile of v3, /device:TPU:25, one launch (start us, length us, event | category | flops | bytes accessed | tf_op | source)
XLA Modules:
  0.0 106.6 jit_solution(8651338369360124457)
XLA Ops:
  0.0 0.8 pad_maximum_fusion.1
  0.8 7.0 %collective-permute-start.6 = (bf16[16,256]{1,0:T(8,128)(2,1)S(1)}, bf16[16,256]{1,0:T(8,128)(2,1)S(1)}, u32[]{:S(2)}, u32[]{:S(2)}) collective-permute-start(bf16[16,256]{1,0:T(8,128)(2,1)S(1)} %pad_maximum_fusion.1), channel_id=1, source_target_pairs={{0,2},{1,3},{2,0},{3,1},{4,6},{5,7},{6,4},{7,5},{8,10},{9,11},{10,... | collective-permute-start | bytes 24584 | tf_op jit(solution)/shard_map/ppermute | solution.py:196
  7.8 2.3 %fusion.1 = (bf16[4,256,256]{2,1,0:T(8,128)(2,1)}, bf16[4,256,256]{2,1,0:T(8,128)(2,1)}) fusion(bf16[8,256,256]{2,1,0:T(8,128)(2,1)} %own.1), kind=kLoop, calls=%fused_computation.12 | loop fusion | bytes 2097152 | tf_op jit(solution)/shard_map/slice | solution.py:201
  10.1 5.0 %concatenate.14 = bf16[1056,256]{1,0:T(8,128)(2,1)} concatenate(bf16[1024,256]{1,0:T(8,128)(2,1)} %bitcast.3, bf16[8,256]{1,0:T(8,128)(2,1)S(1)} %copy-done.19, bf16[4,256]{1,0:T(4,128)(2,1)S(1)} %copy-done.20, bf16[4,256]{1,0:T(4,128)(2,1)S(1)} %broadcast_in_dim.6, bf16[16,256]{1,0:T(8,128)(2,1)S(1)} %broadcast_in_dim.7), dimensions={0} | concatenate | bytes 1081344 | tf_op jit(solution)/shard_map/concatenate | solution.py:203
  15.7 1.2 %collective-permute-start.7 = (bf16[1056,256]{1,0:T(8,128)(2,1)}, bf16[1056,256]{1,0:T(8,128)(2,1)}, u32[]{:S(2)}, u32[]{:S(2)}) collective-permute-start(bf16[1056,256]{1,0:T(8,128)(2,1)} %constant_dynamic-update-slice_fusion.7), channel_id=1, source_target_pairs={{0,1},{1,0},{2,3},{3,2},{4,5},{5,4},{6,7},{7,6},{8,9},{9,8},{10,11... | collective-permute-start | bytes 1622024 | tf_op jit(solution)/shard_map/ppermute | solution.py:206
  16.9 3.4 %collective-permute-start.8 = (bf16[4,256,256]{2,1,0:T(8,128)(2,1)}, bf16[4,256,256]{2,1,0:T(8,128)(2,1)}, u32[]{:S(2)}, u32[]{:S(2)}) collective-permute-start(bf16[4,256,256]{2,1,0:T(8,128)(2,1)} %get-tuple-element.48), channel_id=1, source_target_pairs={{1,2},{3,4},{5,6},{7,8},{9,10},{11,12},{13,14},{15,16},{17,18},{19... | collective-permute-start | bytes 1572872 | tf_op jit(solution)/shard_map/ppermute | solution.py:207
  20.4 2.8 %copy-done = s32[8,256,3,256]{3,1,2,0:T(8,128)S(1)} copy-done((s32[8,256,3,256]{3,1,2,0:T(8,128)S(1)}, s32[8,256,3,256]{3,1,2,0:T(8,128)}, u32[]{:S(2)}) %copy-start) | copy-done | bytes 6291480
  23.1 1.2 %copy-done.3 = bf16[8,256,256]{2,1,0:T(8,128)(2,1)S(1)} copy-done((bf16[8,256,256]{2,1,0:T(8,128)(2,1)S(1)}, bf16[8,256,256]{2,1,0:T(8,128)(2,1)}, u32[]{:S(2)}) %copy-start.3) | copy-done | bytes 1048600
  24.4 2.7 %own_block.1 = (f32[8,256,256]{2,1,0:T(8,128)S(1)}, bf16[8,2,256,256]{3,2,1,0:T(8,128)(2,1)S(1)}, f32[8,256,128]{2,1,0:T(8,128)S(1)}) custom-call(s32[2]{0:T(128)S(1)} %pad_add_fusion.where, s32[8,3,256,256]{3,2,1,0:T(8,128)S(1)} %bitcast.6, bf16[8,256,256]{2,1,0:T(8,128)(2,1)S(1)} %copy-done.3, bf16[256,256]{1,0:T(8,128)(2,1)S(1)} %copy-done.6), custom_call_target="tpu_custom_call" | custom-call | flops 536870912 | bytes 67108864 | tf_op jit(solution)/shard_map/own_block/pallas_call | solution.py:223
  27.1 1.4 %copy-done.4 = f32[8,256,256]{2,1,0:T(8,128)} copy-done((f32[8,256,256]{2,1,0:T(8,128)}, f32[8,256,256]{2,1,0:T(8,128)S(1)}, u32[]{:S(2)}) %copy-start.4) | copy-done | bytes 2097176
  28.4 7.0 %collective-permute-start.11 = (bf16[4,256,256]{2,1,0:T(8,128)(2,1)}, bf16[4,256,256]{2,1,0:T(8,128)(2,1)}, u32[]{:S(2)}, u32[]{:S(2)}) collective-permute-start(bf16[4,256,256]{2,1,0:T(8,128)(2,1)} %get-tuple-element.57), channel_id=1, source_target_pairs={{1,2},{3,4},{5,6},{7,8},{9,10},{11,12},{13,14},{15,16},{17,18},{19... | collective-permute-start | bytes 1572872 | tf_op jit(solution)/shard_map/ppermute | solution.py:240
  35.5 23.8 %collective-permute-done.8.odd_rows = bf16[4,256,256]{2,1,0:T(8,128)(2,1)} collective-permute-done((bf16[4,256,256]{2,1,0:T(8,128)(2,1)}, bf16[4,256,256]{2,1,0:T(8,128)(2,1)}, u32[]{:S(2)}, u32[]{:S(2)}) %collective-permute-start.8) | collective-permute-done | bytes 524320 | tf_op jit(solution)/shard_map/ppermute | solution.py:207
  59.3 24.0 %conditional.1 = (bf16[256,256]{1,0:T(8,128)(2,1)}, bf16[256,256]{1,0:T(8,128)(2,1)}, bf16[256,256]{1,0:T(8,128)(2,1)}, bf16[256,256]{1,0:T(8,128)(2,1)}) conditional(s32[]{:T(128)} %convert_element_type.3, () %tuple.19, (bf16[1056,256]{1,0:T(8,128)(2,1)}, bf16[16,256]{1,0:T(8,128)(2,1)}, bf16[16,256]{1,0:T(8,128)(2,1)}) %tuple.27), branch_computations={%region_0.0_spmd, %region_1.0_spmd} | conditional | flops 131072 | bytes 2318608 | solution.py:251
  59.3 1.3 %constant_dynamic-update-slice_fusion.6 = bf16[256,256]{1,0:T(8,128)(2,1)} fusion(bf16[16,256]{1,0:T(8,128)(2,1)} %get-tuple-element.14), kind=kLoop, calls=%fused_computation.7 | loop fusion | bytes 16384 | tf_op jit(solution)/shard_map/cond
  60.6 1.3 %fusion = (bf16[16,256]{1,0:T(8,128)(2,1)S(1)}, bf16[256,256]{1,0:T(8,128)(2,1)}, bf16[16,256]{1,0:T(8,128)(2,1)S(1)}) fusion(bf16[1056,256]{1,0:T(8,128)(2,1)} %get-tuple-element.15, bf16[256,256]{1,0:T(8,128)(2,1)} %constant_dynamic-update-slice_fusion.6), kind=kLoop, calls=%fused_computation.11 | loop fusion | bytes 40960 | tf_op jit(solution)/shard_map/slice | solution.py:249
  61.9 0.7 pad_maximum_fusion
  63.2 2.7 %collective-permute-start = (bf16[64,256]{1,0:T(8,128)(2,1)S(1)}, bf16[64,256]{1,0:T(8,128)(2,1)S(1)}, u32[]{:S(2)}, u32[]{:S(2)}) collective-permute-start(bf16[64,256]{1,0:T(8,128)(2,1)S(1)} %pad_maximum_fusion), channel_id=1, source_target_pairs={{0,4},{1,5},{2,6},{3,7},{4,0},{5,1},{6,2},{7,3},{8,12},{9,13},{10,... | collective-permute-start | bytes 98312 | tf_op jit(solution)/shard_map/cond/branch_1_fun/ppermute | solution.py:196
  65.9 1.3 %constant_dynamic-update-slice_fusion.4 = bf16[256,256]{1,0:T(8,128)(2,1)} fusion(bf16[256,256]{1,0:T(8,128)(2,1)} %get-tuple-element.68, bf16[16,256]{1,0:T(8,128)(2,1)} %get-tuple-element.16), kind=kLoop, calls=%fused_computation.5 | loop fusion | bytes 16384 | tf_op jit(solution)/shard_map/cond
  67.2 1.3 %constant_dynamic-update-slice_fusion.3 = bf16[256,256]{1,0:T(8,128)(2,1)} fusion(bf16[256,256]{1,0:T(8,128)(2,1)} %constant_dynamic-update-slice_fusion.4, bf16[1056,256]{1,0:T(8,128)(2,1)} %get-tuple-element.15), kind=kLoop, calls=%fused_computation.4 | loop fusion | bytes 16384 | tf_op jit(solution)/shard_map/cond
  68.5 1.3 %collective-permute-done = bf16[64,256]{1,0:T(8,128)(2,1)S(1)} collective-permute-done((bf16[64,256]{1,0:T(8,128)(2,1)S(1)}, bf16[64,256]{1,0:T(8,128)(2,1)S(1)}, u32[]{:S(2)}, u32[]{:S(2)}) %collective-permute-start) | collective-permute-done | bytes 32800 | tf_op jit(solution)/shard_map/cond/branch_1_fun/ppermute | solution.py:196
  70.4 2.3 %collective-permute-done.1 = bf16[64,256]{1,0:T(8,128)(2,1)S(1)} collective-permute-done((bf16[64,256]{1,0:T(8,128)(2,1)S(1)}, bf16[64,256]{1,0:T(8,128)(2,1)S(1)}, u32[]{:S(2)}, u32[]{:S(2)}) %collective-permute-start.1) | collective-permute-done | bytes 32800 | tf_op jit(solution)/shard_map/cond/branch_1_fun/ppermute | solution.py:196
  73.9 2.2 %collective-permute-start.4 = (bf16[256,256]{1,0:T(8,128)(2,1)}, bf16[256,256]{1,0:T(8,128)(2,1)}, u32[]{:S(2)}, u32[]{:S(2)}) collective-permute-start(bf16[256,256]{1,0:T(8,128)(2,1)} %constant_dynamic-update-slice_fusion), channel_id=1, source_target_pairs={{0,32},{1,33},{2,34},{3,35},{4,36},{5,37},{6,38},{7,39},{8,40},{9,... | collective-permute-start | bytes 393224 | tf_op jit(solution)/shard_map/cond/branch_1_fun/ppermute | solution.py:196
  76.2 1.0 collective-permute-start.3
  77.2 6.2 %collective-permute-done.5 = bf16[256,256]{1,0:T(8,128)(2,1)} collective-permute-done((bf16[256,256]{1,0:T(8,128)(2,1)}, bf16[256,256]{1,0:T(8,128)(2,1)}, u32[]{:S(2)}, u32[]{:S(2)}) %collective-permute-start.5) | collective-permute-done | bytes 131104 | tf_op jit(solution)/shard_map/cond/branch_1_fun/ppermute | solution.py:196
  83.4 1.6 %copy-done.5 = f32[8,256,256]{2,1,0:T(8,128)S(1)} copy-done((f32[8,256,256]{2,1,0:T(8,128)S(1)}, f32[8,256,256]{2,1,0:T(8,128)}, u32[]{:S(2)}) %copy-start.5) | copy-done | bytes 2097176
  85.0 0.9 copy-done.10
  85.9 0.7 copy-done.14
  87.2 4.8 %late_months.1 = (f32[4,256,256]{2,1,0:T(8,128)S(1)}, f32[4,256,256]{2,1,0:T(8,128)S(1)}, bf16[3,256,256]{2,1,0:T(8,128)(2,1)S(1)}, bf16[4,256,256]{2,1,0:T(8,12...) custom-call(s32[2]{0:T(128)S(1)} %copy-done.16, f32[8,256,256]{2,1,0:T(8,128)S(1)} %copy-done.5, ...), custom_call_target="tpu_custom_call" | custom-call | flops 33554432 | bytes 1024 | tf_op jit(solution)/shard_map/late_months/pallas_call | solution.py:255
  92.0 2.1 %collective-permute-start.9 = (bf16[3,256,256]{2,1,0:T(8,128)(2,1)S(1)}, bf16[3,256,256]{2,1,0:T(8,128)(2,1)S(1)}, u32[]{:S(2)}, u32[]{:S(2)}) collective-permute-start(bf16[3,256,256]{2,1,0:T(8,128)(2,1)S(1)} %get-tuple-element.55), channel_id=1, source_target_pairs={{0,64},{64,128},{128,192},{1,65},{65,129},{129,193},{2,66},{66,130... | collective-permute-start | bytes 1179656 | tf_op jit(solution)/shard_map/ppermute | solution.py:270
  94.2 2.0 %last_month.1.started = bf16[8,256,256]{2,1,0:T(8,128)(2,1)} custom-call(f32[4,256,256]{2,1,0:T(8,128)S(1)} %get-tuple-element.58.mixed.late_mixed, bf16[4,256,256]{2,1,0:T(8,128)(2,1)S(1)} %get-tuple-element.59.query.late_query, bf16[4,256,256]{2,1,0:T(8,128)(2,1)S(1)} %get-tuple-element.60.key.late_key, ...), custom_call_target="tpu_custom_call" | custom-call | flops 33554432 | bytes 1024 | tf_op jit(solution)/shard_map/last_month/pallas_call | solution.py:276
  96.2 6.6 %early_months.1 = (bf16[8,256,256]{2,1,0:T(8,128)(2,1)}, f32[3,256,256]{2,1,0:T(8,128)S(1)}, bf16[3,256,256]{2,1,0:T(8,128)(2,1)S(1)}, bf16[3,256,256]{2,1,0:T(8,128)(2,1)S(1)}, bf16[3,256,256]{2,1,0:T(8,128)(2,1)S(1)}) custom-call(f32[4,256,256]{2,1,0:T(8,128)S(1)} %get-tuple-element.56.base, ...), custom_call_target="tpu_custom_call", output_to_operand_aliasing={{0}: (18, {})} | custom-call | flops 33554432 | bytes 1024 | tf_op jit(solution)/shard_map/early_months/pallas_call | solution.py:287
  102.9 3.6 %first_months.1 = bf16[8,256,256]{2,1,0:T(8,128)(2,1)} custom-call(bf16[3,256,256]{2,1,0:T(8,128)(2,1)S(1)} %collective-permute-done.9.earlier, f32[3,256,256]{2,1,0:T(8,128)S(1)} %get-tuple-element.62.mixed, bf16[3,256,256]{2,1,0:T(8,128)(2,1)S(1)} %get-tuple-element.63.query, ...), custom_call_target="tpu_custom_call", output_to_operand_aliasing={{}: (11, {})} | custom-call | flops 33554432 | bytes 1024 | tf_op jit(solution)/shard_map/first_months/pallas_call | solution.py:302
  (55 shorter events, 3.9 us)
Async XLA Ops:
  0.0 10.1 %copy-start.20 = (bf16[4,256]{1,0:T(4,128)(2,1)S(1)}, bf16[4,256]{1,0:T(4,128)(2,1)}, u32[]{:S(2)}) copy-start(bf16[4,256]{1,0:T(4,128)(2,1)} %param.22) | copy-start | bytes 6148
  0.0 10.1 %copy-start.19 = (bf16[8,256]{1,0:T(8,128)(2,1)S(1)}, bf16[8,256]{1,0:T(8,128)(2,1)}, u32[]{:S(2)}) copy-start(bf16[8,256]{1,0:T(8,128)(2,1)} %param.21) | copy-start | bytes 12292
  0.0 20.3 %copy-start.6 = (bf16[256,256]{1,0:T(8,128)(2,1)S(1)}, bf16[256,256]{1,0:T(8,128)(2,1)}, u32[]{:S(2)}) copy-start(bf16[256,256]{1,0:T(8,128)(2,1)} %w_supply.3) | copy-start | bytes 393220
  0.8 19.5 %copy-start.17 = (bf16[16,256]{1,0:T(8,128)(2,1)}, bf16[16,256]{1,0:T(8,128)(2,1)S(1)}, u32[]{:S(2)}) copy-start(bf16[16,256]{1,0:T(8,128)(2,1)S(1)} %pad_maximum_fusion.1) | copy-start | bytes 24580
  0.8 14.3 %collective-permute-start.6 = (bf16[16,256]{1,0:T(8,128)(2,1)S(1)}, bf16[16,256]{1,0:T(8,128)(2,1)S(1)}, u32[]{:S(2)}, u32[]{:S(2)}) collective-permute-start(bf16[16,256]{1,0:T(8,128)(2,1)S(1)} %pad_maximum_fusion.1), channel_id=1, source_target_pairs={{0,2},{1,3},{2,0},{3,1},{4,6},{5,7},{6,4},{7,5},{8,10},{9,11},{10,... | collective-permute-start | bytes 24584 | tf_op jit(solution)/shard_map/ppermute | solution.py:196
  15.1 5.3 %copy-start.18 = (bf16[16,256]{1,0:T(8,128)(2,1)}, bf16[16,256]{1,0:T(8,128)(2,1)S(1)}, u32[]{:S(2)}) copy-start(bf16[16,256]{1,0:T(8,128)(2,1)S(1)} %collective-permute-done.6) | copy-start | bytes 24580
  15.7 43.7 %collective-permute-start.7 = (bf16[1056,256]{1,0:T(8,128)(2,1)}, bf16[1056,256]{1,0:T(8,128)(2,1)}, u32[]{:S(2)}, u32[]{:S(2)}) collective-permute-start(bf16[1056,256]{1,0:T(8,128)(2,1)} %constant_dynamic-update-slice_fusion.7), channel_id=1, source_target_pairs={{0,1},{1,0},{2,3},{3,2},{4,5},{5,4},{6,7},{7,6},{8,9},{9,8},{10,11... | collective-permute-start | bytes 1622024 | tf_op jit(solution)/shard_map/ppermute | solution.py:206
  16.9 42.5 %collective-permute-start.8 = (bf16[4,256,256]{2,1,0:T(8,128)(2,1)}, bf16[4,256,256]{2,1,0:T(8,128)(2,1)}, u32[]{:S(2)}, u32[]{:S(2)}) collective-permute-start(bf16[4,256,256]{2,1,0:T(8,128)(2,1)} %get-tuple-element.48), channel_id=1, source_target_pairs={{1,2},{3,4},{5,6},{7,8},{9,10},{11,12},{13,14},{15,16},{17,18},{19... | collective-permute-start | bytes 1572872 | tf_op jit(solution)/shard_map/ppermute | solution.py:207
  20.3 6.7 %copy-start.15 = (s32[2]{0:T(128)}, s32[2]{0:T(128)S(1)}, u32[]{:S(2)}) copy-start(s32[2]{0:T(128)S(1)} %pad_add_fusion.where) | copy-start | bytes 28
  20.3 2.8 %copy-start = (s32[8,256,3,256]{3,1,2,0:T(8,128)S(1)}, s32[8,256,3,256]{3,1,2,0:T(8,128)}, u32[]{:S(2)}) copy-start(s32[8,256,3,256]{3,1,2,0:T(8,128)} %param.18) | copy-start | bytes 18874372
  23.1 1.2 %copy-start.3 = (bf16[8,256,256]{2,1,0:T(8,128)(2,1)S(1)}, bf16[8,256,256]{2,1,0:T(8,128)(2,1)}, u32[]{:S(2)}) copy-start(bf16[8,256,256]{2,1,0:T(8,128)(2,1)} %own.1) | copy-start | bytes 3145732
  24.4 59.0 %copy-start.7 = (bf16[256,256]{1,0:T(8,128)(2,1)S(1)}, bf16[256,256]{1,0:T(8,128)(2,1)}, u32[]{:S(2)}) copy-start(bf16[256,256]{1,0:T(8,128)(2,1)} %w_key.3) | copy-start | bytes 393220
  24.4 59.0 %copy-start.8 = (bf16[256,256]{1,0:T(8,128)(2,1)S(1)}, bf16[256,256]{1,0:T(8,128)(2,1)}, u32[]{:S(2)}) copy-start(bf16[256,256]{1,0:T(8,128)(2,1)} %w_value.3) | copy-start | bytes 393220
  24.4 59.0 %copy-start.12 = (s32[8,256]{1,0:T(8,128)S(1)}, s32[8,256]{1,0:T(8,128)}, u32[]{:S(2)}) copy-start(s32[8,256]{1,0:T(8,128)} %banks.1) | copy-start | bytes 24580
  24.4 59.0 %copy-start.13 = (s32[8,256]{1,0:T(8,128)S(1)}, s32[8,256]{1,0:T(8,128)}, u32[]{:S(2)}) copy-start(s32[8,256]{1,0:T(8,128)} %sectors.1) | copy-start | bytes 24580
  27.0 1.4 %copy-start.4 = (f32[8,256,256]{2,1,0:T(8,128)}, f32[8,256,256]{2,1,0:T(8,128)S(1)}, u32[]{:S(2)}) copy-start(f32[8,256,256]{2,1,0:T(8,128)S(1)} %get-tuple-element.43.base) | copy-start | bytes 6291460
  28.4 67.8 %collective-permute-start.11 = (bf16[4,256,256]{2,1,0:T(8,128)(2,1)}, bf16[4,256,256]{2,1,0:T(8,128)(2,1)}, u32[]{:S(2)}, u32[]{:S(2)}) collective-permute-start(bf16[4,256,256]{2,1,0:T(8,128)(2,1)} %get-tuple-element.57), channel_id=1, source_target_pairs={{1,2},{3,4},{5,6},{7,8},{9,10},{11,12},{13,14},{15,16},{17,18},{19... | collective-permute-start | bytes 1572872 | tf_op jit(solution)/shard_map/ppermute | solution.py:240
  35.4 60.8 %collective-permute-start.10 = (bf16[4,256,256]{2,1,0:T(8,128)(2,1)}, bf16[4,256,256]{2,1,0:T(8,128)(2,1)}, u32[]{:S(2)}, u32[]{:S(2)}) collective-permute-start(bf16[4,256,256]{2,1,0:T(8,128)(2,1)} %get-tuple-element.57), channel_id=1, source_target_pairs={{0,1},{1,0},{2,3},{3,2},{4,5},{5,4},{6,7},{7,6},{8,9},{9,8},{10,11... | collective-permute-start | bytes 1572872 | tf_op jit(solution)/shard_map/ppermute | solution.py:239
  62.6 10.6 %collective-permute-start.2 = (bf16[64,256]{1,0:T(8,128)(2,1)S(1)}, bf16[64,256]{1,0:T(8,128)(2,1)S(1)}, u32[]{:S(2)}, u32[]{:S(2)}) collective-permute-start(bf16[64,256]{1,0:T(8,128)(2,1)S(1)} %pad_maximum_fusion), channel_id=1, source_target_pairs={{0,12},{1,13},{2,14},{3,15},{4,8},{5,9},{6,10},{7,11},{8,4},{9,5},... | collective-permute-start | bytes 98312 | tf_op jit(solution)/shard_map/cond/branch_1_fun/ppermute | solution.py:196
  63.0 9.6 %collective-permute-start.1 = (bf16[64,256]{1,0:T(8,128)(2,1)S(1)}, bf16[64,256]{1,0:T(8,128)(2,1)S(1)}, u32[]{:S(2)}, u32[]{:S(2)}) collective-permute-start(bf16[64,256]{1,0:T(8,128)(2,1)S(1)} %pad_maximum_fusion), channel_id=1, source_target_pairs={{0,8},{1,9},{2,10},{3,11},{4,12},{5,13},{6,14},{7,15},{8,0},{9,1},... | collective-permute-start | bytes 98312 | tf_op jit(solution)/shard_map/cond/branch_1_fun/ppermute | solution.py:196
  63.2 6.6 %collective-permute-start = (bf16[64,256]{1,0:T(8,128)(2,1)S(1)}, bf16[64,256]{1,0:T(8,128)(2,1)S(1)}, u32[]{:S(2)}, u32[]{:S(2)}) collective-permute-start(bf16[64,256]{1,0:T(8,128)(2,1)S(1)} %pad_maximum_fusion), channel_id=1, source_target_pairs={{0,4},{1,5},{2,6},{3,7},{4,0},{5,1},{6,2},{7,3},{8,12},{9,13},{10,... | collective-permute-start | bytes 98312 | tf_op jit(solution)/shard_map/cond/branch_1_fun/ppermute | solution.py:196
  73.9 9.4 %collective-permute-start.5 = (bf16[256,256]{1,0:T(8,128)(2,1)}, bf16[256,256]{1,0:T(8,128)(2,1)}, u32[]{:S(2)}, u32[]{:S(2)}) collective-permute-start(bf16[256,256]{1,0:T(8,128)(2,1)} %constant_dynamic-update-slice_fusion), channel_id=1, source_target_pairs={{0,48},{1,49},{2,50},{3,51},{4,52},{5,53},{6,54},{7,55},{8,56},{9,... | collective-permute-start | bytes 393224 | tf_op jit(solution)/shard_map/cond/branch_1_fun/ppermute | solution.py:196
  73.9 9.4 %collective-permute-start.4 = (bf16[256,256]{1,0:T(8,128)(2,1)}, bf16[256,256]{1,0:T(8,128)(2,1)}, u32[]{:S(2)}, u32[]{:S(2)}) collective-permute-start(bf16[256,256]{1,0:T(8,128)(2,1)} %constant_dynamic-update-slice_fusion), channel_id=1, source_target_pairs={{0,32},{1,33},{2,34},{3,35},{4,36},{5,37},{6,38},{7,39},{8,40},{9,... | collective-permute-start | bytes 393224 | tf_op jit(solution)/shard_map/cond/branch_1_fun/ppermute | solution.py:196
  76.2 7.2 %collective-permute-start.3 = (bf16[256,256]{1,0:T(8,128)(2,1)}, bf16[256,256]{1,0:T(8,128)(2,1)}, u32[]{:S(2)}, u32[]{:S(2)}) collective-permute-start(bf16[256,256]{1,0:T(8,128)(2,1)} %constant_dynamic-update-slice_fusion), channel_id=1, source_target_pairs={{0,16},{1,17},{2,18},{3,19},{4,20},{5,21},{6,22},{7,23},{8,24},{9,... | collective-permute-start | bytes 393224 | tf_op jit(solution)/shard_map/cond/branch_1_fun/ppermute | solution.py:196
  83.4 1.6 %copy-start.5 = (f32[8,256,256]{2,1,0:T(8,128)S(1)}, f32[8,256,256]{2,1,0:T(8,128)}, u32[]{:S(2)}) copy-start(f32[8,256,256]{2,1,0:T(8,128)} %copy-done.4) | copy-start | bytes 6291460
  85.0 0.9 copy-start.10
  85.9 0.7 copy-start.14
  87.2 7.0 %copy-start.1 = (bf16[256,1024]{1,0:T(8,128)(2,1)S(1)}, bf16[256,1024]{1,0:T(8,128)(2,1)}, u32[]{:S(2)}) copy-start(bf16[256,1024]{1,0:T(8,128)(2,1)} %w_in.5) | copy-start | bytes 1572868
  87.2 7.0 %copy-start.2 = (bf16[1024,256]{1,0:T(8,128)(2,1)S(1)}, bf16[1024,256]{1,0:T(8,128)(2,1)}, u32[]{:S(2)}) copy-start(bf16[1024,256]{1,0:T(8,128)(2,1)} %w_down.5) | copy-start | bytes 1572868
  87.2 7.0 %copy-start.9 = (bf16[256,256]{1,0:T(8,128)(2,1)S(1)}, bf16[256,256]{1,0:T(8,128)(2,1)}, u32[]{:S(2)}) copy-start(bf16[256,256]{1,0:T(8,128)(2,1)} %w_out.5) | copy-start | bytes 393220
  87.2 7.0 %copy-start.11 = (f32[256]{0:T(256)S(1)}, f32[256]{0:T(256)}, u32[]{:S(2)}) copy-start(f32[256]{0:T(256)} %param.31) | copy-start | bytes 3076
  92.0 10.8 %collective-permute-start.9 = (bf16[3,256,256]{2,1,0:T(8,128)(2,1)S(1)}, bf16[3,256,256]{2,1,0:T(8,128)(2,1)S(1)}, u32[]{:S(2)}, u32[]{:S(2)}) collective-permute-start(bf16[3,256,256]{2,1,0:T(8,128)(2,1)S(1)} %get-tuple-element.55), channel_id=1, source_target_pairs={{0,64},{64,128},{128,192},{1,65},{65,129},{129,193},{2,66},{66,130... | collective-permute-start | bytes 1179656 | tf_op jit(solution)/shard_map/ppermute | solution.py:270
  (1 other events, 0.6 us)

commit v4 on v2

--- a/solution.py
+++ b/solution.py
@@ -9,7 +9,8 @@
 
 HEADS = 4
 LAGS = 3
-HALF = 4
+EARLY = 3
+LATE = 5
 SLOT = 16
 LOG2 = math.log(2.0)
 GELU = math.sqrt(2.0 / math.pi)
@@ -92,7 +93,7 @@
     rows_each, firms = tables[0].shape[0], base.shape[1]
     row = lax.broadcasted_iota(jnp.int32, (rows_each, firms), 0)
     normed = []
-    for m in list(range(HALF, 2 * HALF)) + list(range(HALF)):
+    for m in list(range(EARLY, EARLY + LATE)) + list(range(EARLY)):
         bank, sector = banks[m : m + 1], sectors[m : m + 1]
         bank = (lax.shift_right_logical(bank, 3) ^ me) * SLOT + (bank & 7)
         sector = (lax.shift_right_logical(sector, 2) ^ me) * SLOT + 8 + (sector & 3)
@@ -102,19 +103,26 @@
             total = total + lax.dot_general(
                 chosen.astype(BF), table[...], (((0,), (0,)), ((), ())), preferred_element_type=F32
             )
-        if m < HALF:
+        if m < EARLY:
             early_base[m] = total
         else:
-            mixed = mix(m, total, tiles, scale, even_rows[m - HALF], odd_rows[m - HALF], w_supply[...])
-            mixed_out[m - HALF] = mixed
+            i = m - EARLY
+            mixed = mix(m, total, tiles, scale, even_rows[i], odd_rows[i], w_supply[...])
+            mixed_out[i] = mixed
             normed.append(rms_norm(mixed, gain_mix[...]).astype(BF))
-            if m >= 2 * HALF - LAGS:
-                normed_out[m - 2 * HALF + LAGS] = normed[-1]
+            if i >= LATE - LAGS:
+                normed_out[i - LATE + LAGS] = normed[-1]
     shape = query_out.shape
     rows = stack(normed)
     query_out[...] = mm(rows, w_query[...]).astype(BF).reshape(shape)
     key_out[...] = mm(rows, w_key[...]).astype(BF).reshape(shape)
     value_out[...] = mm(rows, w_value[...]).astype(BF).reshape(shape)
+
+
+def join_kernel(*refs):
+    rows = refs[0].shape[0]
+    for i, part in enumerate(refs[:-1]):
+        refs[-1][i * rows : (i + 1) * rows] = part[...]
 
 
 def write_back(final, buffer, result, sems, first):
@@ -129,12 +137,14 @@
 
 
 def last_kernel(mixed, query, key, value, w_out, w_in, w_down, gain_ffn, result, buffer, sems):
-    attended = attend(
-        query[LAGS], [key[LAGS - j] for j in range(LAGS + 1)], [value[LAGS - j] for j in range(LAGS + 1)],
-        head_matrix(query.shape[-1]),
-    )
-    final = finish(mixed[LAGS], attended, w_out[...], w_in[...], w_down[...], gain_ffn[...])
-    write_back(final, buffer, result, sems, 2 * HALF - 1)
+    count = LATE - LAGS
+    firms, width = query.shape[1:]
+    flat = (count * firms, width)
+    keys = lagged([key[i] for i in range(LATE)], count)
+    values = lagged([value[i] for i in range(LATE)], count)
+    attended = attend(query[LAGS:].reshape(flat), keys, values, head_matrix(width))
+    final = finish(mixed[LAGS:].reshape(flat), attended, w_out[...], w_in[...], w_down[...], gain_ffn[...])
+    write_back(final, buffer, result, sems, EARLY + LAGS)
 
 
 def early_kernel(
@@ -145,21 +155,21 @@
     del started
     firms = base.shape[1]
     mixed, normed = [], []
-    for m in range(HALF):
+    for m in range(EARLY):
         mixed.append(mix(m, base[m], tiles, scale, even_rows[m], odd_rows[m], w_supply[...]))
         normed.append(rms_norm(mixed[-1], gain_mix[...]).astype(BF))
     rows = stack(normed)
-    cut = lambda rows: [rows[i * firms : (i + 1) * firms] for i in range(HALF)]
+    cut = lambda rows: [rows[i * firms : (i + 1) * firms] for i in range(EARLY)]
     query = cut(mm(rows, w_query[...]).astype(BF))
     key = cut(mm(rows, w_key[...]).astype(BF))
     value = cut(mm(rows, w_value[...]).astype(BF))
     for m in range(LAGS):
         mixed_out[m], query_out[m], key_out[m], value_out[m] = mixed[m], query[m], key[m], value[m]
-    keys = lagged(key + [late_key[m] for m in range(LAGS)], HALF)
-    values = lagged(value + [late_value[m] for m in range(LAGS)], HALF)
-    queries = stack([query[LAGS]] + [late_query[m] for m in range(LAGS)])
+    keys = lagged(key + [late_key[m] for m in range(LAGS)], EARLY)
+    values = lagged(value + [late_value[m] for m in range(LAGS)], EARLY)
+    queries = stack(query[LAGS:] + [late_query[m] for m in range(LAGS)])
     attended = attend(queries, keys, values, head_matrix(base.shape[-1]))
-    total = stack([mixed[LAGS]] + [late_mixed[m] for m in range(LAGS)])
+    total = stack(mixed[LAGS:] + [late_mixed[m] for m in range(LAGS)])
     final = finish(total, attended, w_out[...], w_in[...], w_down[...], gain_ffn[...])
     write_back(final, buffer, result, sems, LAGS)
 
@@ -195,29 +205,41 @@
     def swap(x, bits):
         return lax.ppermute(x, "firm", [(i, i ^ bits) for i in range(devices)])
 
-    late = features[HALF:]
+    spare = SLOT - bank_table.shape[0] - sector_table.shape[0]
+    hub = jnp.concatenate([bank_table, sector_table, jnp.zeros((spare, width), BF)], axis=0)
+    near = [hub] + [swap(hub, i) for i in (1, 2, 3)]
+    late = features[EARLY:]
     late_even = lax.ppermute(late, "firm", even_pairs)
     late_odd = lax.ppermute(late, "firm", odd_pairs)
 
-    spare = SLOT - bank_table.shape[0] - sector_table.shape[0]
-    hub = jnp.concatenate([bank_table, sector_table, jnp.zeros((spare, width), BF)], axis=0)
-    hub, late = lax.optimization_barrier((hub, late))
-    hub = jnp.concatenate([hub] + [swap(hub, i) for i in (1, 2, 3)], axis=0)
-
-    early = features[:HALF]
+    def joined(parts):
+        rows = parts[0].shape[0]
+        return pl.pallas_call(
+            join_kernel,
+            in_specs=[VM] * len(parts),
+            out_specs=VM,
+            out_shape=jax.ShapeDtypeStruct((len(parts) * rows, width), BF),
+            cost_estimate=pl.CostEstimate(flops=0, bytes_accessed=1 << 10, transcendentals=0),
+            name="join",
+        )(*parts)
+
+    def spread(near):
+        hub = joined(near)
+        hub = joined([hub] + [swap(hub, i) for i in (4, 8, 12)])
+        return [hub] + [swap(hub, i) for i in (16, 32, 48)]
+
+    tables = spread(near)
+    tables, early = lax.optimization_barrier((tables, features[:EARLY]))
     early_even = lax.ppermute(early, "firm", even_pairs)
     early_odd = lax.ppermute(early, "firm", odd_pairs)
-
-    hub = jnp.concatenate([hub] + [swap(hub, i) for i in (4, 8, 12)], axis=0)
-    tables = [hub] + [swap(hub, i) for i in (16, 32, 48)]
 
     counts = jnp.transpose(supply_counts, (0, 2, 1, 3))
     gain_mix = gain_mix.reshape(1, width)
     gain_ffn = gain_ffn.reshape(1, width)
 
-    def cost(units, mebibytes):
+    def cost(units, kibibytes):
         return pl.CostEstimate(
-            flops=2 * units * firms * width * width, bytes_accessed=mebibytes << 20, transcendentals=0
+            flops=2 * units * firms * width * width, bytes_accessed=kibibytes << 10, transcendentals=0
         )
 
     def like(count, dtype, lanes=width):
@@ -236,7 +258,7 @@
             like(months, F32), jax.ShapeDtypeStruct((months, 2, firms, firms), BF), like(months, F32, 128),
         ],
         compiler_params=params,
-        cost_estimate=cost(16, 12),
+        cost_estimate=cost(200, 1 << 14),
         name="own_block",
     )(where, counts, features, w_supply)
 
@@ -245,10 +267,10 @@
         in_specs=[SM] + [VM] * 16,
         out_specs=[VM] * 6,
         out_shape=[
-            like(HALF, F32), like(HALF, F32), like(LAGS, BF), like(HALF, BF), like(HALF, BF), like(HALF, BF),
+            like(EARLY, F32), like(LATE, F32), like(LAGS, BF), like(LATE, BF), like(LATE, BF), like(LATE, BF),
         ],
         compiler_params=params,
-        cost_estimate=cost(60, 12),
+        cost_estimate=cost(1, 1),
         name="late_months",
     )(
         where, base, tiles, scale, late_even, late_odd, bank_ids, sector_ids, *tables,
@@ -266,9 +288,9 @@
         in_specs=[VM] * 8,
         out_specs=ANY,
         out_shape=like(months, BF),
-        scratch_shapes=scratch(1),
-        compiler_params=params,
-        cost_estimate=cost(16, 3),
+        scratch_shapes=scratch(LATE - LAGS),
+        compiler_params=params,
+        cost_estimate=cost(1, 1),
         name="last_month",
     )(late_mixed, late_query, late_key, late_value, *end_weights)
 
@@ -277,10 +299,10 @@
         in_specs=[VM] * 18 + [ANY],
         out_specs=[ANY] + [VM] * 4,
         out_shape=[like(months, BF), like(LAGS, F32), like(LAGS, BF), like(LAGS, BF), like(LAGS, BF)],
-        scratch_shapes=scratch(HALF),
+        scratch_shapes=scratch(EARLY),
         input_output_aliases={18: 0},
         compiler_params=params,
-        cost_estimate=cost(90, 8),
+        cost_estimate=cost(1, 1),
         name="early_months",
     )(
         early_base, tiles, scale, early_even, early_odd, late_mixed, late_query, late_key, late_value,
@@ -295,7 +317,7 @@
         scratch_shapes=scratch(LAGS),
         input_output_aliases={11: 0},
         compiler_params=params,
-        cost_estimate=cost(54, 4),
+        cost_estimate=cost(1, 1),
         name="first_months",
     )(earlier, mixed, query, key, value, w_key, w_value, *end_weights, result)
 

time: 80.3 us -> 77 us (0.959)
  the two profiles are of different devices: /device:TPU:25 before, /device:TPU:40 now
where the time goes in v4:
time: 77 us; the launch traced here: 76.5 us
  starting transfers between devices  28.3 us (37%)
  Pallas kernels  20.8 us (27%)
  waiting for transfers between devices  17.5 us (23%)
  local copies, waits for them, and re-layouts  8.58 us (11%)
  other arithmetic  0.85 us (1%)
    ppermute x9, starting transfers between devices, swap(): return lax.ppermute(x, 'firm', [(i, i ^ bits) for i in range(devices)])  16.1 us
    ppermute x9, waiting for transfers between devices, swap(): return lax.ppermute(x, 'firm', [(i, i ^ bits) for i in range(devices)])  8.99 us
    ppermute x1, waiting for transfers between devices, body(): early_odd = lax.ppermute(early, 'firm', odd_pairs)  8.46 us
    ppermute x1, starting transfers between devices, body(): late_odd = lax.ppermute(late, 'firm', odd_pairs)  8.02 us
    unnamed x44, local copies, waits for them, and re-layouts  7.34 us
    pallas_call x1, Pallas kernels, body(): pl.pallas_call(early_kernel, in_specs=[VM] * 18 + [ANY], out_specs=[ANY]...  4.49 us
    pallas_call x1, Pallas kernels, body(): pl.pallas_call(late_kernel, in_specs=[SM] + [VM] * 16, out_specs=[VM] * 6...  4.43 us
    pallas_call x1, Pallas kernels, body(): pl.pallas_call(first_kernel, in_specs=[VM] * 11 + [ANY], out_specs=ANY, o...  3.63 us
  transfers between devices with their start and end apart: 14, of which 4 were waited for; matrix products, arithmetic and copies ran while one was open for 2% of the time, Pallas kernels for 22%

profile of v4, /device:TPU:40, one launch (start us, length us, event | category | flops | bytes accessed | tf_op | source)
XLA Modules:
  0.0 76.5 jit_solution(8543753134431991818)
XLA Ops:
  0.1 0.8 %maximum_maximum_fusion.refs_0_ = bf16[16,256]{1,0:T(8,128)(2,1)S(1)} fusion(bf16[4,256]{1,0:T(4,128)(2,1)} %param.20, bf16[8,256]{1,0:T(8,128)(2,1)} %param.19, bf16[16]{0:T(256)(128)(2,1)S(1)} %pad.2.clone), kind=kLoop, calls=%fused_computation | loop fusion | flops 24576 | bytes 14368 | tf_op jit(solution)/shard_map/concatenate | solution.py:209
  0.9 5.4 %collective-permute-start.4 = (bf16[16,256]{1,0:T(8,128)(2,1)S(1)}, bf16[16,256]{1,0:T(8,128)(2,1)S(1)}, u32[]{:S(2)}, u32[]{:S(2)}) collective-permute-start(bf16[16,256]{1,0:T(8,128)(2,1)S(1)} %maximum_maximum_fusion.refs_0_), channel_id=1, source_target_pairs={{0,3},{1,2},{2,1},{3,0},{4,7},{5,6},{6,5},{7,4},{8,11},{9,10},{10,... | collective-permute-start | bytes 24584 | tf_op jit(solution)/shard_map/ppermute | solution.py:206
  6.3 1.4 %collective-permute-start.3 = (bf16[16,256]{1,0:T(8,128)(2,1)S(1)}, bf16[16,256]{1,0:T(8,128)(2,1)S(1)}, u32[]{:S(2)}, u32[]{:S(2)}) collective-permute-start(bf16[16,256]{1,0:T(8,128)(2,1)S(1)} %maximum_maximum_fusion.refs_0_), channel_id=1, source_target_pairs={{0,2},{1,3},{2,0},{3,1},{4,6},{5,7},{6,4},{7,5},{8,10},{9,11},{10,... | collective-permute-start | bytes 24584 | tf_op jit(solution)/shard_map/ppermute | solution.py:206
  7.7 1.0 %collective-permute-start.2 = (bf16[16,256]{1,0:T(8,128)(2,1)S(1)}, bf16[16,256]{1,0:T(8,128)(2,1)S(1)}, u32[]{:S(2)}, u32[]{:S(2)}) collective-permute-start(bf16[16,256]{1,0:T(8,128)(2,1)S(1)} %maximum_maximum_fusion.refs_0_), channel_id=1, source_target_pairs={{0,1},{1,0},{2,3},{3,2},{4,5},{5,4},{6,7},{7,6},{8,9},{9,8},{10,11... | collective-permute-start | bytes 24584 | tf_op jit(solution)/shard_map/ppermute | solution.py:206
  8.8 1.1 %slice.6 = bf16[5,256,256]{2,1,0:T(8,128)(2,1)S(1)} slice(bf16[8,256,256]{2,1,0:T(8,128)(2,1)} %own.1), slice={[3:8], [0:256], [0:256]} | slice | bytes 1310720 | tf_op jit(solution)/shard_map/slice | solution.py:211
  9.9 8.0 %collective-permute-start.1 = (bf16[5,256,256]{2,1,0:T(8,128)(2,1)S(1)}, bf16[5,256,256]{2,1,0:T(8,128)(2,1)S(1)}, u32[]{:S(2)}, u32[]{:S(2)}) collective-permute-start(bf16[5,256,256]{2,1,0:T(8,128)(2,1)S(1)} %slice.6), channel_id=1, source_target_pairs={{1,2},{3,4},{5,6},{7,8},{9,10},{11,12},{13,14},{15,16},{17,18},{19... | collective-permute-start | bytes 1966088 | tf_op jit(solution)/shard_map/ppermute | solution.py:213
  18.1 0.6 copy-done.19
  18.6 0.6 copy-done.21
  19.2 1.4 %join.2.refs_0_ = bf16[64,256]{1,0:T(8,128)(2,1)} custom-call(bf16[16,256]{1,0:T(8,128)(2,1)} %copy-done.15, bf16[16,256]{1,0:T(8,128)(2,1)} %copy-done.21, bf16[16,256]{1,0:T(8,128)(2,1)} %copy-done.20, bf16[16,256]{1,0:T(8,128)(2,1)} %copy-done.19), custom_call_target="tpu_custom_call" | custom-call | bytes 1024 | tf_op jit(solution)/shard_map/join/pallas_call | solution.py:217
  20.6 2.1 %collective-permute-start.7 = (bf16[64,256]{1,0:T(8,128)(2,1)}, bf16[64,256]{1,0:T(8,128)(2,1)S(1)}, u32[]{:S(2)}, u32[]{:S(2)}) collective-permute-start(bf16[64,256]{1,0:T(8,128)(2,1)} %join.2.refs_0_), channel_id=1, source_target_pairs={{0,12},{1,13},{2,14},{3,15},{4,8},{5,9},{6,10},{7,11},{8,4},{9,5},... | collective-permute-start | bytes 98312 | tf_op jit(solution)/shard_map/ppermute | solution.py:206
  22.7 0.8 %collective-permute-start.6 = (bf16[64,256]{1,0:T(8,128)(2,1)}, bf16[64,256]{1,0:T(8,128)(2,1)S(1)}, u32[]{:S(2)}, u32[]{:S(2)}) collective-permute-start(bf16[64,256]{1,0:T(8,128)(2,1)} %join.2.refs_0_), channel_id=1, source_target_pairs={{0,8},{1,9},{2,10},{3,11},{4,12},{5,13},{6,14},{7,15},{8,0},{9,1},... | collective-permute-start | bytes 98312 | tf_op jit(solution)/shard_map/ppermute | solution.py:206
  23.5 1.2 %collective-permute-start.5 = (bf16[64,256]{1,0:T(8,128)(2,1)}, bf16[64,256]{1,0:T(8,128)(2,1)S(1)}, u32[]{:S(2)}, u32[]{:S(2)}) collective-permute-start(bf16[64,256]{1,0:T(8,128)(2,1)} %join.2.refs_0_), channel_id=1, source_target_pairs={{0,4},{1,5},{2,6},{3,7},{4,0},{5,1},{6,2},{7,3},{8,12},{9,13},{10,... | collective-permute-start | bytes 98312 | tf_op jit(solution)/shard_map/ppermute | solution.py:206
  24.8 1.3 %collective-permute-done.7.refs_3_ = bf16[64,256]{1,0:T(8,128)(2,1)S(1)} collective-permute-done((bf16[64,256]{1,0:T(8,128)(2,1)}, bf16[64,256]{1,0:T(8,128)(2,1)S(1)}, u32[]{:S(2)}, u32[]{:S(2)}) %collective-permute-start.7) | collective-permute-done | bytes 32800 | tf_op jit(solution)/shard_map/ppermute | solution.py:206
  26.1 2.4 %collective-permute-done.6.refs_2_ = bf16[64,256]{1,0:T(8,128)(2,1)S(1)} collective-permute-done((bf16[64,256]{1,0:T(8,128)(2,1)}, bf16[64,256]{1,0:T(8,128)(2,1)S(1)}, u32[]{:S(2)}, u32[]{:S(2)}) %collective-permute-start.6) | collective-permute-done | bytes 32800 | tf_op jit(solution)/shard_map/ppermute | solution.py:206
  28.4 0.6 copy-done.17
  29.0 0.6 copy-done.18
  29.6 1.5 %join.3.rest_0_ = bf16[256,256]{1,0:T(8,128)(2,1)} custom-call(bf16[64,256]{1,0:T(8,128)(2,1)} %join.2.refs_0_, bf16[64,256]{1,0:T(8,128)(2,1)} %copy-done.18, bf16[64,256]{1,0:T(8,128)(2,1)} %copy-done.17, bf16[64,256]{1,0:T(8,128)(2,1)} %copy-done.16), custom_call_target="tpu_custom_call" | custom-call | bytes 1024 | tf_op jit(solution)/shard_map/join/pallas_call | solution.py:217
  31.1 1.6 %collective-permute-start.10 = (bf16[256,256]{1,0:T(8,128)(2,1)}, bf16[256,256]{1,0:T(8,128)(2,1)S(1)}, u32[]{:S(2)}, u32[]{:S(2)}) collective-permute-start(bf16[256,256]{1,0:T(8,128)(2,1)} %join.3.rest_0_), channel_id=1, source_target_pairs={{0,48},{1,49},{2,50},{3,51},{4,52},{5,53},{6,54},{7,55},{8,56},{9,... | collective-permute-start | bytes 393224 | tf_op jit(solution)/shard_map/ppermute | solution.py:206
  32.7 0.9 %collective-permute-start.9 = (bf16[256,256]{1,0:T(8,128)(2,1)}, bf16[256,256]{1,0:T(8,128)(2,1)S(1)}, u32[]{:S(2)}, u32[]{:S(2)}) collective-permute-start(bf16[256,256]{1,0:T(8,128)(2,1)} %join.3.rest_0_), channel_id=1, source_target_pairs={{0,32},{1,33},{2,34},{3,35},{4,36},{5,37},{6,38},{7,39},{8,40},{9,... | collective-permute-start | bytes 393224 | tf_op jit(solution)/shard_map/ppermute | solution.py:206
  33.6 1.6 %collective-permute-start.8 = (bf16[256,256]{1,0:T(8,128)(2,1)}, bf16[256,256]{1,0:T(8,128)(2,1)S(1)}, u32[]{:S(2)}, u32[]{:S(2)}) collective-permute-start(bf16[256,256]{1,0:T(8,128)(2,1)} %join.3.rest_0_), channel_id=1, source_target_pairs={{0,16},{1,17},{2,18},{3,19},{4,20},{5,21},{6,22},{7,23},{8,24},{9,... | collective-permute-start | bytes 393224 | tf_op jit(solution)/shard_map/ppermute | solution.py:206
  35.2 1.2 %copy-done.5 = bf16[8,256,256]{2,1,0:T(8,128)(2,1)S(1)} copy-done((bf16[8,256,256]{2,1,0:T(8,128)(2,1)S(1)}, bf16[8,256,256]{2,1,0:T(8,128)(2,1)}, u32[]{:S(2)}) %copy-start.5) | copy-done | bytes 1048600
  36.4 0.9 %copy-done.6 = bf16[256,256]{1,0:T(8,128)(2,1)S(1)} copy-done((bf16[256,256]{1,0:T(8,128)(2,1)S(1)}, bf16[256,256]{1,0:T(8,128)(2,1)}, u32[]{:S(2)}) %copy-start.6) | copy-done | bytes 131096
  37.3 2.8 %copy-done.14 = s32[8,256,3,256]{3,1,2,0:T(8,128)S(1)} copy-done((s32[8,256,3,256]{3,1,2,0:T(8,128)S(1)}, s32[8,256,3,256]{3,1,2,0:T(8,128)}, u32[]{:S(2)}) %copy-start.14) | copy-done | bytes 6291480
  40.2 2.7 %own_block.1 = (f32[8,256,256]{2,1,0:T(8,128)S(1)}, bf16[8,2,256,256]{3,2,1,0:T(8,128)(2,1)S(1)}, f32[8,256,128]{2,1,0:T(8,128)S(1)}) custom-call(s32[2]{0:T(128)S(1)} %pad_add_fusion.where, s32[8,3,256,256]{3,2,1,0:T(8,128)S(1)} %bitcast.10, bf16[8,256,256]{2,1,0:T(8,128)(2,1)S(1)} %copy-done.5, bf16[256,256]{1,0:T(8,128)(2,1)S(1)} %copy-done.6), custom_call_target="tpu_custom_call" | custom-call | flops 6710886400 | bytes 16777216 | tf_op jit(solution)/shard_map/own_block/pallas_call | solution.py:250
  42.9 5.3 %collective-permute-done.8.rest_1_ = bf16[256,256]{1,0:T(8,128)(2,1)S(1)} collective-permute-done((bf16[256,256]{1,0:T(8,128)(2,1)}, bf16[256,256]{1,0:T(8,128)(2,1)S(1)}, u32[]{:S(2)}, u32[]{:S(2)}) %collective-permute-start.8) | collective-permute-done | bytes 131104 | tf_op jit(solution)/shard_map/ppermute | solution.py:206
  48.2 1.9 %collective-permute-start.13 = (bf16[3,256,256]{2,1,0:T(8,128)(2,1)S(1)}, bf16[3,256,256]{2,1,0:T(8,128)(2,1)S(1)}, u32[]{:S(2)}, u32[]{:S(2)}) collective-permute-start(bf16[3,256,256]{2,1,0:T(8,128)(2,1)S(1)} %slice.7), channel_id=1, source_target_pairs={{1,2},{3,4},{5,6},{7,8},{9,10},{11,12},{13,14},{15,16},{17,18},{19... | collective-permute-start | bytes 1179656 | tf_op jit(solution)/shard_map/ppermute | solution.py:234
  50.4 4.4 %late_months.1 = (f32[3,256,256]{2,1,0:T(8,128)S(1)}, f32[5,256,256]{2,1,0:T(8,128)S(1)}, bf16[3,256,256]{2,1,0:T(8,128)(2,1)S(1)}, bf16[5,256,256]{2,1,0:T(8,12...) custom-call(s32[2]{0:T(128)S(1)} %pad_add_fusion.where, ...), custom_call_target="tpu_custom_call" | custom-call | flops 33554432 | bytes 1024 | tf_op jit(solution)/shard_map/late_months/pallas_call | solution.py:265
  54.8 2.1 %collective-permute-start.11 = (bf16[3,256,256]{2,1,0:T(8,128)(2,1)S(1)}, bf16[3,256,256]{2,1,0:T(8,128)(2,1)S(1)}, u32[]{:S(2)}, u32[]{:S(2)}) collective-permute-start(bf16[3,256,256]{2,1,0:T(8,128)(2,1)S(1)} %get-tuple-element.31), channel_id=1, source_target_pairs={{0,64},{64,128},{128,192},{1,65},{65,129},{129,193},{2,66},{66,130... | collective-permute-start | bytes 1179656 | tf_op jit(solution)/shard_map/ppermute | solution.py:280
  57.0 2.8 %last_month.1.started = bf16[8,256,256]{2,1,0:T(8,128)(2,1)} custom-call(f32[5,256,256]{2,1,0:T(8,128)S(1)} %get-tuple-element.34.mixed.late_mixed, bf16[5,256,256]{2,1,0:T(8,128)(2,1)S(1)} %get-tuple-element.35.query.late_query, bf16[5,256,256]{2,1,0:T(8,128)(2,1)S(1)} %get-tuple-element.36.key.late_key, ...), custom_call_target="tpu_custom_call" | custom-call | flops 33554432 | bytes 1024 | tf_op jit(solution)/shard_map/last_month/pallas_call | solution.py:286
  59.8 8.5 %collective-permute-done.13.odd_rows = bf16[3,256,256]{2,1,0:T(8,128)(2,1)S(1)} collective-permute-done((bf16[3,256,256]{2,1,0:T(8,128)(2,1)S(1)}, bf16[3,256,256]{2,1,0:T(8,128)(2,1)S(1)}, u32[]{:S(2)}, u32[]{:S(2)}) %collective-permute-start.13) | collective-permute-done | bytes 393248 | tf_op jit(solution)/shard_map/ppermute | solution.py:234
  68.2 4.5 %early_months.1 = (bf16[8,256,256]{2,1,0:T(8,128)(2,1)}, f32[3,256,256]{2,1,0:T(8,128)S(1)}, bf16[3,256,256]{2,1,0:T(8,128)(2,1)S(1)}, bf16[3,256,256]{2,1,0:T(8,128)(2,1)S(1)}, bf16[3,256,256]{2,1,0:T(8,128)(2,1)S(1)}) custom-call(f32[3,256,256]{2,1,0:T(8,128)S(1)} %get-tuple-element.32.base, ...), custom_call_target="tpu_custom_call", output_to_operand_aliasing={{0}: (18, {})} | custom-call | flops 33554432 | bytes 1024 | tf_op jit(solution)/shard_map/early_months/pallas_call | solution.py:297
  72.7 3.6 %first_months.1 = bf16[8,256,256]{2,1,0:T(8,128)(2,1)} custom-call(bf16[3,256,256]{2,1,0:T(8,128)(2,1)S(1)} %collective-permute-done.11.earlier, f32[3,256,256]{2,1,0:T(8,128)S(1)} %get-tuple-element.38.mixed, bf16[3,256,256]{2,1,0:T(8,128)(2,1)S(1)} %get-tuple-element.39.query, ...), custom_call_target="tpu_custom_call", output_to_operand_aliasing={{}: (11, {})} | custom-call | flops 33554432 | bytes 1024 | tf_op jit(solution)/shard_map/first_months/pallas_call | solution.py:312
  (53 shorter events, 0.5 us)
Async XLA Ops:
  0.9 17.2 %copy-start.15 = (bf16[16,256]{1,0:T(8,128)(2,1)}, bf16[16,256]{1,0:T(8,128)(2,1)S(1)}, u32[]{:S(2)}) copy-start(bf16[16,256]{1,0:T(8,128)(2,1)S(1)} %maximum_maximum_fusion.refs_0_) | copy-start | bytes 24580
  0.9 17.2 %collective-permute-start.4 = (bf16[16,256]{1,0:T(8,128)(2,1)S(1)}, bf16[16,256]{1,0:T(8,128)(2,1)S(1)}, u32[]{:S(2)}, u32[]{:S(2)}) collective-permute-start(bf16[16,256]{1,0:T(8,128)(2,1)S(1)} %maximum_maximum_fusion.refs_0_), channel_id=1, source_target_pairs={{0,3},{1,2},{2,1},{3,0},{4,7},{5,6},{6,5},{7,4},{8,11},{9,10},{10,... | collective-permute-start | bytes 24584 | tf_op jit(solution)/shard_map/ppermute | solution.py:206
  6.3 11.8 %collective-permute-start.3 = (bf16[16,256]{1,0:T(8,128)(2,1)S(1)}, bf16[16,256]{1,0:T(8,128)(2,1)S(1)}, u32[]{:S(2)}, u32[]{:S(2)}) collective-permute-start(bf16[16,256]{1,0:T(8,128)(2,1)S(1)} %maximum_maximum_fusion.refs_0_), channel_id=1, source_target_pairs={{0,2},{1,3},{2,0},{3,1},{4,6},{5,7},{6,4},{7,5},{8,10},{9,11},{10,... | collective-permute-start | bytes 24584 | tf_op jit(solution)/shard_map/ppermute | solution.py:206
  7.7 10.3 %collective-permute-start.2 = (bf16[16,256]{1,0:T(8,128)(2,1)S(1)}, bf16[16,256]{1,0:T(8,128)(2,1)S(1)}, u32[]{:S(2)}, u32[]{:S(2)}) collective-permute-start(bf16[16,256]{1,0:T(8,128)(2,1)S(1)} %maximum_maximum_fusion.refs_0_), channel_id=1, source_target_pairs={{0,1},{1,0},{2,3},{3,2},{4,5},{5,4},{6,7},{7,6},{8,9},{9,8},{10,11... | collective-permute-start | bytes 24584 | tf_op jit(solution)/shard_map/ppermute | solution.py:206
  9.9 40.4 %collective-permute-start.1 = (bf16[5,256,256]{2,1,0:T(8,128)(2,1)S(1)}, bf16[5,256,256]{2,1,0:T(8,128)(2,1)S(1)}, u32[]{:S(2)}, u32[]{:S(2)}) collective-permute-start(bf16[5,256,256]{2,1,0:T(8,128)(2,1)S(1)} %slice.6), channel_id=1, source_target_pairs={{1,2},{3,4},{5,6},{7,8},{9,10},{11,12},{13,14},{15,16},{17,18},{19... | collective-permute-start | bytes 1966088 | tf_op jit(solution)/shard_map/ppermute | solution.py:213
  17.9 32.3 %collective-permute-start = (bf16[5,256,256]{2,1,0:T(8,128)(2,1)S(1)}, bf16[5,256,256]{2,1,0:T(8,128)(2,1)S(1)}, u32[]{:S(2)}, u32[]{:S(2)}) collective-permute-start(bf16[5,256,256]{2,1,0:T(8,128)(2,1)S(1)} %slice.6), channel_id=1, source_target_pairs={{0,1},{1,0},{2,3},{3,2},{4,5},{5,4},{6,7},{7,6},{8,9},{9,8},{10,11... | collective-permute-start | bytes 1966088 | tf_op jit(solution)/shard_map/ppermute | solution.py:212
  18.0 0.6 copy-start.19
  20.6 5.4 %collective-permute-start.7 = (bf16[64,256]{1,0:T(8,128)(2,1)}, bf16[64,256]{1,0:T(8,128)(2,1)S(1)}, u32[]{:S(2)}, u32[]{:S(2)}) collective-permute-start(bf16[64,256]{1,0:T(8,128)(2,1)} %join.2.refs_0_), channel_id=1, source_target_pairs={{0,12},{1,13},{2,14},{3,15},{4,8},{5,9},{6,10},{7,11},{8,4},{9,5},... | collective-permute-start | bytes 98312 | tf_op jit(solution)/shard_map/ppermute | solution.py:206
  22.7 5.7 %collective-permute-start.6 = (bf16[64,256]{1,0:T(8,128)(2,1)}, bf16[64,256]{1,0:T(8,128)(2,1)S(1)}, u32[]{:S(2)}, u32[]{:S(2)}) collective-permute-start(bf16[64,256]{1,0:T(8,128)(2,1)} %join.2.refs_0_), channel_id=1, source_target_pairs={{0,8},{1,9},{2,10},{3,11},{4,12},{5,13},{6,14},{7,15},{8,0},{9,1},... | collective-permute-start | bytes 98312 | tf_op jit(solution)/shard_map/ppermute | solution.py:206
  23.5 4.9 %collective-permute-start.5 = (bf16[64,256]{1,0:T(8,128)(2,1)}, bf16[64,256]{1,0:T(8,128)(2,1)S(1)}, u32[]{:S(2)}, u32[]{:S(2)}) collective-permute-start(bf16[64,256]{1,0:T(8,128)(2,1)} %join.2.refs_0_), channel_id=1, source_target_pairs={{0,4},{1,5},{2,6},{3,7},{4,0},{5,1},{6,2},{7,3},{8,12},{9,13},{10,... | collective-permute-start | bytes 98312 | tf_op jit(solution)/shard_map/ppermute | solution.py:206
  26.1 2.4 %copy-start.16 = (bf16[64,256]{1,0:T(8,128)(2,1)}, bf16[64,256]{1,0:T(8,128)(2,1)S(1)}, u32[]{:S(2)}) copy-start(bf16[64,256]{1,0:T(8,128)(2,1)S(1)} %collective-permute-done.7.refs_3_) | copy-start | bytes 98308
  31.1 11.8 %collective-permute-start.10 = (bf16[256,256]{1,0:T(8,128)(2,1)}, bf16[256,256]{1,0:T(8,128)(2,1)S(1)}, u32[]{:S(2)}, u32[]{:S(2)}) collective-permute-start(bf16[256,256]{1,0:T(8,128)(2,1)} %join.3.rest_0_), channel_id=1, source_target_pairs={{0,48},{1,49},{2,50},{3,51},{4,52},{5,53},{6,54},{7,55},{8,56},{9,... | collective-permute-start | bytes 393224 | tf_op jit(solution)/shard_map/ppermute | solution.py:206
  32.7 10.2 %collective-permute-start.9 = (bf16[256,256]{1,0:T(8,128)(2,1)}, bf16[256,256]{1,0:T(8,128)(2,1)S(1)}, u32[]{:S(2)}, u32[]{:S(2)}) collective-permute-start(bf16[256,256]{1,0:T(8,128)(2,1)} %join.3.rest_0_), channel_id=1, source_target_pairs={{0,32},{1,33},{2,34},{3,35},{4,36},{5,37},{6,38},{7,39},{8,40},{9,... | collective-permute-start | bytes 393224 | tf_op jit(solution)/shard_map/ppermute | solution.py:206
  33.6 14.6 %collective-permute-start.8 = (bf16[256,256]{1,0:T(8,128)(2,1)}, bf16[256,256]{1,0:T(8,128)(2,1)S(1)}, u32[]{:S(2)}, u32[]{:S(2)}) collective-permute-start(bf16[256,256]{1,0:T(8,128)(2,1)} %join.3.rest_0_), channel_id=1, source_target_pairs={{0,16},{1,17},{2,18},{3,19},{4,20},{5,21},{6,22},{7,23},{8,24},{9,... | collective-permute-start | bytes 393224 | tf_op jit(solution)/shard_map/ppermute | solution.py:206
  35.2 1.2 %copy-start.5 = (bf16[8,256,256]{2,1,0:T(8,128)(2,1)S(1)}, bf16[8,256,256]{2,1,0:T(8,128)(2,1)}, u32[]{:S(2)}) copy-start(bf16[8,256,256]{2,1,0:T(8,128)(2,1)} %own.1) | copy-start | bytes 3145732
  36.4 0.9 %copy-start.6 = (bf16[256,256]{1,0:T(8,128)(2,1)S(1)}, bf16[256,256]{1,0:T(8,128)(2,1)}, u32[]{:S(2)}) copy-start(bf16[256,256]{1,0:T(8,128)(2,1)} %w_supply.3) | copy-start | bytes 393220
  37.3 2.8 %copy-start.14 = (s32[8,256,3,256]{3,1,2,0:T(8,128)S(1)}, s32[8,256,3,256]{3,1,2,0:T(8,128)}, u32[]{:S(2)}) copy-start(s32[8,256,3,256]{3,1,2,0:T(8,128)} %param.16) | copy-start | bytes 18874372
  40.1 10.2 %copy-start.2 = (bf16[256,256]{1,0:T(8,128)(2,1)S(1)}, bf16[256,256]{1,0:T(8,128)(2,1)}, u32[]{:S(2)}) copy-start(bf16[256,256]{1,0:T(8,128)(2,1)} %w_key.3) | copy-start | bytes 393220
  40.1 10.2 %copy-start.3 = (bf16[256,256]{1,0:T(8,128)(2,1)S(1)}, bf16[256,256]{1,0:T(8,128)(2,1)}, u32[]{:S(2)}) copy-start(bf16[256,256]{1,0:T(8,128)(2,1)} %w_value.3) | copy-start | bytes 393220
  40.1 10.2 %copy-start.7 = (bf16[256,256]{1,0:T(8,128)(2,1)S(1)}, bf16[256,256]{1,0:T(8,128)(2,1)}, u32[]{:S(2)}) copy-start(bf16[256,256]{1,0:T(8,128)(2,1)} %w_supply.3) | copy-start | bytes 393220
  40.1 10.2 %copy-start.8 = (bf16[256,256]{1,0:T(8,128)(2,1)S(1)}, bf16[256,256]{1,0:T(8,128)(2,1)}, u32[]{:S(2)}) copy-start(bf16[256,256]{1,0:T(8,128)(2,1)} %w_query.1) | copy-start | bytes 393220
  40.1 10.2 %copy-start.9 = (bf16[256,256]{1,0:T(8,128)(2,1)S(1)}, bf16[256,256]{1,0:T(8,128)(2,1)}, u32[]{:S(2)}) copy-start(bf16[256,256]{1,0:T(8,128)(2,1)} %join.3.rest_0_) | copy-start | bytes 393220
  40.1 10.2 %copy-start.11 = (s32[8,256]{1,0:T(8,128)S(1)}, s32[8,256]{1,0:T(8,128)}, u32[]{:S(2)}) copy-start(s32[8,256]{1,0:T(8,128)} %banks.1) | copy-start | bytes 24580
  40.2 10.2 %copy-start.12 = (s32[8,256]{1,0:T(8,128)S(1)}, s32[8,256]{1,0:T(8,128)}, u32[]{:S(2)}) copy-start(s32[8,256]{1,0:T(8,128)} %sectors.1) | copy-start | bytes 24580
  40.2 10.2 %copy-start.13 = (f32[256]{0:T(256)S(1)}, f32[256]{0:T(256)}, u32[]{:S(2)}) copy-start(f32[256]{0:T(256)} %param.28) | copy-start | bytes 3076
  48.2 20.0 %collective-permute-start.13 = (bf16[3,256,256]{2,1,0:T(8,128)(2,1)S(1)}, bf16[3,256,256]{2,1,0:T(8,128)(2,1)S(1)}, u32[]{:S(2)}, u32[]{:S(2)}) collective-permute-start(bf16[3,256,256]{2,1,0:T(8,128)(2,1)S(1)} %slice.7), channel_id=1, source_target_pairs={{1,2},{3,4},{5,6},{7,8},{9,10},{11,12},{13,14},{15,16},{17,18},{19... | collective-permute-start | bytes 1179656 | tf_op jit(solution)/shard_map/ppermute | solution.py:234
  50.1 18.1 %collective-permute-start.12 = (bf16[3,256,256]{2,1,0:T(8,128)(2,1)S(1)}, bf16[3,256,256]{2,1,0:T(8,128)(2,1)S(1)}, u32[]{:S(2)}, u32[]{:S(2)}) collective-permute-start(bf16[3,256,256]{2,1,0:T(8,128)(2,1)S(1)} %slice.7), channel_id=1, source_target_pairs={{0,1},{1,0},{2,3},{3,2},{4,5},{5,4},{6,7},{7,6},{8,9},{9,8},{10,11... | collective-permute-start | bytes 1179656 | tf_op jit(solution)/shard_map/ppermute | solution.py:233
  50.4 6.6 %copy-start = (bf16[256,1024]{1,0:T(8,128)(2,1)S(1)}, bf16[256,1024]{1,0:T(8,128)(2,1)}, u32[]{:S(2)}) copy-start(bf16[256,1024]{1,0:T(8,128)(2,1)} %w_in.5) | copy-start | bytes 1572868
  50.4 6.6 %copy-start.1 = (bf16[1024,256]{1,0:T(8,128)(2,1)S(1)}, bf16[1024,256]{1,0:T(8,128)(2,1)}, u32[]{:S(2)}) copy-start(bf16[1024,256]{1,0:T(8,128)(2,1)} %w_down.5) | copy-start | bytes 1572868
  50.4 6.6 %copy-start.4 = (bf16[256,256]{1,0:T(8,128)(2,1)S(1)}, bf16[256,256]{1,0:T(8,128)(2,1)}, u32[]{:S(2)}) copy-start(bf16[256,256]{1,0:T(8,128)(2,1)} %w_out.5) | copy-start | bytes 393220
  50.4 6.6 %copy-start.10 = (f32[256]{0:T(256)S(1)}, f32[256]{0:T(256)}, u32[]{:S(2)}) copy-start(f32[256]{0:T(256)} %param.29) | copy-start | bytes 3076
  54.8 17.9 %collective-permute-start.11 = (bf16[3,256,256]{2,1,0:T(8,128)(2,1)S(1)}, bf16[3,256,256]{2,1,0:T(8,128)(2,1)S(1)}, u32[]{:S(2)}, u32[]{:S(2)}) collective-permute-start(bf16[3,256,256]{2,1,0:T(8,128)(2,1)S(1)} %get-tuple-element.31), channel_id=1, source_target_pairs={{0,64},{64,128},{128,192},{1,65},{65,129},{129,193},{2,66},{66,130... | collective-permute-start | bytes 1179656 | tf_op jit(solution)/shard_map/ppermute | solution.py:280
  (4 other events, 2.4 us)

commit v5 on v4

--- a/solution.py
+++ b/solution.py
@@ -84,8 +84,12 @@
     return base + spread * message
 
 
+def slot(apart):
+    return apart ^ ((apart & 21) << 1)
+
+
 def late_kernel(
-    where, base, tiles, scale, even_rows, odd_rows, banks, sectors, *rest,
+    where, base, tiles, scale, odd_rows, even_rows, banks, sectors, *rest,
 ):
     tables, (w_supply, w_query, w_key, w_value, gain_mix) = rest[:4], rest[4:9]
     early_base, mixed_out, normed_out, query_out, key_out, value_out = rest[9:]
@@ -95,8 +99,8 @@
     normed = []
     for m in list(range(EARLY, EARLY + LATE)) + list(range(EARLY)):
         bank, sector = banks[m : m + 1], sectors[m : m + 1]
-        bank = (lax.shift_right_logical(bank, 3) ^ me) * SLOT + (bank & 7)
-        sector = (lax.shift_right_logical(sector, 2) ^ me) * SLOT + 8 + (sector & 3)
+        bank = slot(lax.shift_right_logical(bank, 3) ^ me) * SLOT + (bank & 7)
+        sector = slot(lax.shift_right_logical(sector, 2) ^ me) * SLOT + 8 + (sector & 3)
         total = base[m]
         for i, table in enumerate(tables):
             chosen = jnp.where((row == bank - i * rows_each) | (row == sector - i * rows_each), 1.0, 0.0)
@@ -148,45 +152,35 @@
 
 
 def early_kernel(
-    base, tiles, scale, even_rows, odd_rows, late_mixed, late_query, late_key, late_value,
+    earlier, base, tiles, scale, odd_rows, even_rows, late_mixed, late_query, late_key, late_value,
     w_supply, w_query, w_key, w_value, gain_mix, w_out, w_in, w_down, gain_ffn, started,
-    result, mixed_out, query_out, key_out, value_out, buffer, sems,
+    result, buffer, sems,
 ):
     del started
-    firms = base.shape[1]
+    firms, width = base.shape[1:]
+    heads = head_matrix(width)
+    cut = lambda rows: [rows[i * firms : (i + 1) * firms] for i in range(rows.shape[0] // firms)]
     mixed, normed = [], []
     for m in range(EARLY):
         mixed.append(mix(m, base[m], tiles, scale, even_rows[m], odd_rows[m], w_supply[...]))
         normed.append(rms_norm(mixed[-1], gain_mix[...]).astype(BF))
-    rows = stack(normed)
-    cut = lambda rows: [rows[i * firms : (i + 1) * firms] for i in range(EARLY)]
-    query = cut(mm(rows, w_query[...]).astype(BF))
-    key = cut(mm(rows, w_key[...]).astype(BF))
-    value = cut(mm(rows, w_value[...]).astype(BF))
-    for m in range(LAGS):
-        mixed_out[m], query_out[m], key_out[m], value_out[m] = mixed[m], query[m], key[m], value[m]
-    keys = lagged(key + [late_key[m] for m in range(LAGS)], EARLY)
-    values = lagged(value + [late_value[m] for m in range(LAGS)], EARLY)
-    queries = stack(query[LAGS:] + [late_query[m] for m in range(LAGS)])
-    attended = attend(queries, keys, values, head_matrix(base.shape[-1]))
-    total = stack(mixed[LAGS:] + [late_mixed[m] for m in range(LAGS)])
-    final = finish(total, attended, w_out[...], w_in[...], w_down[...], gain_ffn[...])
-    write_back(final, buffer, result, sems, LAGS)
-
-
-def first_kernel(
-    earlier, mixed, query, key, value, w_key, w_value, w_out, w_in, w_down, gain_ffn, started, result, buffer, sems,
-):
-    del started
-    firms, width = mixed.shape[1:]
-    rows = earlier[...].reshape(LAGS * firms, width)
-    cut = lambda rows: [rows[i * firms : (i + 1) * firms] for i in range(LAGS)]
-    keys = lagged(cut(mm(rows, w_key[...]).astype(BF)) + [key[m] for m in range(LAGS)], LAGS)
-    values = lagged(cut(mm(rows, w_value[...]).astype(BF)) + [value[m] for m in range(LAGS)], LAGS)
-    flat = (LAGS * firms, width)
-    attended = attend(query[...].reshape(flat), keys, values, head_matrix(width))
-    final = finish(mixed[...].reshape(flat), attended, w_out[...], w_in[...], w_down[...], gain_ffn[...])
-    write_back(final, buffer, result, sems, 0)
+    query = cut(mm(stack(normed), w_query[...]).astype(BF)) + [late_query[m] for m in range(LAGS)]
+    rows = stack([earlier[...].reshape(LAGS * firms, width)] + normed)
+    key = cut(mm(rows, w_key[...]).astype(BF)) + [late_key[m] for m in range(LAGS)]
+    value = cut(mm(rows, w_value[...]).astype(BF)) + [late_value[m] for m in range(LAGS)]
+    mixed = mixed + [late_mixed[m] for m in range(LAGS)]
+    copies = []
+    for first in range(0, EARLY + LAGS, LAGS):
+        months = slice(first, first + LAGS)
+        keys = lagged(key[first : first + 2 * LAGS], LAGS)
+        values = lagged(value[first : first + 2 * LAGS], LAGS)
+        attended = attend(stack(query[months]), keys, values, heads)
+        final = finish(stack(mixed[months]), attended, w_out[...], w_in[...], w_down[...], gain_ffn[...])
+        buffer[months] = final.reshape(LAGS, firms, width)
+        copies.append(pltpu.make_async_copy(buffer.at[months], result.at[months], sems.at[first // LAGS]))
+        copies[-1].start()
+    for copy in copies:
+        copy.wait()
 
 
 def body(
@@ -207,7 +201,7 @@
 
     spare = SLOT - bank_table.shape[0] - sector_table.shape[0]
     hub = jnp.concatenate([bank_table, sector_table, jnp.zeros((spare, width), BF)], axis=0)
-    near = [hub] + [swap(hub, i) for i in (1, 2, 3)]
+    near = [hub] + [swap(hub, i) for i in (3, 2, 1)]
     late = features[EARLY:]
     late_even = lax.ppermute(late, "firm", even_pairs)
     late_odd = lax.ppermute(late, "firm", odd_pairs)
@@ -225,8 +219,8 @@
 
     def spread(near):
         hub = joined(near)
-        hub = joined([hub] + [swap(hub, i) for i in (4, 8, 12)])
-        return [hub] + [swap(hub, i) for i in (16, 32, 48)]
+        hub = joined([hub] + [swap(hub, i) for i in (12, 8, 4)])
+        return [hub] + [swap(hub, i) for i in (48, 32, 16)]
 
     tables = spread(near)
     tables, early = lax.optimization_barrier((tables, features[:EARLY]))
@@ -273,7 +267,7 @@
         cost_estimate=cost(1, 1),
         name="late_months",
     )(
-        where, base, tiles, scale, late_even, late_odd, bank_ids, sector_ids, *tables,
+        where, base, tiles, scale, late_odd, late_even, bank_ids, sector_ids, *tables,
         w_supply, w_query, w_key, w_value, gain_mix,
     )
 
@@ -294,32 +288,20 @@
         name="last_month",
     )(late_mixed, late_query, late_key, late_value, *end_weights)
 
-    result, mixed, query, key, value = pl.pallas_call(
+    return pl.pallas_call(
         early_kernel,
-        in_specs=[VM] * 18 + [ANY],
-        out_specs=[ANY] + [VM] * 4,
-        out_shape=[like(months, BF), like(LAGS, F32), like(LAGS, BF), like(LAGS, BF), like(LAGS, BF)],
-        scratch_shapes=scratch(EARLY),
-        input_output_aliases={18: 0},
+        in_specs=[VM] * 19 + [ANY],
+        out_specs=ANY,
+        out_shape=like(months, BF),
+        scratch_shapes=[pltpu.VMEM((EARLY + LAGS, firms, width), BF), pltpu.SemaphoreType.DMA((2,))],
+        input_output_aliases={19: 0},
         compiler_params=params,
         cost_estimate=cost(1, 1),
         name="early_months",
     )(
-        early_base, tiles, scale, early_even, early_odd, late_mixed, late_query, late_key, late_value,
+        earlier, early_base, tiles, scale, early_odd, early_even, late_mixed, late_query, late_key, late_value,
         w_supply, w_query, w_key, w_value, gain_mix, *end_weights, result,
     )
-
-    return pl.pallas_call(
-        first_kernel,
-        in_specs=[VM] * 11 + [ANY],
-        out_specs=ANY,
-        out_shape=like(months, BF),
-        scratch_shapes=scratch(LAGS),
-        input_output_aliases={11: 0},
-        compiler_params=params,
-        cost_estimate=cost(1, 1),
-        name="first_months",
-    )(earlier, mixed, query, key, value, w_key, w_value, *end_weights, result)
 
 
 def solution(mesh):

time: 77 us -> 75.9 us (0.986)
  the two profiles are of different devices: /device:TPU:40 before, /device:TPU:24 now
where the time goes in v5:
time: 75.9 us; the launch traced here: 75.4 us
  starting transfers between devices  29.2 us (38%)
  Pallas kernels  19.4 us (26%)
  waiting for transfers between devices  17 us (22%)
  local copies, waits for them, and re-layouts  8.57 us (11%)
  other arithmetic  0.85 us (1%)
    ppermute x9, starting transfers between devices, swap(): return lax.ppermute(x, 'firm', [(i, i ^ bits) for i in range(devices)])  17 us
    ppermute x1, starting transfers between devices, body(): late_odd = lax.ppermute(late, 'firm', odd_pairs)  8.32 us
    ppermute x1, waiting for transfers between devices, body(): early_odd = lax.ppermute(early, 'firm', odd_pairs)  7.36 us
    unnamed x44, local copies, waits for them, and re-layouts  7.34 us
    pallas_call x1, Pallas kernels, body(): pl.pallas_call(early_kernel, in_specs=[VM] * 19 + [ANY], out_specs=ANY, o...  6.78 us
    ppermute x9, waiting for transfers between devices, swap(): return lax.ppermute(x, 'firm', [(i, i ^ bits) for i in range(devices)])  4.75 us
    ppermute x1, waiting for transfers between devices, body(): late_even = lax.ppermute(late, 'firm', even_pairs)  4.55 us
    pallas_call x1, Pallas kernels, body(): pl.pallas_call(late_kernel, in_specs=[SM] + [VM] * 16, out_specs=[VM] * 6...  4.4 us
  transfers between devices with their start and end apart: 14, of which 5 were waited for; matrix products, arithmetic and copies ran while one was open for 2% of the time, Pallas kernels for 17%

profile of v5, /device:TPU:24, one launch (start us, length us, event | category | flops | bytes accessed | tf_op | source)
XLA Modules:
  0.0 75.4 jit_solution(10301321442947745774)
XLA Ops:
  0.1 0.8 %maximum_maximum_fusion.refs_0_ = bf16[16,256]{1,0:T(8,128)(2,1)S(1)} fusion(bf16[4,256]{1,0:T(4,128)(2,1)} %param.20, bf16[8,256]{1,0:T(8,128)(2,1)} %param.19, bf16[16]{0:T(256)(128)(2,1)S(1)} %pad.2.clone), kind=kLoop, calls=%fused_computation | loop fusion | flops 24576 | bytes 14368 | tf_op jit(solution)/shard_map/concatenate | solution.py:203
  0.9 6.3 %collective-permute-start.2 = (bf16[16,256]{1,0:T(8,128)(2,1)S(1)}, bf16[16,256]{1,0:T(8,128)(2,1)S(1)}, u32[]{:S(2)}, u32[]{:S(2)}) collective-permute-start(bf16[16,256]{1,0:T(8,128)(2,1)S(1)} %maximum_maximum_fusion.refs_0_), channel_id=1, source_target_pairs={{0,3},{1,2},{2,1},{3,0},{4,7},{5,6},{6,5},{7,4},{8,11},{9,10},{10,... | collective-permute-start | bytes 24584 | tf_op jit(solution)/shard_map/ppermute | solution.py:200
  7.2 1.0 %collective-permute-start.3 = (bf16[16,256]{1,0:T(8,128)(2,1)S(1)}, bf16[16,256]{1,0:T(8,128)(2,1)S(1)}, u32[]{:S(2)}, u32[]{:S(2)}) collective-permute-start(bf16[16,256]{1,0:T(8,128)(2,1)S(1)} %maximum_maximum_fusion.refs_0_), channel_id=1, source_target_pairs={{0,2},{1,3},{2,0},{3,1},{4,6},{5,7},{6,4},{7,5},{8,10},{9,11},{10,... | collective-permute-start | bytes 24584 | tf_op jit(solution)/shard_map/ppermute | solution.py:200
  8.2 1.5 %collective-permute-start.4 = (bf16[16,256]{1,0:T(8,128)(2,1)S(1)}, bf16[16,256]{1,0:T(8,128)(2,1)S(1)}, u32[]{:S(2)}, u32[]{:S(2)}) collective-permute-start(bf16[16,256]{1,0:T(8,128)(2,1)S(1)} %maximum_maximum_fusion.refs_0_), channel_id=1, source_target_pairs={{0,1},{1,0},{2,3},{3,2},{4,5},{5,4},{6,7},{7,6},{8,9},{9,8},{10,11... | collective-permute-start | bytes 24584 | tf_op jit(solution)/shard_map/ppermute | solution.py:200
  9.7 1.1 %slice.6 = bf16[5,256,256]{2,1,0:T(8,128)(2,1)S(1)} slice(bf16[8,256,256]{2,1,0:T(8,128)(2,1)} %own.1), slice={[3:8], [0:256], [0:256]} | slice | bytes 1310720 | tf_op jit(solution)/shard_map/slice | solution.py:205
  10.8 8.3 %collective-permute-start = (bf16[5,256,256]{2,1,0:T(8,128)(2,1)S(1)}, bf16[5,256,256]{2,1,0:T(8,128)(2,1)S(1)}, u32[]{:S(2)}, u32[]{:S(2)}) collective-permute-start(bf16[5,256,256]{2,1,0:T(8,128)(2,1)S(1)} %slice.6), channel_id=1, source_target_pairs={{1,2},{3,4},{5,6},{7,8},{9,10},{11,12},{13,14},{15,16},{17,18},{19... | collective-permute-start | bytes 1966088 | tf_op jit(solution)/shard_map/ppermute | solution.py:207
  19.3 0.5 copy-done.19
  19.8 0.6 copy-done.21
  20.4 1.4 %join.2.refs_0_ = bf16[64,256]{1,0:T(8,128)(2,1)} custom-call(bf16[16,256]{1,0:T(8,128)(2,1)} %copy-done.15, bf16[16,256]{1,0:T(8,128)(2,1)} %copy-done.19, bf16[16,256]{1,0:T(8,128)(2,1)} %copy-done.20, bf16[16,256]{1,0:T(8,128)(2,1)} %copy-done.21), custom_call_target="tpu_custom_call" | custom-call | bytes 1024 | tf_op jit(solution)/shard_map/join/pallas_call | solution.py:211
  21.8 1.8 %collective-permute-start.5 = (bf16[64,256]{1,0:T(8,128)(2,1)}, bf16[64,256]{1,0:T(8,128)(2,1)S(1)}, u32[]{:S(2)}, u32[]{:S(2)}) collective-permute-start(bf16[64,256]{1,0:T(8,128)(2,1)} %join.2.refs_0_), channel_id=1, source_target_pairs={{0,12},{1,13},{2,14},{3,15},{4,8},{5,9},{6,10},{7,11},{8,4},{9,5},... | collective-permute-start | bytes 98312 | tf_op jit(solution)/shard_map/ppermute | solution.py:200
  23.6 0.8 %collective-permute-start.6 = (bf16[64,256]{1,0:T(8,128)(2,1)}, bf16[64,256]{1,0:T(8,128)(2,1)S(1)}, u32[]{:S(2)}, u32[]{:S(2)}) collective-permute-start(bf16[64,256]{1,0:T(8,128)(2,1)} %join.2.refs_0_), channel_id=1, source_target_pairs={{0,8},{1,9},{2,10},{3,11},{4,12},{5,13},{6,14},{7,15},{8,0},{9,1},... | collective-permute-start | bytes 98312 | tf_op jit(solution)/shard_map/ppermute | solution.py:200
  24.4 1.5 %collective-permute-start.7 = (bf16[64,256]{1,0:T(8,128)(2,1)}, bf16[64,256]{1,0:T(8,128)(2,1)S(1)}, u32[]{:S(2)}, u32[]{:S(2)}) collective-permute-start(bf16[64,256]{1,0:T(8,128)(2,1)} %join.2.refs_0_), channel_id=1, source_target_pairs={{0,4},{1,5},{2,6},{3,7},{4,0},{5,1},{6,2},{7,3},{8,12},{9,13},{10,... | collective-permute-start | bytes 98312 | tf_op jit(solution)/shard_map/ppermute | solution.py:200
  26.0 1.4 %collective-permute-done.5.refs_1_ = bf16[64,256]{1,0:T(8,128)(2,1)S(1)} collective-permute-done((bf16[64,256]{1,0:T(8,128)(2,1)}, bf16[64,256]{1,0:T(8,128)(2,1)S(1)}, u32[]{:S(2)}, u32[]{:S(2)}) %collective-permute-start.5) | collective-permute-done | bytes 32800 | tf_op jit(solution)/shard_map/ppermute | solution.py:200
  27.4 3.3 %collective-permute-done.6.refs_2_ = bf16[64,256]{1,0:T(8,128)(2,1)S(1)} collective-permute-done((bf16[64,256]{1,0:T(8,128)(2,1)}, bf16[64,256]{1,0:T(8,128)(2,1)S(1)}, u32[]{:S(2)}, u32[]{:S(2)}) %collective-permute-start.6) | collective-permute-done | bytes 32800 | tf_op jit(solution)/shard_map/ppermute | solution.py:200
  30.7 0.6 copy-done.17
  31.3 0.6 copy-done.18
  31.9 1.5 %join.3.rest_0_ = bf16[256,256]{1,0:T(8,128)(2,1)} custom-call(bf16[64,256]{1,0:T(8,128)(2,1)} %join.2.refs_0_, bf16[64,256]{1,0:T(8,128)(2,1)} %copy-done.16, bf16[64,256]{1,0:T(8,128)(2,1)} %copy-done.17, bf16[64,256]{1,0:T(8,128)(2,1)} %copy-done.18), custom_call_target="tpu_custom_call" | custom-call | bytes 1024 | tf_op jit(solution)/shard_map/join/pallas_call | solution.py:211
  33.4 1.0 %collective-permute-start.10 = (bf16[256,256]{1,0:T(8,128)(2,1)}, bf16[256,256]{1,0:T(8,128)(2,1)S(1)}, u32[]{:S(2)}, u32[]{:S(2)}) collective-permute-start(bf16[256,256]{1,0:T(8,128)(2,1)} %join.3.rest_0_), channel_id=1, source_target_pairs={{0,16},{1,17},{2,18},{3,19},{4,20},{5,21},{6,22},{7,23},{8,24},{9,... | collective-permute-start | bytes 393224 | tf_op jit(solution)/shard_map/ppermute | solution.py:200
  34.3 1.1 %collective-permute-start.8 = (bf16[256,256]{1,0:T(8,128)(2,1)}, bf16[256,256]{1,0:T(8,128)(2,1)S(1)}, u32[]{:S(2)}, u32[]{:S(2)}) collective-permute-start(bf16[256,256]{1,0:T(8,128)(2,1)} %join.3.rest_0_), channel_id=1, source_target_pairs={{0,48},{1,49},{2,50},{3,51},{4,52},{5,53},{6,54},{7,55},{8,56},{9,... | collective-permute-start | bytes 393224 | tf_op jit(solution)/shard_map/ppermute | solution.py:200
  35.4 2.1 %collective-permute-start.9 = (bf16[256,256]{1,0:T(8,128)(2,1)}, bf16[256,256]{1,0:T(8,128)(2,1)S(1)}, u32[]{:S(2)}, u32[]{:S(2)}) collective-permute-start(bf16[256,256]{1,0:T(8,128)(2,1)} %join.3.rest_0_), channel_id=1, source_target_pairs={{0,32},{1,33},{2,34},{3,35},{4,36},{5,37},{6,38},{7,39},{8,40},{9,... | collective-permute-start | bytes 393224 | tf_op jit(solution)/shard_map/ppermute | solution.py:200
  37.5 1.2 %copy-done.2 = bf16[8,256,256]{2,1,0:T(8,128)(2,1)S(1)} copy-done((bf16[8,256,256]{2,1,0:T(8,128)(2,1)S(1)}, bf16[8,256,256]{2,1,0:T(8,128)(2,1)}, u32[]{:S(2)}) %copy-start.2) | copy-done | bytes 1048600
  38.7 0.9 %copy-done.3 = bf16[256,256]{1,0:T(8,128)(2,1)S(1)} copy-done((bf16[256,256]{1,0:T(8,128)(2,1)S(1)}, bf16[256,256]{1,0:T(8,128)(2,1)}, u32[]{:S(2)}) %copy-start.3) | copy-done | bytes 131096
  39.6 2.8 %copy-done.14 = s32[8,256,3,256]{3,1,2,0:T(8,128)S(1)} copy-done((s32[8,256,3,256]{3,1,2,0:T(8,128)S(1)}, s32[8,256,3,256]{3,1,2,0:T(8,128)}, u32[]{:S(2)}) %copy-start.14) | copy-done | bytes 6291480
  42.4 2.7 %own_block.1 = (f32[8,256,256]{2,1,0:T(8,128)S(1)}, bf16[8,2,256,256]{3,2,1,0:T(8,128)(2,1)S(1)}, f32[8,256,128]{2,1,0:T(8,128)S(1)}) custom-call(s32[2]{0:T(128)S(1)} %pad_add_fusion.where, s32[8,3,256,256]{3,2,1,0:T(8,128)S(1)} %bitcast.9, bf16[8,256,256]{2,1,0:T(8,128)(2,1)S(1)} %copy-done.2, bf16[256,256]{1,0:T(8,128)(2,1)S(1)} %copy-done.3), custom_call_target="tpu_custom_call" | custom-call | flops 6710886400 | bytes 16777216 | tf_op jit(solution)/shard_map/own_block/pallas_call | solution.py:244
  45.2 1.9 %collective-permute-start.12 = (bf16[3,256,256]{2,1,0:T(8,128)(2,1)S(1)}, bf16[3,256,256]{2,1,0:T(8,128)(2,1)S(1)}, u32[]{:S(2)}, u32[]{:S(2)}) collective-permute-start(bf16[3,256,256]{2,1,0:T(8,128)(2,1)S(1)} %slice.7), channel_id=1, source_target_pairs={{1,2},{3,4},{5,6},{7,8},{9,10},{11,12},{13,14},{15,16},{17,18},{19... | collective-permute-start | bytes 1179656 | tf_op jit(solution)/shard_map/ppermute | solution.py:228
  47.1 0.4 collective-permute-start.13
  47.7 4.6 %collective-permute-done.1.even_rows = bf16[5,256,256]{2,1,0:T(8,128)(2,1)S(1)} collective-permute-done((bf16[5,256,256]{2,1,0:T(8,128)(2,1)S(1)}, bf16[5,256,256]{2,1,0:T(8,128)(2,1)S(1)}, u32[]{:S(2)}, u32[]{:S(2)}) %collective-permute-start.1) | collective-permute-done | bytes 655392 | tf_op jit(solution)/shard_map/ppermute | solution.py:206
  52.4 4.4 %late_months.1 = (f32[3,256,256]{2,1,0:T(8,128)S(1)}, f32[5,256,256]{2,1,0:T(8,128)S(1)}, bf16[3,256,256]{2,1,0:T(8,128)(2,1)S(1)}, bf16[5,256,256]{2,1,0:T(8,12...) custom-call(s32[2]{0:T(128)S(1)} %pad_add_fusion.where, ...), custom_call_target="tpu_custom_call" | custom-call | flops 33554432 | bytes 1024 | tf_op jit(solution)/shard_map/late_months/pallas_call | solution.py:259
  56.8 1.5 %collective-permute-start.11 = (bf16[3,256,256]{2,1,0:T(8,128)(2,1)S(1)}, bf16[3,256,256]{2,1,0:T(8,128)(2,1)S(1)}, u32[]{:S(2)}, u32[]{:S(2)}) collective-permute-start(bf16[3,256,256]{2,1,0:T(8,128)(2,1)S(1)} %get-tuple-element.26), channel_id=1, source_target_pairs={{0,64},{64,128},{128,192},{1,65},{65,129},{129,193},{2,66},{66,130... | collective-permute-start | bytes 1179656 | tf_op jit(solution)/shard_map/ppermute | solution.py:274
  58.4 2.8 %last_month.1.started = bf16[8,256,256]{2,1,0:T(8,128)(2,1)} custom-call(f32[5,256,256]{2,1,0:T(8,128)S(1)} %get-tuple-element.29.mixed.late_mixed, bf16[5,256,256]{2,1,0:T(8,128)(2,1)S(1)} %get-tuple-element.30.query.late_query, bf16[5,256,256]{2,1,0:T(8,128)(2,1)S(1)} %get-tuple-element.31.key.late_key, ...), custom_call_target="tpu_custom_call" | custom-call | flops 33554432 | bytes 1024 | tf_op jit(solution)/shard_map/last_month/pallas_call | solution.py:280
  61.1 7.4 %collective-permute-done.12.odd_rows = bf16[3,256,256]{2,1,0:T(8,128)(2,1)S(1)} collective-permute-done((bf16[3,256,256]{2,1,0:T(8,128)(2,1)S(1)}, bf16[3,256,256]{2,1,0:T(8,128)(2,1)S(1)}, u32[]{:S(2)}, u32[]{:S(2)}) %collective-permute-start.12) | collective-permute-done | bytes 393248 | tf_op jit(solution)/shard_map/ppermute | solution.py:228
  68.5 6.8 %early_months.1 = bf16[8,256,256]{2,1,0:T(8,128)(2,1)} custom-call(bf16[3,256,256]{2,1,0:T(8,128)(2,1)S(1)} %collective-permute-done.11.earlier, f32[3,256,256]{2,1,0:T(8,128)S(1)} %get-tuple-element.27.base, bf16[8,2,256,256]{3,2,1,0:T(8,128)(2,1)S(1)} %get-tuple-element.20.tiles, ...), custom_call_target="tpu_custom_call", output_to_operand_aliasing={{}: (19, {})} | custom-call | flops 33554432 | bytes 1024 | tf_op jit(solution)/shard_map/early_months/pallas_call | solution.py:291
  (52 shorter events, 0.7 us)
Async XLA Ops:
  0.9 18.4 %copy-start.15 = (bf16[16,256]{1,0:T(8,128)(2,1)}, bf16[16,256]{1,0:T(8,128)(2,1)S(1)}, u32[]{:S(2)}) copy-start(bf16[16,256]{1,0:T(8,128)(2,1)S(1)} %maximum_maximum_fusion.refs_0_) | copy-start | bytes 24580
  0.9 18.4 %collective-permute-start.2 = (bf16[16,256]{1,0:T(8,128)(2,1)S(1)}, bf16[16,256]{1,0:T(8,128)(2,1)S(1)}, u32[]{:S(2)}, u32[]{:S(2)}) collective-permute-start(bf16[16,256]{1,0:T(8,128)(2,1)S(1)} %maximum_maximum_fusion.refs_0_), channel_id=1, source_target_pairs={{0,3},{1,2},{2,1},{3,0},{4,7},{5,6},{6,5},{7,4},{8,11},{9,10},{10,... | collective-permute-start | bytes 24584 | tf_op jit(solution)/shard_map/ppermute | solution.py:200
  7.2 12.0 %collective-permute-start.3 = (bf16[16,256]{1,0:T(8,128)(2,1)S(1)}, bf16[16,256]{1,0:T(8,128)(2,1)S(1)}, u32[]{:S(2)}, u32[]{:S(2)}) collective-permute-start(bf16[16,256]{1,0:T(8,128)(2,1)S(1)} %maximum_maximum_fusion.refs_0_), channel_id=1, source_target_pairs={{0,2},{1,3},{2,0},{3,1},{4,6},{5,7},{6,4},{7,5},{8,10},{9,11},{10,... | collective-permute-start | bytes 24584 | tf_op jit(solution)/shard_map/ppermute | solution.py:200
  8.2 11.1 %collective-permute-start.4 = (bf16[16,256]{1,0:T(8,128)(2,1)S(1)}, bf16[16,256]{1,0:T(8,128)(2,1)S(1)}, u32[]{:S(2)}, u32[]{:S(2)}) collective-permute-start(bf16[16,256]{1,0:T(8,128)(2,1)S(1)} %maximum_maximum_fusion.refs_0_), channel_id=1, source_target_pairs={{0,1},{1,0},{2,3},{3,2},{4,5},{5,4},{6,7},{7,6},{8,9},{9,8},{10,11... | collective-permute-start | bytes 24584 | tf_op jit(solution)/shard_map/ppermute | solution.py:200
  10.8 37.0 %collective-permute-start = (bf16[5,256,256]{2,1,0:T(8,128)(2,1)S(1)}, bf16[5,256,256]{2,1,0:T(8,128)(2,1)S(1)}, u32[]{:S(2)}, u32[]{:S(2)}) collective-permute-start(bf16[5,256,256]{2,1,0:T(8,128)(2,1)S(1)} %slice.6), channel_id=1, source_target_pairs={{1,2},{3,4},{5,6},{7,8},{9,10},{11,12},{13,14},{15,16},{17,18},{19... | collective-permute-start | bytes 1966088 | tf_op jit(solution)/shard_map/ppermute | solution.py:207
  19.1 33.2 %collective-permute-start.1 = (bf16[5,256,256]{2,1,0:T(8,128)(2,1)S(1)}, bf16[5,256,256]{2,1,0:T(8,128)(2,1)S(1)}, u32[]{:S(2)}, u32[]{:S(2)}) collective-permute-start(bf16[5,256,256]{2,1,0:T(8,128)(2,1)S(1)} %slice.6), channel_id=1, source_target_pairs={{0,1},{1,0},{2,3},{3,2},{4,5},{5,4},{6,7},{7,6},{8,9},{9,8},{10,11... | collective-permute-start | bytes 1966088 | tf_op jit(solution)/shard_map/ppermute | solution.py:206
  21.8 5.6 %collective-permute-start.5 = (bf16[64,256]{1,0:T(8,128)(2,1)}, bf16[64,256]{1,0:T(8,128)(2,1)S(1)}, u32[]{:S(2)}, u32[]{:S(2)}) collective-permute-start(bf16[64,256]{1,0:T(8,128)(2,1)} %join.2.refs_0_), channel_id=1, source_target_pairs={{0,12},{1,13},{2,14},{3,15},{4,8},{5,9},{6,10},{7,11},{8,4},{9,5},... | collective-permute-start | bytes 98312 | tf_op jit(solution)/shard_map/ppermute | solution.py:200
  23.6 7.1 %collective-permute-start.6 = (bf16[64,256]{1,0:T(8,128)(2,1)}, bf16[64,256]{1,0:T(8,128)(2,1)S(1)}, u32[]{:S(2)}, u32[]{:S(2)}) collective-permute-start(bf16[64,256]{1,0:T(8,128)(2,1)} %join.2.refs_0_), channel_id=1, source_target_pairs={{0,8},{1,9},{2,10},{3,11},{4,12},{5,13},{6,14},{7,15},{8,0},{9,1},... | collective-permute-start | bytes 98312 | tf_op jit(solution)/shard_map/ppermute | solution.py:200
  24.4 6.3 %collective-permute-start.7 = (bf16[64,256]{1,0:T(8,128)(2,1)}, bf16[64,256]{1,0:T(8,128)(2,1)S(1)}, u32[]{:S(2)}, u32[]{:S(2)}) collective-permute-start(bf16[64,256]{1,0:T(8,128)(2,1)} %join.2.refs_0_), channel_id=1, source_target_pairs={{0,4},{1,5},{2,6},{3,7},{4,0},{5,1},{6,2},{7,3},{8,12},{9,13},{10,... | collective-permute-start | bytes 98312 | tf_op jit(solution)/shard_map/ppermute | solution.py:200
  27.4 3.3 %copy-start.16 = (bf16[64,256]{1,0:T(8,128)(2,1)}, bf16[64,256]{1,0:T(8,128)(2,1)S(1)}, u32[]{:S(2)}) copy-start(bf16[64,256]{1,0:T(8,128)(2,1)S(1)} %collective-permute-done.5.refs_1_) | copy-start | bytes 98308
  30.7 0.6 copy-start.17
  33.4 11.8 %collective-permute-start.10 = (bf16[256,256]{1,0:T(8,128)(2,1)}, bf16[256,256]{1,0:T(8,128)(2,1)S(1)}, u32[]{:S(2)}, u32[]{:S(2)}) collective-permute-start(bf16[256,256]{1,0:T(8,128)(2,1)} %join.3.rest_0_), channel_id=1, source_target_pairs={{0,16},{1,17},{2,18},{3,19},{4,20},{5,21},{6,22},{7,23},{8,24},{9,... | collective-permute-start | bytes 393224 | tf_op jit(solution)/shard_map/ppermute | solution.py:200
  34.3 10.8 %collective-permute-start.8 = (bf16[256,256]{1,0:T(8,128)(2,1)}, bf16[256,256]{1,0:T(8,128)(2,1)S(1)}, u32[]{:S(2)}, u32[]{:S(2)}) collective-permute-start(bf16[256,256]{1,0:T(8,128)(2,1)} %join.3.rest_0_), channel_id=1, source_target_pairs={{0,48},{1,49},{2,50},{3,51},{4,52},{5,53},{6,54},{7,55},{8,56},{9,... | collective-permute-start | bytes 393224 | tf_op jit(solution)/shard_map/ppermute | solution.py:200
  35.4 9.8 %collective-permute-start.9 = (bf16[256,256]{1,0:T(8,128)(2,1)}, bf16[256,256]{1,0:T(8,128)(2,1)S(1)}, u32[]{:S(2)}, u32[]{:S(2)}) collective-permute-start(bf16[256,256]{1,0:T(8,128)(2,1)} %join.3.rest_0_), channel_id=1, source_target_pairs={{0,32},{1,33},{2,34},{3,35},{4,36},{5,37},{6,38},{7,39},{8,40},{9,... | collective-permute-start | bytes 393224 | tf_op jit(solution)/shard_map/ppermute | solution.py:200
  37.5 1.2 %copy-start.2 = (bf16[8,256,256]{2,1,0:T(8,128)(2,1)S(1)}, bf16[8,256,256]{2,1,0:T(8,128)(2,1)}, u32[]{:S(2)}) copy-start(bf16[8,256,256]{2,1,0:T(8,128)(2,1)} %own.1) | copy-start | bytes 3145732
  38.7 0.9 %copy-start.3 = (bf16[256,256]{1,0:T(8,128)(2,1)S(1)}, bf16[256,256]{1,0:T(8,128)(2,1)}, u32[]{:S(2)}) copy-start(bf16[256,256]{1,0:T(8,128)(2,1)} %w_supply.3) | copy-start | bytes 393220
  39.6 2.8 %copy-start.14 = (s32[8,256,3,256]{3,1,2,0:T(8,128)S(1)}, s32[8,256,3,256]{3,1,2,0:T(8,128)}, u32[]{:S(2)}) copy-start(s32[8,256,3,256]{3,1,2,0:T(8,128)} %param.16) | copy-start | bytes 18874372
  42.4 9.9 %copy-start.4 = (bf16[256,256]{1,0:T(8,128)(2,1)S(1)}, bf16[256,256]{1,0:T(8,128)(2,1)}, u32[]{:S(2)}) copy-start(bf16[256,256]{1,0:T(8,128)(2,1)} %w_supply.3) | copy-start | bytes 393220
  42.4 9.9 %copy-start.5 = (bf16[256,256]{1,0:T(8,128)(2,1)S(1)}, bf16[256,256]{1,0:T(8,128)(2,1)}, u32[]{:S(2)}) copy-start(bf16[256,256]{1,0:T(8,128)(2,1)} %w_query.1) | copy-start | bytes 393220
  42.4 9.9 %copy-start.6 = (bf16[256,256]{1,0:T(8,128)(2,1)S(1)}, bf16[256,256]{1,0:T(8,128)(2,1)}, u32[]{:S(2)}) copy-start(bf16[256,256]{1,0:T(8,128)(2,1)} %w_key.1) | copy-start | bytes 393220
  42.4 9.9 %copy-start.7 = (bf16[256,256]{1,0:T(8,128)(2,1)S(1)}, bf16[256,256]{1,0:T(8,128)(2,1)}, u32[]{:S(2)}) copy-start(bf16[256,256]{1,0:T(8,128)(2,1)} %w_value.1) | copy-start | bytes 393220
  42.4 9.9 %copy-start.9 = (bf16[256,256]{1,0:T(8,128)(2,1)S(1)}, bf16[256,256]{1,0:T(8,128)(2,1)}, u32[]{:S(2)}) copy-start(bf16[256,256]{1,0:T(8,128)(2,1)} %join.3.rest_0_) | copy-start | bytes 393220
  42.4 9.9 %copy-start.10 = (s32[8,256]{1,0:T(8,128)S(1)}, s32[8,256]{1,0:T(8,128)}, u32[]{:S(2)}) copy-start(s32[8,256]{1,0:T(8,128)} %banks.1) | copy-start | bytes 24580
  42.4 9.9 %copy-start.11 = (s32[8,256]{1,0:T(8,128)S(1)}, s32[8,256]{1,0:T(8,128)}, u32[]{:S(2)}) copy-start(s32[8,256]{1,0:T(8,128)} %sectors.1) | copy-start | bytes 24580
  42.4 9.9 %copy-start.12 = (f32[256]{0:T(256)S(1)}, f32[256]{0:T(256)}, u32[]{:S(2)}) copy-start(f32[256]{0:T(256)} %param.28) | copy-start | bytes 3076
  45.2 23.3 %collective-permute-start.12 = (bf16[3,256,256]{2,1,0:T(8,128)(2,1)S(1)}, bf16[3,256,256]{2,1,0:T(8,128)(2,1)S(1)}, u32[]{:S(2)}, u32[]{:S(2)}) collective-permute-start(bf16[3,256,256]{2,1,0:T(8,128)(2,1)S(1)} %slice.7), channel_id=1, source_target_pairs={{1,2},{3,4},{5,6},{7,8},{9,10},{11,12},{13,14},{15,16},{17,18},{19... | collective-permute-start | bytes 1179656 | tf_op jit(solution)/shard_map/ppermute | solution.py:228
  47.1 21.4 %collective-permute-start.13 = (bf16[3,256,256]{2,1,0:T(8,128)(2,1)S(1)}, bf16[3,256,256]{2,1,0:T(8,128)(2,1)S(1)}, u32[]{:S(2)}, u32[]{:S(2)}) collective-permute-start(bf16[3,256,256]{2,1,0:T(8,128)(2,1)S(1)} %slice.7), channel_id=1, source_target_pairs={{0,1},{1,0},{2,3},{3,2},{4,5},{5,4},{6,7},{7,6},{8,9},{9,8},{10,11... | collective-permute-start | bytes 1179656 | tf_op jit(solution)/shard_map/ppermute | solution.py:227
  52.4 6.0 %copy-start = (bf16[256,1024]{1,0:T(8,128)(2,1)S(1)}, bf16[256,1024]{1,0:T(8,128)(2,1)}, u32[]{:S(2)}) copy-start(bf16[256,1024]{1,0:T(8,128)(2,1)} %w_in.3) | copy-start | bytes 1572868
  52.4 6.0 %copy-start.1 = (bf16[1024,256]{1,0:T(8,128)(2,1)S(1)}, bf16[1024,256]{1,0:T(8,128)(2,1)}, u32[]{:S(2)}) copy-start(bf16[1024,256]{1,0:T(8,128)(2,1)} %w_down.3) | copy-start | bytes 1572868
  52.4 6.0 %copy-start.8 = (bf16[256,256]{1,0:T(8,128)(2,1)S(1)}, bf16[256,256]{1,0:T(8,128)(2,1)}, u32[]{:S(2)}) copy-start(bf16[256,256]{1,0:T(8,128)(2,1)} %w_out.3) | copy-start | bytes 393220
  52.4 6.0 %copy-start.13 = (f32[256]{0:T(256)S(1)}, f32[256]{0:T(256)}, u32[]{:S(2)}) copy-start(f32[256]{0:T(256)} %param.29) | copy-start | bytes 3076
  56.8 11.7 %collective-permute-start.11 = (bf16[3,256,256]{2,1,0:T(8,128)(2,1)S(1)}, bf16[3,256,256]{2,1,0:T(8,128)(2,1)S(1)}, u32[]{:S(2)}, u32[]{:S(2)}) collective-permute-start(bf16[3,256,256]{2,1,0:T(8,128)(2,1)S(1)} %get-tuple-element.26), channel_id=1, source_target_pairs={{0,64},{64,128},{128,192},{1,65},{65,129},{129,193},{2,66},{66,130... | collective-permute-start | bytes 1179656 | tf_op jit(solution)/shard_map/ppermute | solution.py:274
  (4 other events, 2.4 us)

commit v6 on v5

--- a/solution.py
+++ b/solution.py
@@ -88,34 +88,36 @@
     return apart ^ ((apart & 21) << 1)
 
 
+def with_hubs(m, me, base, banks, sectors, tables):
+    rows_each, firms = tables[0].shape[0], base.shape[1]
+    row = lax.broadcasted_iota(jnp.int32, (rows_each, firms), 0)
+    bank, sector = banks[m : m + 1], sectors[m : m + 1]
+    bank = slot(lax.shift_right_logical(bank, 3) ^ me) * SLOT + (bank & 7)
+    sector = slot(lax.shift_right_logical(sector, 2) ^ me) * SLOT + 8 + (sector & 3)
+    total = base[m]
+    for i, table in enumerate(tables):
+        chosen = jnp.where((row == bank - i * rows_each) | (row == sector - i * rows_each), 1.0, 0.0)
+        total = total + lax.dot_general(
+            chosen.astype(BF), table[...], (((0,), (0,)), ((), ())), preferred_element_type=F32
+        )
+    return total
+
+
 def late_kernel(
     where, base, tiles, scale, odd_rows, even_rows, banks, sectors, *rest,
 ):
     tables, (w_supply, w_query, w_key, w_value, gain_mix) = rest[:4], rest[4:9]
-    early_base, mixed_out, normed_out, query_out, key_out, value_out = rest[9:]
-    me = where[0]
-    rows_each, firms = tables[0].shape[0], base.shape[1]
-    row = lax.broadcasted_iota(jnp.int32, (rows_each, firms), 0)
+    mixed_out, normed_out, query_out, key_out, value_out = rest[9:]
+    firms = base.shape[1]
     normed = []
-    for m in list(range(EARLY, EARLY + LATE)) + list(range(EARLY)):
-        bank, sector = banks[m : m + 1], sectors[m : m + 1]
-        bank = slot(lax.shift_right_logical(bank, 3) ^ me) * SLOT + (bank & 7)
-        sector = slot(lax.shift_right_logical(sector, 2) ^ me) * SLOT + 8 + (sector & 3)
-        total = base[m]
-        for i, table in enumerate(tables):
-            chosen = jnp.where((row == bank - i * rows_each) | (row == sector - i * rows_each), 1.0, 0.0)
-            total = total + lax.dot_general(
-                chosen.astype(BF), table[...], (((0,), (0,)), ((), ())), preferred_element_type=F32
-            )
-        if m < EARLY:
-            early_base[m] = total
-        else:
-            i = m - EARLY
-            mixed = mix(m, total, tiles, scale, even_rows[i], odd_rows[i], w_supply[...])
-            mixed_out[i] = mixed
-            normed.append(rms_norm(mixed, gain_mix[...]).astype(BF))
-            if i >= LATE - LAGS:
-                normed_out[i - LATE + LAGS] = normed[-1]
+    for i in range(LATE):
+        m = EARLY + i
+        total = with_hubs(m, where[0], base, banks, sectors, tables)
+        mixed = mix(m, total, tiles, scale, even_rows[i], odd_rows[i], w_supply[...])
+        mixed_out[i] = mixed
+        normed.append(rms_norm(mixed, gain_mix[...]).astype(BF))
+        if i >= LATE - LAGS:
+            normed_out[i - LATE + LAGS] = normed[-1]
     shape = query_out.shape
     rows = stack(normed)
     query_out[...] = mm(rows, w_query[...]).astype(BF).reshape(shape)
@@ -140,7 +142,13 @@
         copy.wait()
 
 
-def last_kernel(mixed, query, key, value, w_out, w_in, w_down, gain_ffn, result, buffer, sems):
+def last_kernel(
+    where, base, banks, sectors, *rest,
+):
+    tables, (mixed, query, key, value, w_out, w_in, w_down, gain_ffn) = rest[:4], rest[4:12]
+    result, early_base, buffer, sems = rest[12:]
+    for m in range(EARLY):
+        early_base[m] = with_hubs(m, where[0], base, banks, sectors, tables)
     count = LATE - LAGS
     firms, width = query.shape[1:]
     flat = (count * firms, width)
@@ -256,12 +264,12 @@
         name="own_block",
     )(where, counts, features, w_supply)
 
-    early_base, late_mixed, late_normed, late_query, late_key, late_value = pl.pallas_call(
+    late_mixed, late_normed, late_query, late_key, late_value = pl.pallas_call(
         late_kernel,
         in_specs=[SM] + [VM] * 16,
-        out_specs=[VM] * 6,
+        out_specs=[VM] * 5,
         out_shape=[
-            like(EARLY, F32), like(LATE, F32), like(LAGS, BF), like(LATE, BF), like(LATE, BF), like(LATE, BF),
+            like(LATE, F32), like(LAGS, BF), like(LATE, BF), like(LATE, BF), like(LATE, BF),
         ],
         compiler_params=params,
         cost_estimate=cost(1, 1),
@@ -277,16 +285,18 @@
     def scratch(count):
         return [pltpu.VMEM((count, firms, width), BF), pltpu.SemaphoreType.DMA((count,))]
 
-    result = pl.pallas_call(
+    result, early_base = pl.pallas_call(
         last_kernel,
-        in_specs=[VM] * 8,
-        out_specs=ANY,
-        out_shape=like(months, BF),
+        in_specs=[SM] + [VM] * 15,
+        out_specs=[ANY, VM],
+        out_shape=[like(months, BF), like(EARLY, F32)],
         scratch_shapes=scratch(LATE - LAGS),
         compiler_params=params,
         cost_estimate=cost(1, 1),
         name="last_month",
-    )(late_mixed, late_query, late_key, late_value, *end_weights)
+    )(
+        where, base, bank_ids, sector_ids, *tables, late_mixed, late_query, late_key, late_value, *end_weights,
+    )
 
     return pl.pallas_call(
         early_kernel,

time: 75.9 us -> 75.5 us (level)
  the two profiles are of different devices: /device:TPU:24 before, /device:TPU:25 now
where the time goes in v6:
time: 75.5 us; the launch traced here: 74.3 us
  starting transfers between devices  30.8 us (41%)
  Pallas kernels  19.8 us (26%)
  waiting for transfers between devices  13.8 us (18%)
  local copies, waits for them, and re-layouts  8.57 us (11%)
  other arithmetic  0.85 us (1%)
    ppermute x9, starting transfers between devices, swap(): return lax.ppermute(x, 'firm', [(i, i ^ bits) for i in range(devices)])  14.7 us
    ppermute x1, starting transfers between devices, body(): late_odd = lax.ppermute(late, 'firm', odd_pairs)  7.76 us
    unnamed x42, local copies, waits for them, and re-layouts  7.33 us
    pallas_call x1, Pallas kernels, body(): pl.pallas_call(early_kernel, in_specs=[VM] * 19 + [ANY], out_specs=ANY, o...  6.78 us
    ppermute x1, starting transfers between devices, body(): lax.ppermute(late_normed, 'tm', [(i, i + 1) for i in range(lax.axis_size(...  6.23 us
    ppermute x9, waiting for transfers between devices, swap(): return lax.ppermute(x, 'firm', [(i, i ^ bits) for i in range(devices)])  4.55 us
    ppermute x1, waiting for transfers between devices, body(): lax.ppermute(late_normed, 'tm', [(i, i + 1) for i in range(lax.axis_size(...  3.96 us
    pallas_call x1, Pallas kernels, body(): pl.pallas_call(last_kernel, in_specs=[SM] + [VM] * 15, out_specs=[ANY, VM...  3.89 us
  transfers between devices with their start and end apart: 14, of which 7 were waited for; matrix products, arithmetic and copies ran while one was open for 2% of the time, Pallas kernels for 18%

profile of v6, /device:TPU:25, one launch (start us, length us, event | category | flops | bytes accessed | tf_op | source)
XLA Modules:
  0.0 74.3 jit_solution(110476091154378605)
XLA Ops:
  0.1 0.8 %maximum_maximum_fusion.refs_0_ = bf16[16,256]{1,0:T(8,128)(2,1)S(1)} fusion(bf16[4,256]{1,0:T(4,128)(2,1)} %param.20, bf16[8,256]{1,0:T(8,128)(2,1)} %param.19, bf16[16]{0:T(256)(128)(2,1)S(1)} %pad.2.clone), kind=kLoop, calls=%fused_computation | loop fusion | flops 24576 | bytes 14368 | tf_op jit(solution)/shard_map/concatenate | solution.py:211
  0.9 6.0 %collective-permute-start.2 = (bf16[16,256]{1,0:T(8,128)(2,1)S(1)}, bf16[16,256]{1,0:T(8,128)(2,1)S(1)}, u32[]{:S(2)}, u32[]{:S(2)}) collective-permute-start(bf16[16,256]{1,0:T(8,128)(2,1)S(1)} %maximum_maximum_fusion.refs_0_), channel_id=1, source_target_pairs={{0,3},{1,2},{2,1},{3,0},{4,7},{5,6},{6,5},{7,4},{8,11},{9,10},{10,... | collective-permute-start | bytes 24584 | tf_op jit(solution)/shard_map/ppermute | solution.py:208
  6.9 1.0 %collective-permute-start.3 = (bf16[16,256]{1,0:T(8,128)(2,1)S(1)}, bf16[16,256]{1,0:T(8,128)(2,1)S(1)}, u32[]{:S(2)}, u32[]{:S(2)}) collective-permute-start(bf16[16,256]{1,0:T(8,128)(2,1)S(1)} %maximum_maximum_fusion.refs_0_), channel_id=1, source_target_pairs={{0,2},{1,3},{2,0},{3,1},{4,6},{5,7},{6,4},{7,5},{8,10},{9,11},{10,... | collective-permute-start | bytes 24584 | tf_op jit(solution)/shard_map/ppermute | solution.py:208
  7.9 1.2 %collective-permute-start.4 = (bf16[16,256]{1,0:T(8,128)(2,1)S(1)}, bf16[16,256]{1,0:T(8,128)(2,1)S(1)}, u32[]{:S(2)}, u32[]{:S(2)}) collective-permute-start(bf16[16,256]{1,0:T(8,128)(2,1)S(1)} %maximum_maximum_fusion.refs_0_), channel_id=1, source_target_pairs={{0,1},{1,0},{2,3},{3,2},{4,5},{5,4},{6,7},{7,6},{8,9},{9,8},{10,11... | collective-permute-start | bytes 24584 | tf_op jit(solution)/shard_map/ppermute | solution.py:208
  9.1 1.1 %slice.6 = bf16[5,256,256]{2,1,0:T(8,128)(2,1)S(1)} slice(bf16[8,256,256]{2,1,0:T(8,128)(2,1)} %own.1), slice={[3:8], [0:256], [0:256]} | slice | bytes 1310720 | tf_op jit(solution)/shard_map/slice | solution.py:213
  10.2 7.8 %collective-permute-start = (bf16[5,256,256]{2,1,0:T(8,128)(2,1)S(1)}, bf16[5,256,256]{2,1,0:T(8,128)(2,1)S(1)}, u32[]{:S(2)}, u32[]{:S(2)}) collective-permute-start(bf16[5,256,256]{2,1,0:T(8,128)(2,1)S(1)} %slice.6), channel_id=1, source_target_pairs={{1,2},{3,4},{5,6},{7,8},{9,10},{11,12},{13,14},{15,16},{17,18},{19... | collective-permute-start | bytes 1966088 | tf_op jit(solution)/shard_map/ppermute | solution.py:215
  18.2 0.5 copy-done.18
  18.7 0.6 copy-done.20
  19.3 1.4 %join.2.refs_0_ = bf16[64,256]{1,0:T(8,128)(2,1)} custom-call(bf16[16,256]{1,0:T(8,128)(2,1)} %copy-done.14, bf16[16,256]{1,0:T(8,128)(2,1)} %copy-done.18, bf16[16,256]{1,0:T(8,128)(2,1)} %copy-done.19, bf16[16,256]{1,0:T(8,128)(2,1)} %copy-done.20), custom_call_target="tpu_custom_call" | custom-call | bytes 1024 | tf_op jit(solution)/shard_map/join/pallas_call | solution.py:219
  20.7 1.2 %collective-permute-start.5 = (bf16[64,256]{1,0:T(8,128)(2,1)}, bf16[64,256]{1,0:T(8,128)(2,1)S(1)}, u32[]{:S(2)}, u32[]{:S(2)}) collective-permute-start(bf16[64,256]{1,0:T(8,128)(2,1)} %join.2.refs_0_), channel_id=1, source_target_pairs={{0,12},{1,13},{2,14},{3,15},{4,8},{5,9},{6,10},{7,11},{8,4},{9,5},... | collective-permute-start | bytes 98312 | tf_op jit(solution)/shard_map/ppermute | solution.py:208
  22.4 1.5 %collective-permute-start.7 = (bf16[64,256]{1,0:T(8,128)(2,1)}, bf16[64,256]{1,0:T(8,128)(2,1)S(1)}, u32[]{:S(2)}, u32[]{:S(2)}) collective-permute-start(bf16[64,256]{1,0:T(8,128)(2,1)} %join.2.refs_0_), channel_id=1, source_target_pairs={{0,4},{1,5},{2,6},{3,7},{4,0},{5,1},{6,2},{7,3},{8,12},{9,13},{10,... | collective-permute-start | bytes 98312 | tf_op jit(solution)/shard_map/ppermute | solution.py:208
  24.0 1.2 %collective-permute-done.5.refs_1_ = bf16[64,256]{1,0:T(8,128)(2,1)S(1)} collective-permute-done((bf16[64,256]{1,0:T(8,128)(2,1)}, bf16[64,256]{1,0:T(8,128)(2,1)S(1)}, u32[]{:S(2)}, u32[]{:S(2)}) %collective-permute-start.5) | collective-permute-done | bytes 32800 | tf_op jit(solution)/shard_map/ppermute | solution.py:208
  25.2 2.2 %collective-permute-done.6.refs_2_ = bf16[64,256]{1,0:T(8,128)(2,1)S(1)} collective-permute-done((bf16[64,256]{1,0:T(8,128)(2,1)}, bf16[64,256]{1,0:T(8,128)(2,1)S(1)}, u32[]{:S(2)}, u32[]{:S(2)}) %collective-permute-start.6) | collective-permute-done | bytes 32800 | tf_op jit(solution)/shard_map/ppermute | solution.py:208
  27.4 0.6 copy-done.16
  28.0 0.6 copy-done.17
  28.6 1.5 %join.3.rest_0_ = bf16[256,256]{1,0:T(8,128)(2,1)} custom-call(bf16[64,256]{1,0:T(8,128)(2,1)} %join.2.refs_0_, bf16[64,256]{1,0:T(8,128)(2,1)} %copy-done.15, bf16[64,256]{1,0:T(8,128)(2,1)} %copy-done.16, bf16[64,256]{1,0:T(8,128)(2,1)} %copy-done.17), custom_call_target="tpu_custom_call" | custom-call | bytes 1024 | tf_op jit(solution)/shard_map/join/pallas_call | solution.py:219
  30.0 2.2 %collective-permute-start.9 = (bf16[256,256]{1,0:T(8,128)(2,1)}, bf16[256,256]{1,0:T(8,128)(2,1)S(1)}, u32[]{:S(2)}, u32[]{:S(2)}) collective-permute-start(bf16[256,256]{1,0:T(8,128)(2,1)} %join.3.rest_0_), channel_id=1, source_target_pairs={{0,32},{1,33},{2,34},{3,35},{4,36},{5,37},{6,38},{7,39},{8,40},{9,... | collective-permute-start | bytes 393224 | tf_op jit(solution)/shard_map/ppermute | solution.py:208
  32.3 1.0 %collective-permute-start.10 = (bf16[256,256]{1,0:T(8,128)(2,1)}, bf16[256,256]{1,0:T(8,128)(2,1)S(1)}, u32[]{:S(2)}, u32[]{:S(2)}) collective-permute-start(bf16[256,256]{1,0:T(8,128)(2,1)} %join.3.rest_0_), channel_id=1, source_target_pairs={{0,16},{1,17},{2,18},{3,19},{4,20},{5,21},{6,22},{7,23},{8,24},{9,... | collective-permute-start | bytes 393224 | tf_op jit(solution)/shard_map/ppermute | solution.py:208
  33.3 1.2 %copy-done.3 = bf16[8,256,256]{2,1,0:T(8,128)(2,1)S(1)} copy-done((bf16[8,256,256]{2,1,0:T(8,128)(2,1)S(1)}, bf16[8,256,256]{2,1,0:T(8,128)(2,1)}, u32[]{:S(2)}) %copy-start.3) | copy-done | bytes 1048600
  34.5 0.9 %copy-done.4 = bf16[256,256]{1,0:T(8,128)(2,1)S(1)} copy-done((bf16[256,256]{1,0:T(8,128)(2,1)S(1)}, bf16[256,256]{1,0:T(8,128)(2,1)}, u32[]{:S(2)}) %copy-start.4) | copy-done | bytes 131096
  35.4 2.8 %copy-done.13 = s32[8,256,3,256]{3,1,2,0:T(8,128)S(1)} copy-done((s32[8,256,3,256]{3,1,2,0:T(8,128)S(1)}, s32[8,256,3,256]{3,1,2,0:T(8,128)}, u32[]{:S(2)}) %copy-start.13) | copy-done | bytes 6291480
  38.3 2.7 %own_block.1 = (f32[8,256,256]{2,1,0:T(8,128)S(1)}, bf16[8,2,256,256]{3,2,1,0:T(8,128)(2,1)S(1)}, f32[8,256,128]{2,1,0:T(8,128)S(1)}) custom-call(s32[2]{0:T(128)S(1)} %pad_add_fusion.where, s32[8,3,256,256]{3,2,1,0:T(8,128)S(1)} %bitcast.9, bf16[8,256,256]{2,1,0:T(8,128)(2,1)S(1)} %copy-done.3, bf16[256,256]{1,0:T(8,128)(2,1)S(1)} %copy-done.4), custom_call_target="tpu_custom_call" | custom-call | flops 6710886400 | bytes 16777216 | tf_op jit(solution)/shard_map/own_block/pallas_call | solution.py:252
  41.0 1.2 %collective-permute-done.10.rest_3_ = bf16[256,256]{1,0:T(8,128)(2,1)S(1)} collective-permute-done((bf16[256,256]{1,0:T(8,128)(2,1)}, bf16[256,256]{1,0:T(8,128)(2,1)S(1)}, u32[]{:S(2)}, u32[]{:S(2)}) %collective-permute-start.10) | collective-permute-done | bytes 131104 | tf_op jit(solution)/shard_map/ppermute | solution.py:208
  42.2 1.9 %collective-permute-start.12 = (bf16[3,256,256]{2,1,0:T(8,128)(2,1)S(1)}, bf16[3,256,256]{2,1,0:T(8,128)(2,1)S(1)}, u32[]{:S(2)}, u32[]{:S(2)}) collective-permute-start(bf16[3,256,256]{2,1,0:T(8,128)(2,1)S(1)} %slice.7), channel_id=1, source_target_pairs={{1,2},{3,4},{5,6},{7,8},{9,10},{11,12},{13,14},{15,16},{17,18},{19... | collective-permute-start | bytes 1179656 | tf_op jit(solution)/shard_map/ppermute | solution.py:236
  44.2 0.6 collective-permute-done.odd_rows
  44.7 3.8 %collective-permute-done.1.even_rows = bf16[5,256,256]{2,1,0:T(8,128)(2,1)S(1)} collective-permute-done((bf16[5,256,256]{2,1,0:T(8,128)(2,1)S(1)}, bf16[5,256,256]{2,1,0:T(8,128)(2,1)S(1)}, u32[]{:S(2)}, u32[]{:S(2)}) %collective-permute-start.1) | collective-permute-done | bytes 655392 | tf_op jit(solution)/shard_map/ppermute | solution.py:214
  48.6 3.6 %late_months.1 = (f32[5,256,256]{2,1,0:T(8,128)S(1)}, bf16[3,256,256]{2,1,0:T(8,128)(2,1)S(1)}, bf16[5,256,256]{2,1,0:T(8,128)(2,1)S(1)}, bf16[5,256,256]{2,1,0:T(8,128)(2,1)S(1)}, bf16[5,256,256]{2,1,0:T(8,128)(2,1)S(1)}) custom-call(s32[2]{0:T(128)S(1)} %pad_add_fusion.where, f32[8,256,256]{2,1,0:T(8,128)S(1)} %get-tuple-element.20.base, ...), custom_call_target="tpu_custom_call" | custom-call | flops 33554432 | bytes 1024 | tf_op jit(solution)/shard_map/late_months/pallas_call | solution.py:267
  52.2 6.2 %collective-permute-start.11 = (bf16[3,256,256]{2,1,0:T(8,128)(2,1)S(1)}, bf16[3,256,256]{2,1,0:T(8,128)(2,1)S(1)}, u32[]{:S(2)}, u32[]{:S(2)}) collective-permute-start(bf16[3,256,256]{2,1,0:T(8,128)(2,1)S(1)} %get-tuple-element.27), channel_id=1, source_target_pairs={{0,64},{64,128},{128,192},{1,65},{65,129},{129,193},{2,66},{66,130... | collective-permute-start | bytes 1179656 | tf_op jit(solution)/shard_map/ppermute | solution.py:282
  58.5 3.9 %last_month.1 = (bf16[8,256,256]{2,1,0:T(8,128)(2,1)}, f32[3,256,256]{2,1,0:T(8,128)S(1)}) custom-call(s32[2]{0:T(128)S(1)} %pad_add_fusion.where, f32[8,256,256]{2,1,0:T(8,128)S(1)} %get-tuple-element.20.base, s32[8,256]{1,0:T(8,128)S(1)} %copy-done.9, s32[8,256]{1,0:T(8,128)S(1)} %copy-done.10, bf16[256,256]{1,0:T(8,128)(2,1)S(1)} %copy-done.2, ...), custom_call_target="tpu_custom_call" | custom-call | flops 33554432 | bytes 1024 | tf_op jit(solution)/shard_map/last_month/pallas_call | solution.py:288
  62.4 0.9 %collective-permute-done.12.odd_rows = bf16[3,256,256]{2,1,0:T(8,128)(2,1)S(1)} collective-permute-done((bf16[3,256,256]{2,1,0:T(8,128)(2,1)S(1)}, bf16[3,256,256]{2,1,0:T(8,128)(2,1)S(1)}, u32[]{:S(2)}, u32[]{:S(2)}) %collective-permute-start.12) | collective-permute-done | bytes 393248 | tf_op jit(solution)/shard_map/ppermute | solution.py:236
  63.4 4.0 %collective-permute-done.11.earlier = bf16[3,256,256]{2,1,0:T(8,128)(2,1)S(1)} collective-permute-done((bf16[3,256,256]{2,1,0:T(8,128)(2,1)S(1)}, bf16[3,256,256]{2,1,0:T(8,128)(2,1)S(1)}, u32[]{:S(2)}, u32[]{:S(2)}) %collective-permute-start.11) | collective-permute-done | bytes 393248 | tf_op jit(solution)/shard_map/ppermute | solution.py:282
  67.3 6.8 %early_months.1 = bf16[8,256,256]{2,1,0:T(8,128)(2,1)} custom-call(bf16[3,256,256]{2,1,0:T(8,128)(2,1)S(1)} %collective-permute-done.11.earlier, f32[3,256,256]{2,1,0:T(8,128)S(1)} %get-tuple-element.32.base, bf16[8,2,256,256]{3,2,1,0:T(8,128)(2,1)S(1)} %get-tuple-element.21.tiles, ...), custom_call_target="tpu_custom_call", output_to_operand_aliasing={{}: (19, {})} | custom-call | flops 33554432 | bytes 1024 | tf_op jit(solution)/shard_map/early_months/pallas_call | solution.py:301
  (50 shorter events, 1.0 us)
Async XLA Ops:
  0.9 17.3 %copy-start.14 = (bf16[16,256]{1,0:T(8,128)(2,1)}, bf16[16,256]{1,0:T(8,128)(2,1)S(1)}, u32[]{:S(2)}) copy-start(bf16[16,256]{1,0:T(8,128)(2,1)S(1)} %maximum_maximum_fusion.refs_0_) | copy-start | bytes 24580
  0.9 17.2 %collective-permute-start.2 = (bf16[16,256]{1,0:T(8,128)(2,1)S(1)}, bf16[16,256]{1,0:T(8,128)(2,1)S(1)}, u32[]{:S(2)}, u32[]{:S(2)}) collective-permute-start(bf16[16,256]{1,0:T(8,128)(2,1)S(1)} %maximum_maximum_fusion.refs_0_), channel_id=1, source_target_pairs={{0,3},{1,2},{2,1},{3,0},{4,7},{5,6},{6,5},{7,4},{8,11},{9,10},{10,... | collective-permute-start | bytes 24584 | tf_op jit(solution)/shard_map/ppermute | solution.py:208
  6.9 11.2 %collective-permute-start.3 = (bf16[16,256]{1,0:T(8,128)(2,1)S(1)}, bf16[16,256]{1,0:T(8,128)(2,1)S(1)}, u32[]{:S(2)}, u32[]{:S(2)}) collective-permute-start(bf16[16,256]{1,0:T(8,128)(2,1)S(1)} %maximum_maximum_fusion.refs_0_), channel_id=1, source_target_pairs={{0,2},{1,3},{2,0},{3,1},{4,6},{5,7},{6,4},{7,5},{8,10},{9,11},{10,... | collective-permute-start | bytes 24584 | tf_op jit(solution)/shard_map/ppermute | solution.py:208
  7.9 10.2 %collective-permute-start.4 = (bf16[16,256]{1,0:T(8,128)(2,1)S(1)}, bf16[16,256]{1,0:T(8,128)(2,1)S(1)}, u32[]{:S(2)}, u32[]{:S(2)}) collective-permute-start(bf16[16,256]{1,0:T(8,128)(2,1)S(1)} %maximum_maximum_fusion.refs_0_), channel_id=1, source_target_pairs={{0,1},{1,0},{2,3},{3,2},{4,5},{5,4},{6,7},{7,6},{8,9},{9,8},{10,11... | collective-permute-start | bytes 24584 | tf_op jit(solution)/shard_map/ppermute | solution.py:208
  10.2 34.5 %collective-permute-start = (bf16[5,256,256]{2,1,0:T(8,128)(2,1)S(1)}, bf16[5,256,256]{2,1,0:T(8,128)(2,1)S(1)}, u32[]{:S(2)}, u32[]{:S(2)}) collective-permute-start(bf16[5,256,256]{2,1,0:T(8,128)(2,1)S(1)} %slice.6), channel_id=1, source_target_pairs={{1,2},{3,4},{5,6},{7,8},{9,10},{11,12},{13,14},{15,16},{17,18},{19... | collective-permute-start | bytes 1966088 | tf_op jit(solution)/shard_map/ppermute | solution.py:215
  18.0 30.5 %collective-permute-start.1 = (bf16[5,256,256]{2,1,0:T(8,128)(2,1)S(1)}, bf16[5,256,256]{2,1,0:T(8,128)(2,1)S(1)}, u32[]{:S(2)}, u32[]{:S(2)}) collective-permute-start(bf16[5,256,256]{2,1,0:T(8,128)(2,1)S(1)} %slice.6), channel_id=1, source_target_pairs={{0,1},{1,0},{2,3},{3,2},{4,5},{5,4},{6,7},{7,6},{8,9},{9,8},{10,11... | collective-permute-start | bytes 1966088 | tf_op jit(solution)/shard_map/ppermute | solution.py:214
  20.7 4.5 %collective-permute-start.5 = (bf16[64,256]{1,0:T(8,128)(2,1)}, bf16[64,256]{1,0:T(8,128)(2,1)S(1)}, u32[]{:S(2)}, u32[]{:S(2)}) collective-permute-start(bf16[64,256]{1,0:T(8,128)(2,1)} %join.2.refs_0_), channel_id=1, source_target_pairs={{0,12},{1,13},{2,14},{3,15},{4,8},{5,9},{6,10},{7,11},{8,4},{9,5},... | collective-permute-start | bytes 98312 | tf_op jit(solution)/shard_map/ppermute | solution.py:208
  21.9 5.5 %collective-permute-start.6 = (bf16[64,256]{1,0:T(8,128)(2,1)}, bf16[64,256]{1,0:T(8,128)(2,1)S(1)}, u32[]{:S(2)}, u32[]{:S(2)}) collective-permute-start(bf16[64,256]{1,0:T(8,128)(2,1)} %join.2.refs_0_), channel_id=1, source_target_pairs={{0,8},{1,9},{2,10},{3,11},{4,12},{5,13},{6,14},{7,15},{8,0},{9,1},... | collective-permute-start | bytes 98312 | tf_op jit(solution)/shard_map/ppermute | solution.py:208
  22.4 4.9 %collective-permute-start.7 = (bf16[64,256]{1,0:T(8,128)(2,1)}, bf16[64,256]{1,0:T(8,128)(2,1)S(1)}, u32[]{:S(2)}, u32[]{:S(2)}) collective-permute-start(bf16[64,256]{1,0:T(8,128)(2,1)} %join.2.refs_0_), channel_id=1, source_target_pairs={{0,4},{1,5},{2,6},{3,7},{4,0},{5,1},{6,2},{7,3},{8,12},{9,13},{10,... | collective-permute-start | bytes 98312 | tf_op jit(solution)/shard_map/ppermute | solution.py:208
  25.1 2.2 %copy-start.15 = (bf16[64,256]{1,0:T(8,128)(2,1)}, bf16[64,256]{1,0:T(8,128)(2,1)S(1)}, u32[]{:S(2)}) copy-start(bf16[64,256]{1,0:T(8,128)(2,1)S(1)} %collective-permute-done.5.refs_1_) | copy-start | bytes 98308
  27.4 0.6 copy-start.16
  28.0 0.6 copy-start.17
  30.0 10.9 %collective-permute-start.8 = (bf16[256,256]{1,0:T(8,128)(2,1)}, bf16[256,256]{1,0:T(8,128)(2,1)S(1)}, u32[]{:S(2)}, u32[]{:S(2)}) collective-permute-start(bf16[256,256]{1,0:T(8,128)(2,1)} %join.3.rest_0_), channel_id=1, source_target_pairs={{0,48},{1,49},{2,50},{3,51},{4,52},{5,53},{6,54},{7,55},{8,56},{9,... | collective-permute-start | bytes 393224 | tf_op jit(solution)/shard_map/ppermute | solution.py:208
  30.0 10.9 %collective-permute-start.9 = (bf16[256,256]{1,0:T(8,128)(2,1)}, bf16[256,256]{1,0:T(8,128)(2,1)S(1)}, u32[]{:S(2)}, u32[]{:S(2)}) collective-permute-start(bf16[256,256]{1,0:T(8,128)(2,1)} %join.3.rest_0_), channel_id=1, source_target_pairs={{0,32},{1,33},{2,34},{3,35},{4,36},{5,37},{6,38},{7,39},{8,40},{9,... | collective-permute-start | bytes 393224 | tf_op jit(solution)/shard_map/ppermute | solution.py:208
  32.3 9.9 %collective-permute-start.10 = (bf16[256,256]{1,0:T(8,128)(2,1)}, bf16[256,256]{1,0:T(8,128)(2,1)S(1)}, u32[]{:S(2)}, u32[]{:S(2)}) collective-permute-start(bf16[256,256]{1,0:T(8,128)(2,1)} %join.3.rest_0_), channel_id=1, source_target_pairs={{0,16},{1,17},{2,18},{3,19},{4,20},{5,21},{6,22},{7,23},{8,24},{9,... | collective-permute-start | bytes 393224 | tf_op jit(solution)/shard_map/ppermute | solution.py:208
  33.3 1.2 %copy-start.3 = (bf16[8,256,256]{2,1,0:T(8,128)(2,1)S(1)}, bf16[8,256,256]{2,1,0:T(8,128)(2,1)}, u32[]{:S(2)}) copy-start(bf16[8,256,256]{2,1,0:T(8,128)(2,1)} %own.1) | copy-start | bytes 3145732
  34.5 0.9 %copy-start.4 = (bf16[256,256]{1,0:T(8,128)(2,1)S(1)}, bf16[256,256]{1,0:T(8,128)(2,1)}, u32[]{:S(2)}) copy-start(bf16[256,256]{1,0:T(8,128)(2,1)} %w_supply.3) | copy-start | bytes 393220
  35.4 2.8 %copy-start.13 = (s32[8,256,3,256]{3,1,2,0:T(8,128)S(1)}, s32[8,256,3,256]{3,1,2,0:T(8,128)}, u32[]{:S(2)}) copy-start(s32[8,256,3,256]{3,1,2,0:T(8,128)} %param.16) | copy-start | bytes 18874372
  38.2 10.3 %copy-start.2 = (bf16[256,256]{1,0:T(8,128)(2,1)S(1)}, bf16[256,256]{1,0:T(8,128)(2,1)}, u32[]{:S(2)}) copy-start(bf16[256,256]{1,0:T(8,128)(2,1)} %join.3.rest_0_) | copy-start | bytes 393220
  38.2 10.3 %copy-start.5 = (bf16[256,256]{1,0:T(8,128)(2,1)S(1)}, bf16[256,256]{1,0:T(8,128)(2,1)}, u32[]{:S(2)}) copy-start(bf16[256,256]{1,0:T(8,128)(2,1)} %w_query.1) | copy-start | bytes 393220
  38.2 10.3 %copy-start.6 = (bf16[256,256]{1,0:T(8,128)(2,1)S(1)}, bf16[256,256]{1,0:T(8,128)(2,1)}, u32[]{:S(2)}) copy-start(bf16[256,256]{1,0:T(8,128)(2,1)} %w_key.1) | copy-start | bytes 393220
  38.2 10.3 %copy-start.7 = (bf16[256,256]{1,0:T(8,128)(2,1)S(1)}, bf16[256,256]{1,0:T(8,128)(2,1)}, u32[]{:S(2)}) copy-start(bf16[256,256]{1,0:T(8,128)(2,1)} %w_value.1) | copy-start | bytes 393220
  38.2 10.3 %copy-start.9 = (s32[8,256]{1,0:T(8,128)S(1)}, s32[8,256]{1,0:T(8,128)}, u32[]{:S(2)}) copy-start(s32[8,256]{1,0:T(8,128)} %banks.3) | copy-start | bytes 24580
  38.2 10.3 %copy-start.10 = (s32[8,256]{1,0:T(8,128)S(1)}, s32[8,256]{1,0:T(8,128)}, u32[]{:S(2)}) copy-start(s32[8,256]{1,0:T(8,128)} %sectors.3) | copy-start | bytes 24580
  38.2 10.3 %copy-start.11 = (f32[256]{0:T(256)S(1)}, f32[256]{0:T(256)}, u32[]{:S(2)}) copy-start(f32[256]{0:T(256)} %param.28) | copy-start | bytes 3076
  42.2 21.2 %collective-permute-start.12 = (bf16[3,256,256]{2,1,0:T(8,128)(2,1)S(1)}, bf16[3,256,256]{2,1,0:T(8,128)(2,1)S(1)}, u32[]{:S(2)}, u32[]{:S(2)}) collective-permute-start(bf16[3,256,256]{2,1,0:T(8,128)(2,1)S(1)} %slice.7), channel_id=1, source_target_pairs={{1,2},{3,4},{5,6},{7,8},{9,10},{11,12},{13,14},{15,16},{17,18},{19... | collective-permute-start | bytes 1179656 | tf_op jit(solution)/shard_map/ppermute | solution.py:236
  44.1 19.3 %collective-permute-start.13 = (bf16[3,256,256]{2,1,0:T(8,128)(2,1)S(1)}, bf16[3,256,256]{2,1,0:T(8,128)(2,1)S(1)}, u32[]{:S(2)}, u32[]{:S(2)}) collective-permute-start(bf16[3,256,256]{2,1,0:T(8,128)(2,1)S(1)} %slice.7), channel_id=1, source_target_pairs={{0,1},{1,0},{2,3},{3,2},{4,5},{5,4},{6,7},{7,6},{8,9},{9,8},{10,11... | collective-permute-start | bytes 1179656 | tf_op jit(solution)/shard_map/ppermute | solution.py:235
  48.6 9.9 %copy-start = (bf16[256,1024]{1,0:T(8,128)(2,1)S(1)}, bf16[256,1024]{1,0:T(8,128)(2,1)}, u32[]{:S(2)}) copy-start(bf16[256,1024]{1,0:T(8,128)(2,1)} %w_in.1) | copy-start | bytes 1572868
  48.6 9.9 %copy-start.1 = (bf16[1024,256]{1,0:T(8,128)(2,1)S(1)}, bf16[1024,256]{1,0:T(8,128)(2,1)}, u32[]{:S(2)}) copy-start(bf16[1024,256]{1,0:T(8,128)(2,1)} %w_down.1) | copy-start | bytes 1572868
  48.6 9.9 %copy-start.8 = (bf16[256,256]{1,0:T(8,128)(2,1)S(1)}, bf16[256,256]{1,0:T(8,128)(2,1)}, u32[]{:S(2)}) copy-start(bf16[256,256]{1,0:T(8,128)(2,1)} %w_out.1) | copy-start | bytes 393220
  48.6 9.9 %copy-start.12 = (f32[256]{0:T(256)S(1)}, f32[256]{0:T(256)}, u32[]{:S(2)}) copy-start(f32[256]{0:T(256)} %param.29) | copy-start | bytes 3076
  52.2 15.1 %collective-permute-start.11 = (bf16[3,256,256]{2,1,0:T(8,128)(2,1)S(1)}, bf16[3,256,256]{2,1,0:T(8,128)(2,1)S(1)}, u32[]{:S(2)}, u32[]{:S(2)}) collective-permute-start(bf16[3,256,256]{2,1,0:T(8,128)(2,1)S(1)} %get-tuple-element.27), channel_id=1, source_target_pairs={{0,64},{64,128},{128,192},{1,65},{65,129},{129,193},{2,66},{66,130... | collective-permute-start | bytes 1179656 | tf_op jit(solution)/shard_map/ppermute | solution.py:282
  (3 other events, 1.8 us)
